TPU v7x, 256 devices: a whole 4x4x8 slice. The times are simulated.
256 devices in a mesh: mem: 16 (over z, core), reg: 16 (over x, y).
Axes of the slice: x: 4, y: 4, z: 8, core: 2. Of those that a mesh axis runs over, the one named last changes fastest.
Arguments:
- member_vectors: float32 [131072, 2048], P('reg', 'mem'), may hold values from -6 to 6
- flow_speed_ratio: float32 [131072], P('reg'), may hold values from 0.3 to 0.95
- obs_pert: bfloat16 [8192, 2048], P('reg', 'mem'), may hold values from -6 to 6
- obs_incr: bfloat16 [8192, 2048], P('reg', 'mem'), may hold values from -12 to 12
- edge_list: int32 [16, 2, 64], P('reg'), may hold values from 0 to 511
- block_obs: int32 [2048, 64], P('reg'), may hold values from 0 to 639
- block_count: int32 [2048], P('reg'), may hold values from 1 to 64
- obs_offset: float32 [2048, 64], P('reg'), may hold values from -64 to 128
Outputs:
- analysis: float32 [131072, 2048], P('reg', 'mem')
All inputs are finite; a program needn't handle non-finite values.
Results may differ from a plain program's by a relative error of at most 0.0014.
Values may be sent and summed in bfloat16 or wider, within the bound.
A program may use at most 128 MiB of HBM per device.

v0:
```python
import jax
import jax.numpy as jnp
from jax import lax
from jax.sharding import PartitionSpec as P

BLOCK = 64
KB = 64
STEPS = 4


def passed_along(block, axis, distance):
    devices = range(lax.axis_size(axis))
    route = [((i - distance) % len(devices), i) for i in devices]
    return lax.ppermute(block, axis, route)


def padded(block, sides, width):
    for axis, dim in sides:
        count = lax.axis_size(axis)
        forward = [(i, i + 1) for i in range(count - 1)]
        forward.append((count - 1, 0))
        backward = [(target, source) for source, target in forward]
        low = lax.ppermute(
            lax.slice_in_dim(block, block.shape[dim] - width, None, axis=dim), axis, forward
        )
        high = lax.ppermute(lax.slice_in_dim(block, 0, width, axis=dim), axis, backward)
        block = jnp.concatenate([low, block, high], axis=dim)
    return block


def side_by_side(arrays, axis, dim, along):
    columns = [a.reshape(*a.shape[:along], -1) for a in arrays]
    both = jnp.concatenate(columns, axis=along)
    whole, at, gathered = (lax.psum_scatter(both, axis, scatter_dimension=dim, tiled=True), 0, [])
    for a, column in zip(arrays, columns):
        piece = whole[..., at : at + column.shape[along]]
        gathered.append(piece.reshape(*piece.shape[:along], *a.shape[along:]))
        at += column.shape[along]
    return tuple(gathered)


def laid_out(parts, dim):
    parts = jnp.moveaxis(parts, 0, dim)
    lengths = parts.shape
    return parts.reshape(*lengths[:dim], lengths[dim] * lengths[dim + 1], *lengths[dim + 2 :])


def from_everyone(value, axis):
    copies = jnp.broadcast_to(value, (lax.axis_size(axis), *value.shape))
    return lax.all_to_all(copies, axis, split_axis=0, concat_axis=0, tiled=True)


def gathered_copies(value, axis, dim):
    return laid_out(from_everyone(value, axis), dim)


def taper_mask(positions, live_counts):
    position = jnp.arange(BLOCK).astype(jnp.float32)
    distance = (position[None, :, None] - positions[:, None, :]) / (0.5 * BLOCK)
    active = jnp.arange(KB)[None, :] < live_counts[:, None]
    return jnp.where(active[:, None, :], 1.0 / (1.0 + distance * distance), 0.0)


def block_sums(mesh_point_entries, obs_rows):
    cross = jnp.einsum(
        "bcm,bkm->bck", mesh_point_entries, obs_rows, preferred_element_type=jnp.float32
    )
    sum_cells = jnp.sum(mesh_point_entries.astype(jnp.float32), 2)
    sum_obs = jnp.sum(obs_rows.astype(jnp.float32), 2)
    return (cross, sum_cells, sum_obs)


def covariances(cross, sum_cells, sum_obs, positions, live_counts, members):
    return (
        (cross - sum_cells[:, :, None] * sum_obs[:, None, :] / members)
        / (members - 1)
        * taper_mask(positions, live_counts)
    ).astype(jnp.bfloat16)


def apply_cov(covariance, incr_rows):
    correction_delta = jnp.einsum(
        "bck,bkm->bcm", covariance, incr_rows, preferred_element_type=jnp.float32
    )
    return correction_delta.astype(jnp.bfloat16)


def per_device(
    member_vectors,
    flow_speed_ratio,
    obs_pert,
    obs_incr,
    edge_list,
    block_obs,
    block_count,
    obs_offset,
):
    concentration_map = member_vectors
    outgoing = jnp.concatenate([concentration_map[-STEPS:, :], flow_speed_ratio[-STEPS:, None]], 1)
    arrived = passed_along(outgoing, "reg", 1)
    widened = jnp.concatenate([arrived[:, :-1], concentration_map], 0)
    speeds = jnp.concatenate([arrived[:, -1], flow_speed_ratio], 0)
    for sweep in range(STEPS):
        widened = widened[1:] - speeds[sweep + 1 :, None] * (widened[1:] - widened[:-1])
    concentration_map = widened
    first_guess_state = concentration_map.astype(jnp.bfloat16)
    lend = edge_list.shape[2]
    edge_rows = edge_list.reshape(-1)
    chosen = jnp.stack([obs_pert[edge_rows], obs_incr[edge_rows]])
    rimmed = padded(chosen, (("reg", 1),), lend)
    extended = jnp.concatenate(
        [rimmed[:, :lend], jnp.stack([obs_pert, obs_incr]), rimmed[:, -lend:]], 1
    )
    member_dev = member_vectors.shape[1]
    members = member_dev * lax.axis_size("mem")
    per_region = block_obs.shape[0]
    share = per_region // lax.axis_size("mem")
    mesh_point_entries = first_guess_state.reshape(per_region, BLOCK, member_dev)
    partial_value = block_sums(mesh_point_entries, extended[0][block_obs])
    cross, sum_cells, sum_obs = side_by_side(
        (partial_value[0], partial_value[1], partial_value[2]), "mem", 0, 2
    )
    first_block = lax.axis_index("mem") * share
    live_counts = lax.dynamic_slice_in_dim(block_count, first_block, share, 0)
    positions = lax.dynamic_slice_in_dim(obs_offset, first_block, share, 0)
    own_cov = covariances(cross, sum_cells, sum_obs, positions, live_counts, members)
    covariance = gathered_copies(own_cov, "mem", 0)
    correction_delta = apply_cov(covariance, extended[1][block_obs])
    returned = correction_delta.reshape(per_region * BLOCK, member_dev)
    return concentration_map + returned.astype(jnp.float32)


def solution(mesh):
    return jax.shard_map(
        per_device,
        mesh=mesh,
        in_specs=(
            P("reg", "mem"),
            P("reg"),
            P("reg", "mem"),
            P("reg", "mem"),
            P("reg", None, None),
            P("reg", None),
            P("reg"),
            P("reg", None),
        ),
        out_specs=P("reg", "mem"),
        check_vma=False,
    )
```

profile of v0, /device:TPU:1, one launch (start us, length us, event | category | flops | bytes accessed | tf_op | source)
XLA Modules:
  0.0 206.1 jit_solution(5425803664370170043)
XLA Ops:
  6.5 0.8 slice_bitcast_fusion.2
  7.4 0.7 slice.70
  8.1 2.1 %collective-permute-start = (f32[4,129]{1,0:T(4,128)S(1)}, f32[4,129]{1,0:T(4,128)S(1)}, u32[]{:S(2)}, u32[]{:S(2)}) collective-permute-start(f32[4,129]{1,0:T(4,128)S(1)} %pad_maximum_fusion.5), channel_id=1, source_target_pairs={{15,0},{0,1},{1,2},{2,3},{3,4},{4,5},{5,6},{6,7},{7,8},{8,9},{9,10... | collective-permute-start | bytes 6200 | tf_op jit(solution)/shard_map/ppermute | solution.py:14
  10.2 0.8 reshape.76
  11.0 1.6 gather_fusion
  12.6 1.6 gather_fusion.1
  14.1 1.4 collective-permute-start.1
  15.5 3.5 %collective-permute-start.2 = (bf16[2,64,128]{2,1,0:T(8,128)(2,1)S(1)}, bf16[2,64,128]{2,1,0:T(8,128)(2,1)S(1)}, u32[]{:S(2)}, u32[]{:S(2)}) collective-permute-start(bf16[2,64,128]{2,1,0:T(8,128)(2,1)S(1)} %get-tuple-element.12), channel_id=1, source_target_pairs={{1,0},{2,1},{3,2},{4,3},{5,4},{6,5},{7,6},{8,7},{9,8},{10,9},{11,1... | collective-permute-start | bytes 98312 | tf_op jit(solution)/shard_map/ppermute | solution.py:26
  19.0 0.8 compare_select_fusion
  20.1 0.8 fusion.13
  20.9 0.8 fusion.12
  21.8 0.8 pad_maximum_fusion.3
  22.6 6.9 %fusion.6 = f32[8195,128]{1,0:T(8,128)S(1)} fusion(f32[8192,128]{1,0:T(8,128)} %param.8, f32[4,128]{1,0:T(4,128)S(1)} %slice.100, f32[8195]{0:T(1024)S(1)} %fusion.13), kind=kLoop, calls=%fused_computation.13 | loop fusion | flops 5244800 | bytes 8424972 | tf_op jit(solution)/shard_map/sub | solution.py:104
  29.5 3.6 %fusion.3 = f32[8194,128]{1,0:T(8,128)S(1)} fusion(f32[8195,128]{1,0:T(8,128)S(1)} %fusion.6, f32[8194]{0:T(1024)S(1)} %fusion.12), kind=kLoop, calls=%fused_computation.9 | loop fusion | flops 3146496 | bytes 12618760 | tf_op jit(solution)/shard_map/sub | solution.py:104
  33.1 3.6 %fusion.1 = f32[8193,128]{1,0:T(8,128)S(1)} fusion(f32[8194,128]{1,0:T(8,128)S(1)} %fusion.3, f32[8193]{0:T(1024)S(1)} %pad_maximum_fusion.3), kind=kLoop, calls=%fused_computation.6 | loop fusion | flops 3146112 | bytes 12617220 | tf_op jit(solution)/shard_map/sub | solution.py:104
  36.6 3.2 %convert_reduce_fusion.1 = (f32[8192]{0:T(1024)S(1)}, bf16[8192,128]{1,0:T(8,128)(2,1)}) fusion(f32[8193,128]{1,0:T(8,128)S(1)} %fusion.1, f32[8192]{0:T(1024)S(1)} %copy-done.4), kind=kLoop, calls=%fused_computation.20 | loop fusion | flops 6283264 | bytes 10551296 | tf_op jit(solution)/shard_map/reduce_sum | solution.py:68
  39.9 5.2 %reshape.117 = f32[128,64,1]{2,1,0:T(8,128)} reshape(f32[8192]{0:T(1024)S(1)} %get-tuple-element.7) | data formatting | bytes 65536 | tf_op jit(solution)/shard_map/reshape | solution.py:32
  45.2 24.0 %gather_fusion.2 = bf16[8192,128]{1,0:T(8,128)(2,1)S(1)} fusion(bf16[640,128]{1,0:T(8,128)(2,1)S(1)} %get-tuple-element.10, s32[8192]{0:T(1024)S(1)} %broadcast_clamp_fusion), kind=kCustom, calls=%fused_computation.2 | custom fusion | bytes 4227072 | tf_op jit(solution)/shard_map/gather | solution.py:119
  69.2 1.2 convert_reduce_fusion
  70.4 4.8 %fusion.18 = f32[128,64,64]{2,1,0:T(8,128)} fusion(bf16[128,64,128]{2,1,0:T(8,128)(2,1)} %bitcast.28, bf16[128,64,128]{2,1,0:T(8,128)(2,1)S(1)} %bitcast.25), kind=kOutput, calls=%fused_computation.52 | convolution fusion | flops 134217728 | bytes 6291456 | tf_op jit(solution)/shard_map/bcm,bkm->bck/dot_general | solution.py:65
  75.1 2.7 %copy.20 = f32[128,64,1]{2,1,0:T(8,128)} copy(f32[128,64,1]{1,0,2:T(8,128)S(1)} %bitcast.31) | data formatting | bytes 65536 | tf_op jit(solution)/shard_map/reshape | solution.py:32
  77.8 8.8 %pad_maximum_fusion.1 = f32[128,64,66]{2,1,0:T(8,128)} fusion(f32[128,64,1]{2,1,0:T(8,128)} %copy.20, f32[128,64,1]{2,1,0:T(8,128)} %reshape.117, f32[128,64,64]{2,1,0:T(8,128)} %fusion.18), kind=kLoop, calls=%fused_computation.17 | loop fusion | flops 1081344 | bytes 4325376 | tf_op jit(solution)/shard_map/concatenate | solution.py:33
  87.5 59.8 %reduce-scatter.2.cloned.1.call-done = f32[8,64,66]{2,1,0:T(8,128)} async-done(((f32[128,64,66]{2,1,0:T(8,128)}), f32[8,64,66]{2,1,0:T(8,128)}) %reduce-scatter.2.cloned.1.call-update) | async-done | bytes 135184 | tf_op jit(solution)/shard_map/reduce_scatter | solution.py:34
  147.3 1.4 slice_reduce_fusion.1
  148.7 1.1 fusion.11
  150.4 2.2 %reshape.121 = bf16[16,2,16384]{2,1,0:T(2,128)(2,1)} reshape(bf16[16,8,64,64]{3,2,1,0:T(8,128)(2,1)S(1)} %broadcast_in_dim.22) | data formatting | bytes 2097152
  152.6 7.9 %all-to-all-start = ((bf16[16,2,16384]{2,1,0:T(2,128)(2,1)}), bf16[16,2,16384]{2,1,0:T(2,128)(2,1)S(1)}, u32[]{:S(2)}, u32[]{:S(2)}) async-start(bf16[16,2,16384]{2,1,0:T(2,128)(2,1)} %reshape.121), calls=%async_computation.1 | async-start | bytes 2097152 | tf_op jit(solution)/shard_map/all_to_all | solution.py:50
  160.6 24.0 %gather_fusion.3 = bf16[8192,128]{1,0:T(8,128)(2,1)S(1)} fusion(bf16[640,128]{1,0:T(8,128)(2,1)S(1)} %get-tuple-element.9, s32[8192]{0:T(1024)S(1)} %broadcast_clamp_fusion), kind=kCustom, calls=%fused_computation.3 | custom fusion | bytes 4227072 | tf_op jit(solution)/shard_map/gather | solution.py:128
  184.6 4.0 %all-to-all-done = bf16[16,2,16384]{2,1,0:T(2,128)(2,1)S(1)} async-done(((bf16[16,2,16384]{2,1,0:T(2,128)(2,1)}), bf16[16,2,16384]{2,1,0:T(2,128)(2,1)S(1)}, u32[]{:S(2)}, u32[]{:S(2)}) %all-to-all-start) | async-done | bytes 1048608 | tf_op jit(solution)/shard_map/all_to_all | solution.py:50
  188.6 2.3 %reshape.122 = bf16[16,8,64,64]{3,2,1,0:T(8,128)(2,1)} reshape(bf16[16,2,16384]{2,1,0:T(2,128)(2,1)S(1)} %all-to-all-done) | data formatting | bytes 2097152
  190.9 2.3 %convolution_convert_fusion = bf16[128,64,128]{2,1,0:T(8,128)(2,1)S(1)} fusion(bf16[128,64,64]{2,1,0:T(8,128)(2,1)} %bitcast.27, bf16[128,64,128]{2,1,0:T(8,128)(2,1)S(1)} %bitcast.26), kind=kOutput, calls=%fused_computation.21 | convolution fusion | flops 135266304 | bytes 5242880 | tf_op jit(solution)/shard_map/bck,bkm->bcm/dot_general | solution.py:82
  193.2 6.1 %convert_add_fusion = f32[8192,128]{1,0:T(8,128)} fusion(bf16[128,64,128]{2,1,0:T(8,128)(2,1)S(1)} %convolution_convert_fusion, f32[8193,128]{1,0:T(8,128)} %copy-done.1, f32[8192]{0:T(1024)S(1)} %copy-done.4), kind=kLoop, calls=%fused_computation.18 | loop fusion | flops 5242880 | bytes 14712832 | tf_op jit(solution)/shard_map/add | solution.py:130
  (35 shorter events, 1.8 us)
Async XLA Ops:
  6.5 80.2 %copy-start = (f32[128,64]{0,1:T(8,128)S(1)}, f32[128,64]{0,1:T(8,128)}, u32[]{:S(2)}) copy-start(f32[128,64]{0,1:T(8,128)} %param.15) | copy-start | bytes 98308
  6.5 140.8 %reduce-scatter.2.cloned.1.call-start = ((), (), s32[]{:S(2)}) async-start(), calls=%async_computation.2 | async-start | bytes 4456448 | tf_op jit(solution)/shard_map/reduce_scatter | solution.py:34
  8.1 11.9 %collective-permute-start = (f32[4,129]{1,0:T(4,128)S(1)}, f32[4,129]{1,0:T(4,128)S(1)}, u32[]{:S(2)}, u32[]{:S(2)}) collective-permute-start(f32[4,129]{1,0:T(4,128)S(1)} %pad_maximum_fusion.5), channel_id=1, source_target_pairs={{15,0},{0,1},{1,2},{2,3},{3,4},{4,5},{5,6},{6,7},{7,8},{8,9},{9,10... | collective-permute-start | bytes 6200 | tf_op jit(solution)/shard_map/ppermute | solution.py:14
  14.1 31.0 %collective-permute-start.1 = (bf16[2,64,128]{2,1,0:T(8,128)(2,1)S(1)}, bf16[2,64,128]{2,1,0:T(8,128)(2,1)S(1)}, u32[]{:S(2)}, u32[]{:S(2)}) collective-permute-start(bf16[2,64,128]{2,1,0:T(8,128)(2,1)S(1)} %get-tuple-element.11), channel_id=1, source_target_pairs={{0,1},{1,2},{2,3},{3,4},{4,5},{5,6},{6,7},{7,8},{8,9},{9,10},{10,1... | collective-permute-start | bytes 98312 | tf_op jit(solution)/shard_map/ppermute | solution.py:23
  15.5 29.6 %collective-permute-start.2 = (bf16[2,64,128]{2,1,0:T(8,128)(2,1)S(1)}, bf16[2,64,128]{2,1,0:T(8,128)(2,1)S(1)}, u32[]{:S(2)}, u32[]{:S(2)}) collective-permute-start(bf16[2,64,128]{2,1,0:T(8,128)(2,1)S(1)} %get-tuple-element.12), channel_id=1, source_target_pairs={{1,0},{2,1},{3,2},{4,3},{5,4},{6,5},{7,6},{8,7},{9,8},{10,9},{11,1... | collective-permute-start | bytes 98312 | tf_op jit(solution)/shard_map/ppermute | solution.py:26
  33.0 3.6 %copy-start.4 = (f32[8192]{0:T(1024)S(1)}, f32[8192]{0:T(1024)}, u32[]{:S(2)}) copy-start(f32[8192]{0:T(1024)} %param.9) | copy-start | bytes 98308
  36.6 3.2 %copy-start.1 = (f32[8193,128]{1,0:T(8,128)}, f32[8193,128]{1,0:T(8,128)S(1)}, u32[]{:S(2)}) copy-start(f32[8193,128]{1,0:T(8,128)S(1)} %fusion.1) | copy-start | bytes 12584452
  39.9 5.2 %copy-start.2 = (bf16[512,128]{1,0:T(8,128)(2,1)S(1)}, bf16[512,128]{1,0:T(8,128)(2,1)}, u32[]{:S(2)}) copy-start(bf16[512,128]{1,0:T(8,128)(2,1)} %param.10) | copy-start | bytes 393220
  39.9 5.3 %copy-start.3 = (bf16[512,128]{1,0:T(8,128)(2,1)S(1)}, bf16[512,128]{1,0:T(8,128)(2,1)}, u32[]{:S(2)}) copy-start(bf16[512,128]{1,0:T(8,128)(2,1)} %param.11) | copy-start | bytes 393220
  86.7 0.7 copy-start.5
  152.6 35.9 %all-to-all-start = ((bf16[16,2,16384]{2,1,0:T(2,128)(2,1)}), bf16[16,2,16384]{2,1,0:T(2,128)(2,1)S(1)}, u32[]{:S(2)}, u32[]{:S(2)}) async-start(bf16[16,2,16384]{2,1,0:T(2,128)(2,1)} %reshape.121), calls=%async_computation.1 | async-start | bytes 2097152 | tf_op jit(solution)/shard_map/all_to_all | solution.py:50
Sparse Core Ops, SparseCore 0:
  86.8 60.4 reduce-scatter.1
where the time goes:
time: 207 us; the launch traced here: 206 us
  local copies, waits for them, and re-layouts  68.9 us (33%)
  waiting for transfers between devices  63.8 us (31%)
  other arithmetic  37.8 us (18%)
  starting transfers between devices  14.9 us (7%)
  between operations  13.6 us (7%)
  matrix products  7.05 us (3%)
    reduce_scatter x1, waiting for transfers between devices, side_by_side(): lax.psum_scatter(both, axis, scatter_dimension=dim, tiled=True)  59.8 us
    gather x1, local copies, waits for them, and re-layouts, per_device(): partial_value = block_sums(mesh_point_entries, extended[0][block_obs])  24 us
    gather x1, local copies, waits for them, and re-layouts, per_device(): correction_delta = apply_cov(covariance, extended[1][block_obs])  24 us
    sub x3, other arithmetic, per_device(): widened[1:] - speeds[sweep + 1:, None] * (widened[1:] - widened[:-1])  14 us
    concatenate x1, other arithmetic, side_by_side(): both = jnp.concatenate(columns, axis=along)  8.85 us
    all_to_all x1, starting transfers between devices, from_everyone(): return lax.all_to_all(copies, axis, split_axis=0, concat_axis=0, tiled=True)  7.95 us
    reshape x2, local copies, waits for them, and re-layouts, side_by_side(): columns = [a.reshape(*a.shape[:along], -1) for a in arrays]  7.94 us
    add x1, other arithmetic, per_device(): return concentration_map + returned.astype(jnp.float32)  6.06 us
  transfers between devices with their start and end apart: 5, of which 2 were waited for; matrix products, arithmetic and copies ran while one was open for 26% of the time, Pallas kernels for 0%

commit v1 on v0

--- a/solution.py
+++ b/solution.py
@@ -116,7 +116,13 @@
     per_region = block_obs.shape[0]
     share = per_region // lax.axis_size("mem")
     mesh_point_entries = first_guess_state.reshape(per_region, BLOCK, member_dev)
-    partial_value = block_sums(mesh_point_entries, extended[0][block_obs])
+    slots = extended.shape[1]
+    picks = (block_obs.reshape(-1)[:, None] == jnp.arange(slots)[None, :]).astype(jnp.bfloat16)
+    both = jnp.concatenate([extended[0], extended[1]], 1)
+    rows = jnp.dot(picks, both, preferred_element_type=jnp.float32).astype(jnp.bfloat16)
+    obs_rows = rows[:, :member_dev].reshape(per_region, KB, member_dev)
+    incr_rows = rows[:, member_dev:].reshape(per_region, KB, member_dev)
+    partial_value = block_sums(mesh_point_entries, obs_rows)
     cross, sum_cells, sum_obs = side_by_side(
         (partial_value[0], partial_value[1], partial_value[2]), "mem", 0, 2
     )
@@ -125,7 +131,7 @@
     positions = lax.dynamic_slice_in_dim(obs_offset, first_block, share, 0)
     own_cov = covariances(cross, sum_cells, sum_obs, positions, live_counts, members)
     covariance = gathered_copies(own_cov, "mem", 0)
-    correction_delta = apply_cov(covariance, extended[1][block_obs])
+    correction_delta = apply_cov(covariance, incr_rows)
     returned = correction_delta.reshape(per_region * BLOCK, member_dev)
     return concentration_map + returned.astype(jnp.float32)
 

time: 207 us -> 187 us (0.903)
  local copies, waits for them, and re-layouts: 68.9 us -> 28.3 us
  blocking collectives: 0 us -> 36.3 us
  starting transfers between devices: 14.9 us -> 6.98 us
  other arithmetic: 37.8 us -> 31.1 us
  waiting for transfers between devices: 63.8 us -> 59.8 us
  matrix products: 7.05 us -> 9.99 us
    gather x2 -> x0, local copies, waits for them, and re-layouts: 48.1 us -> none  [the longest x1 24 us: per_device(): partial_value = block_sums(mesh_point_entries, extended[0][block_obs])]
    all_to_all x0 -> x1, blocking collectives: none -> 36.3 us  [from_everyone(): return lax.all_to_all(copies, axis, split_axis=0, concat_axis=0, tiled=True)]
    all_to_all x1 -> x0, starting transfers between devices: 7.95 us -> none  [from_everyone(): return lax.all_to_all(copies, axis, split_axis=0, concat_axis=0, tiled=True)]
    dot_general x0 -> x1, matrix products: none -> 4.75 us  [per_device(): jnp.dot(picks, both, preferred_element_type=jnp.float32)]
    concatenate x1, other arithmetic: 8.85 us -> 4.24 us  [side_by_side(): both = jnp.concatenate(columns, axis=along)]
    all_to_all x1 -> x0, waiting for transfers between devices: 3.96 us -> none  [from_everyone(): return lax.all_to_all(copies, axis, split_axis=0, concat_axis=0, tiled=True)]
    unnamed x14 -> x19, local copies, waits for them, and re-layouts: 5.05 us -> 7.71 us
    reshape x2, local copies, waits for them, and re-layouts: 7.94 us -> 10.5 us  [side_by_side(): columns = [a.reshape(*a.shape[:along], -1) for a in arrays]]
  transfers between devices with their start and end apart: 5 -> 4, of which waited for: 2 -> 1; matrix products, arithmetic and copies ran while one was open for 26% -> 16% of each run, Pallas kernels for 0% -> 0%
where the time goes in v1:
time: 187 us; the launch traced here: 186 us
  waiting for transfers between devices  59.8 us (32%)
  blocking collectives  36.3 us (19%)
  other arithmetic  31.1 us (17%)
  local copies, waits for them, and re-layouts  28.3 us (15%)
  between operations  13.6 us (7%)
  matrix products  9.99 us (5%)
  starting transfers between devices  6.98 us (4%)
    reduce_scatter x1, waiting for transfers between devices, side_by_side(): lax.psum_scatter(both, axis, scatter_dimension=dim, tiled=True)  59.8 us
    all_to_all x1, blocking collectives, from_everyone(): return lax.all_to_all(copies, axis, split_axis=0, concat_axis=0, tiled=True)  36.3 us
    sub x3, other arithmetic, per_device(): widened[1:] - speeds[sweep + 1:, None] * (widened[1:] - widened[:-1])  13.9 us
    reshape x2, local copies, waits for them, and re-layouts, side_by_side(): columns = [a.reshape(*a.shape[:along], -1) for a in arrays]  10.5 us
    unnamed x19, local copies, waits for them, and re-layouts  7.71 us
    add x1, other arithmetic, per_device(): return concentration_map + returned.astype(jnp.float32)  5.99 us
    dot_general x1, matrix products, per_device(): jnp.dot(picks, both, preferred_element_type=jnp.float32)  4.75 us
    concatenate x1, other arithmetic, side_by_side(): both = jnp.concatenate(columns, axis=along)  4.24 us
  transfers between devices with their start and end apart: 4, of which 1 were waited for; matrix products, arithmetic and copies ran while one was open for 16% of the time, Pallas kernels for 0%

profile of v1, /device:TPU:1, one launch (start us, length us, event | category | flops | bytes accessed | tf_op | source)
XLA Modules:
  0.0 186.0 jit_solution(5152856613454764492)
XLA Ops:
  6.5 0.8 slice_bitcast_fusion.2
  7.4 0.7 slice.76
  8.1 2.1 %collective-permute-start = (f32[4,129]{1,0:T(4,128)S(1)}, f32[4,129]{1,0:T(4,128)S(1)}, u32[]{:S(2)}, u32[]{:S(2)}) collective-permute-start(f32[4,129]{1,0:T(4,128)S(1)} %pad_maximum_fusion.5), channel_id=1, source_target_pairs={{15,0},{0,1},{1,2},{2,3},{3,4},{4,5},{5,6},{6,7},{7,8},{8,9},{9,10... | collective-permute-start | bytes 6200 | tf_op jit(solution)/shard_map/ppermute | solution.py:14
  10.2 0.8 reshape.85
  11.0 1.6 gather_fusion
  12.6 1.6 gather_fusion.1
  14.1 1.4 collective-permute-start.1
  15.5 3.5 %collective-permute-start.2 = (bf16[2,64,128]{2,1,0:T(8,128)(2,1)S(1)}, bf16[2,64,128]{2,1,0:T(8,128)(2,1)S(1)}, u32[]{:S(2)}, u32[]{:S(2)}) collective-permute-start(bf16[2,64,128]{2,1,0:T(8,128)(2,1)S(1)} %get-tuple-element.14), channel_id=1, source_target_pairs={{1,0},{2,1},{3,2},{4,3},{5,4},{6,5},{7,6},{8,7},{9,8},{10,9},{11,1... | collective-permute-start | bytes 98312 | tf_op jit(solution)/shard_map/ppermute | solution.py:26
  19.0 0.8 copy.12
  20.1 0.8 fusion.19
  20.9 0.8 fusion.18
  21.7 0.8 pad_maximum_fusion.3
  22.6 6.8 %fusion.9 = f32[8195,128]{1,0:T(8,128)S(1)} fusion(f32[8192,128]{1,0:T(8,128)} %param.8, f32[4,128]{1,0:T(4,128)S(1)} %slice.104, f32[8195]{0:T(1024)S(1)} %fusion.19), kind=kLoop, calls=%fused_computation.15 | loop fusion | flops 5244800 | bytes 8424972 | tf_op jit(solution)/shard_map/sub | solution.py:104
  29.3 3.6 %fusion.6 = f32[8194,128]{1,0:T(8,128)S(1)} fusion(f32[8195,128]{1,0:T(8,128)S(1)} %fusion.9, f32[8194]{0:T(1024)S(1)} %fusion.18), kind=kLoop, calls=%fused_computation.11 | loop fusion | flops 3146496 | bytes 12618760 | tf_op jit(solution)/shard_map/sub | solution.py:104
  32.9 3.6 %fusion.4 = f32[8193,128]{1,0:T(8,128)S(1)} fusion(f32[8194,128]{1,0:T(8,128)S(1)} %fusion.6, f32[8193]{0:T(1024)S(1)} %pad_maximum_fusion.3), kind=kLoop, calls=%fused_computation.8 | loop fusion | flops 3146112 | bytes 12617220 | tf_op jit(solution)/shard_map/sub | solution.py:104
  36.5 2.6 %convert_reduce_fusion.1 = (f32[8192]{0:T(1024)S(1)}, bf16[8192,128]{1,0:T(8,128)(2,1)S(1)}) fusion(f32[8193,128]{1,0:T(8,128)S(1)} %fusion.4, f32[8192]{0:T(1024)S(1)} %copy-done.6), kind=kLoop, calls=%fused_computation.22 | loop fusion | flops 6283264 | bytes 10551296 | tf_op jit(solution)/shard_map/reduce_sum | solution.py:68
  39.1 5.3 %reshape.108 = f32[128,64,1]{2,1,0:T(8,128)} reshape(f32[8192]{0:T(1024)S(1)} %get-tuple-element.7) | data formatting | bytes 65536 | tf_op jit(solution)/shard_map/reshape | solution.py:32
  44.5 4.7 %fusion.2 = bf16[8192,256]{1,0:T(8,128)(2,1)S(1)} fusion(s32[8192]{0:T(1024)S(1)} %eq.15, bf16[640,128]{1,0:T(8,128)(2,1)S(1)} %get-tuple-element.12, bf16[640,128]{1,0:T(8,128)(2,1)S(1)} %get-tuple-element.11), kind=kOutput, calls=%fused_computation.5 | convolution fusion | flops 2692349952 | bytes 4554752 | tf_op jit(solution)/shard_map/dot_general | solution.py:122
  49.3 2.2 %fusion.25 = (bf16[8192,128]{1,0:T(8,128)(2,1)}, bf16[8192,128]{1,0:T(8,128)(2,1)}) fusion(bf16[8192,256]{1,0:T(8,128)(2,1)S(1)} %fusion.2), kind=kLoop, calls=%fused_computation.56 | loop fusion | bytes 8388608 | tf_op jit(solution)/shard_map/slice | solution.py:124
  51.5 0.6 convert_reduce_fusion
  52.1 5.3 %reshape.109 = f32[128,64,1]{2,1,0:T(8,128)} reshape(f32[8192]{0:T(1024)S(1)} %convert_reduce_fusion) | data formatting | bytes 65536 | tf_op jit(solution)/shard_map/reshape | solution.py:32
  57.4 3.0 %fusion.26 = f32[128,64,64]{2,1,0:T(8,128)S(1)} fusion(bf16[128,64,128]{2,1,0:T(8,128)(2,1)S(1)} %bitcast.25, bf16[128,64,128]{2,1,0:T(8,128)(2,1)} %bitcast.26), kind=kOutput, calls=%fused_computation.57 | convolution fusion | flops 134217728 | bytes 6291456 | tf_op jit(solution)/shard_map/bcm,bkm->bck/dot_general | solution.py:65
  60.3 1.1 copy-done.3
  61.5 4.2 %pad_maximum_fusion.1 = f32[128,64,66]{2,1,0:T(8,128)} fusion(f32[128,64,1]{2,1,0:T(8,128)S(1)} %copy-done.3, f32[128,64,1]{2,1,0:T(8,128)S(1)} %copy-done.2, f32[128,64,64]{2,1,0:T(8,128)S(1)} %fusion.26), kind=kLoop, calls=%fused_computation.19 | loop fusion | flops 1081344 | bytes 4325376 | tf_op jit(solution)/shard_map/concatenate | solution.py:33
  66.5 59.8 %reduce-scatter.2.cloned.1.call-done = f32[8,64,66]{2,1,0:T(8,128)} async-done(((f32[128,64,66]{2,1,0:T(8,128)}), f32[8,64,66]{2,1,0:T(8,128)}) %reduce-scatter.2.cloned.1.call-update) | async-done | bytes 135184 | tf_op jit(solution)/shard_map/reduce_scatter | solution.py:34
  126.3 1.4 slice_reduce_fusion.1
  127.7 1.1 fusion.17
  129.3 1.5 reshape.113
  130.8 36.3 %all_to_all.5 = bf16[16,2,16384]{2,1,0:T(2,128)(2,1)} all-to-all(bf16[16,2,16384]{2,1,0:T(2,128)(2,1)S(1)} %reshape.113), channel_id=1, replica_groups=mesh['mem'=16,'reg'=16] {'mem'}, dimensions={0} | all-to-all | bytes 2097152 | tf_op jit(solution)/shard_map/all_to_all | solution.py:50
  167.1 3.8 %reshape.114 = bf16[16,8,64,64]{3,2,1,0:T(8,128)(2,1)S(1)} reshape(bf16[16,2,16384]{2,1,0:T(2,128)(2,1)} %all_to_all.5) | data formatting | bytes 2097152
  170.9 2.3 %convolution_convert_fusion = bf16[128,64,128]{2,1,0:T(8,128)(2,1)S(1)} fusion(bf16[128,64,64]{2,1,0:T(8,128)(2,1)S(1)} %bitcast.23, bf16[128,64,128]{2,1,0:T(8,128)(2,1)} %bitcast.24), kind=kOutput, calls=%fused_computation.23 | convolution fusion | flops 135266304 | bytes 5242880 | tf_op jit(solution)/shard_map/bck,bkm->bcm/dot_general | solution.py:82
  173.2 6.0 %convert_add_fusion = f32[8192,128]{1,0:T(8,128)} fusion(bf16[128,64,128]{2,1,0:T(8,128)(2,1)S(1)} %convolution_convert_fusion, f32[8193,128]{1,0:T(8,128)} %copy-done.1, f32[8192]{0:T(1024)S(1)} %copy-done.6), kind=kLoop, calls=%fused_computation.20 | loop fusion | flops 5242880 | bytes 14712832 | tf_op jit(solution)/shard_map/add | solution.py:136
  (36 shorter events, 1.7 us)
Async XLA Ops:
  6.5 59.2 %copy-start = (f32[128,64]{0,1:T(8,128)S(1)}, f32[128,64]{0,1:T(8,128)}, u32[]{:S(2)}) copy-start(f32[128,64]{0,1:T(8,128)} %param.15) | copy-start | bytes 98308
  6.5 119.7 %reduce-scatter.2.cloned.1.call-start = ((), (), s32[]{:S(2)}) async-start(), calls=%async_computation.2 | async-start | bytes 4456448 | tf_op jit(solution)/shard_map/reduce_scatter | solution.py:34
  8.1 11.8 %collective-permute-start = (f32[4,129]{1,0:T(4,128)S(1)}, f32[4,129]{1,0:T(4,128)S(1)}, u32[]{:S(2)}, u32[]{:S(2)}) collective-permute-start(f32[4,129]{1,0:T(4,128)S(1)} %pad_maximum_fusion.5), channel_id=1, source_target_pairs={{15,0},{0,1},{1,2},{2,3},{3,4},{4,5},{5,6},{6,7},{7,8},{8,9},{9,10... | collective-permute-start | bytes 6200 | tf_op jit(solution)/shard_map/ppermute | solution.py:14
  14.1 30.3 %collective-permute-start.1 = (bf16[2,64,128]{2,1,0:T(8,128)(2,1)S(1)}, bf16[2,64,128]{2,1,0:T(8,128)(2,1)S(1)}, u32[]{:S(2)}, u32[]{:S(2)}) collective-permute-start(bf16[2,64,128]{2,1,0:T(8,128)(2,1)S(1)} %get-tuple-element.13), channel_id=1, source_target_pairs={{0,1},{1,2},{2,3},{3,4},{4,5},{5,6},{6,7},{7,8},{8,9},{9,10},{10,1... | collective-permute-start | bytes 98312 | tf_op jit(solution)/shard_map/ppermute | solution.py:23
  15.5 28.9 %collective-permute-start.2 = (bf16[2,64,128]{2,1,0:T(8,128)(2,1)S(1)}, bf16[2,64,128]{2,1,0:T(8,128)(2,1)S(1)}, u32[]{:S(2)}, u32[]{:S(2)}) collective-permute-start(bf16[2,64,128]{2,1,0:T(8,128)(2,1)S(1)} %get-tuple-element.14), channel_id=1, source_target_pairs={{1,0},{2,1},{3,2},{4,3},{5,4},{6,5},{7,6},{8,7},{9,8},{10,9},{11,1... | collective-permute-start | bytes 98312 | tf_op jit(solution)/shard_map/ppermute | solution.py:26
  32.9 3.6 %copy-start.6 = (f32[8192]{0:T(1024)S(1)}, f32[8192]{0:T(1024)}, u32[]{:S(2)}) copy-start(f32[8192]{0:T(1024)} %param.9) | copy-start | bytes 98308
  36.5 2.6 %copy-start.1 = (f32[8193,128]{1,0:T(8,128)}, f32[8193,128]{1,0:T(8,128)S(1)}, u32[]{:S(2)}) copy-start(f32[8193,128]{1,0:T(8,128)S(1)} %fusion.4) | copy-start | bytes 12584452
  39.1 5.3 %copy-start.4 = (bf16[512,128]{1,0:T(8,128)(2,1)S(1)}, bf16[512,128]{1,0:T(8,128)(2,1)}, u32[]{:S(2)}) copy-start(bf16[512,128]{1,0:T(8,128)(2,1)} %param.10) | copy-start | bytes 393220
  39.1 5.3 %copy-start.5 = (bf16[512,128]{1,0:T(8,128)(2,1)S(1)}, bf16[512,128]{1,0:T(8,128)(2,1)}, u32[]{:S(2)}) copy-start(bf16[512,128]{1,0:T(8,128)(2,1)} %param.11) | copy-start | bytes 393220
  57.4 3.0 %copy-start.2 = (f32[128,64,1]{2,1,0:T(8,128)S(1)}, f32[128,64,1]{2,1,0:T(8,128)}, u32[]{:S(2)}) copy-start(f32[128,64,1]{2,1,0:T(8,128)} %reshape.108) | copy-start | bytes 98308
  57.4 4.1 %copy-start.3 = (f32[128,64,1]{2,1,0:T(8,128)S(1)}, f32[128,64,1]{2,1,0:T(8,128)}, u32[]{:S(2)}) copy-start(f32[128,64,1]{2,1,0:T(8,128)} %reshape.109) | copy-start | bytes 98308
  65.7 0.7 copy-start.7
Sparse Core Ops, SparseCore 0:
  65.8 60.3 reduce-scatter.1

commit v2 on v1

--- a/solution.py
+++ b/solution.py
@@ -123,9 +123,16 @@
     obs_rows = rows[:, :member_dev].reshape(per_region, KB, member_dev)
     incr_rows = rows[:, member_dev:].reshape(per_region, KB, member_dev)
     partial_value = block_sums(mesh_point_entries, obs_rows)
-    cross, sum_cells, sum_obs = side_by_side(
-        (partial_value[0], partial_value[1], partial_value[2]), "mem", 0, 2
+    flat = BLOCK * KB
+    payload = jnp.concatenate(
+        [partial_value[0].reshape(per_region, flat), partial_value[1], partial_value[2]], 1
     )
+    parts = lax.axis_size("mem")
+    got = lax.psum_scatter(payload.reshape(parts, share, -1), "mem", scatter_dimension=0, tiled=True)
+    got = got.reshape(share, -1)
+    cross = got[:, :flat].reshape(share, BLOCK, KB)
+    sum_cells = got[:, flat : flat + BLOCK]
+    sum_obs = got[:, flat + BLOCK :]
     first_block = lax.axis_index("mem") * share
     live_counts = lax.dynamic_slice_in_dim(block_count, first_block, share, 0)
     positions = lax.dynamic_slice_in_dim(obs_offset, first_block, share, 0)

time: 187 us -> 175 us (0.936)
  local copies, waits for them, and re-layouts: 28.3 us -> 22.3 us
  other arithmetic: 31.1 us -> 26 us
  waiting for transfers between devices: 59.8 us -> 57.4 us
    reduce_scatter x1 -> x0, waiting for transfers between devices: 59.8 us -> none  [side_by_side(): lax.psum_scatter(both, axis, scatter_dimension=dim, tiled=True)]
    unnamed x1 -> x2, waiting for transfers between devices: 0.02 us -> 57.4 us
    reshape x2 -> x1, local copies, waits for them, and re-layouts: 10.5 us -> 0.1 us  [per_device(): cross = got[:, :flat].reshape(share, BLOCK, KB)]
    concatenate x0 -> x4, local copies, waits for them, and re-layouts: none -> 5.74 us  [per_device(): jnp.concatenate([partial_value[0].reshape(per_region, flat), partial_valu...]
    concatenate x1 -> x0, other arithmetic: 4.24 us -> none  [side_by_side(): both = jnp.concatenate(columns, axis=along)]
    dot_general x1, matrix products: 2.96 us -> 4.83 us  [block_sums(): jnp.einsum('bcm,bkm->bck', mesh_point_entries, obs_rows, preferred_elemen...]
    unnamed x19 -> x15, local copies, waits for them, and re-layouts: 7.71 us -> 6.11 us
  transfers between devices with their start and end apart: 4 -> 4, of which waited for: 1 -> 1; matrix products, arithmetic and copies ran while one was open for 16% -> 14% of each run, Pallas kernels for 0% -> 0%
where the time goes in v2:
time: 175 us
  waiting for transfers between devices  57.4 us (33%)
  blocking collectives  36.5 us (21%)
  other arithmetic  26 us (15%)
  local copies, waits for them, and re-layouts  22.3 us (13%)
  between operations  13.6 us (8%)
  matrix products  11.8 us (7%)
  starting transfers between devices  6.98 us (4%)
    unnamed x2, waiting for transfers between devices  57.4 us
    all_to_all x1, blocking collectives, from_everyone(): return lax.all_to_all(copies, axis, split_axis=0, concat_axis=0, tiled=True)  36.5 us
    sub x3, other arithmetic, per_device(): widened[1:] - speeds[sweep + 1:, None] * (widened[1:] - widened[:-1])  13.9 us
    unnamed x15, local copies, waits for them, and re-layouts  6.11 us
    add x1, other arithmetic, per_device(): return concentration_map + returned.astype(jnp.float32)  6.03 us
    concatenate x4, local copies, waits for them, and re-layouts, per_device(): jnp.concatenate([partial_value[0].reshape(per_region, flat), partial_valu...  5.74 us
    dot_general x1, matrix products, block_sums(): jnp.einsum('bcm,bkm->bck', mesh_point_entries, obs_rows, preferred_elemen...  4.83 us
    dot_general x1, matrix products, per_device(): jnp.dot(picks, both, preferred_element_type=jnp.float32)  4.74 us
  transfers between devices with their start and end apart: 4, of which 1 were waited for; matrix products, arithmetic and copies ran while one was open for 14% of the time, Pallas kernels for 0%

profile of v2, /device:TPU:1, one launch (start us, length us, event | category | flops | bytes accessed | tf_op | source)
XLA Modules:
  0.0 174.6 jit_solution(7626632574805782251)
XLA Ops:
  6.5 0.8 slice_bitcast_fusion.2
  7.4 0.7 slice.76
  8.1 2.1 %collective-permute-start = (f32[4,129]{1,0:T(4,128)S(1)}, f32[4,129]{1,0:T(4,128)S(1)}, u32[]{:S(2)}, u32[]{:S(2)}) collective-permute-start(f32[4,129]{1,0:T(4,128)S(1)} %pad_maximum_fusion.4), channel_id=1, source_target_pairs={{15,0},{0,1},{1,2},{2,3},{3,4},{4,5},{5,6},{6,7},{7,8},{8,9},{9,10... | collective-permute-start | bytes 6200 | tf_op jit(solution)/shard_map/ppermute | solution.py:14
  10.2 0.8 reshape.92
  11.0 1.6 gather_fusion.1
  12.6 1.6 gather_fusion
  14.1 1.4 collective-permute-start.1
  15.5 3.5 %collective-permute-start.2 = (bf16[2,64,128]{2,1,0:T(8,128)(2,1)S(1)}, bf16[2,64,128]{2,1,0:T(8,128)(2,1)S(1)}, u32[]{:S(2)}, u32[]{:S(2)}) collective-permute-start(bf16[2,64,128]{2,1,0:T(8,128)(2,1)S(1)} %get-tuple-element.14), channel_id=1, source_target_pairs={{1,0},{2,1},{3,2},{4,3},{5,4},{6,5},{7,6},{8,7},{9,8},{10,9},{11,1... | collective-permute-start | bytes 98312 | tf_op jit(solution)/shard_map/ppermute | solution.py:26
  19.0 0.8 copy.15
  20.1 0.8 fusion.16
  20.9 0.8 pad_maximum_fusion.2
  21.7 0.8 fusion.15
  22.6 6.8 %fusion.9 = f32[8195,128]{1,0:T(8,128)S(1)} fusion(f32[8192,128]{1,0:T(8,128)} %param.8, f32[4,128]{1,0:T(4,128)S(1)} %slice.104, f32[8195]{0:T(1024)S(1)} %fusion.16), kind=kLoop, calls=%fused_computation.15 | loop fusion | flops 5244800 | bytes 8424972 | tf_op jit(solution)/shard_map/sub | solution.py:104
  29.4 3.6 %fusion.6 = f32[8194,128]{1,0:T(8,128)S(1)} fusion(f32[8195,128]{1,0:T(8,128)S(1)} %fusion.9, f32[8194]{0:T(1024)S(1)} %fusion.15), kind=kLoop, calls=%fused_computation.11 | loop fusion | flops 3146496 | bytes 12618760 | tf_op jit(solution)/shard_map/sub | solution.py:104
  33.0 3.6 %fusion.4 = f32[8193,128]{1,0:T(8,128)S(1)} fusion(f32[8194,128]{1,0:T(8,128)S(1)} %fusion.6, f32[8193]{0:T(1024)S(1)} %pad_maximum_fusion.2), kind=kLoop, calls=%fused_computation.8 | loop fusion | flops 3146112 | bytes 12617220 | tf_op jit(solution)/shard_map/sub | solution.py:104
  36.6 2.6 %convert_reduce_fusion.1 = (f32[8192]{0:T(1024)S(1)}, bf16[8192,128]{1,0:T(8,128)(2,1)S(1)}) fusion(f32[8193,128]{1,0:T(8,128)S(1)} %fusion.4, f32[8192]{0:T(1024)S(1)} %copy-done.4), kind=kLoop, calls=%fused_computation.21 | loop fusion | flops 6283264 | bytes 10551296 | tf_op jit(solution)/shard_map/reduce_sum | solution.py:68
  39.3 4.7 %fusion.2 = bf16[8192,256]{1,0:T(8,128)(2,1)S(1)} fusion(s32[8192]{0:T(1024)S(1)} %eq.15, bf16[640,128]{1,0:T(8,128)(2,1)S(1)} %get-tuple-element.10, bf16[640,128]{1,0:T(8,128)(2,1)S(1)} %get-tuple-element.9), kind=kOutput, calls=%fused_computation.5 | convolution fusion | flops 2692349952 | bytes 4554752 | tf_op jit(solution)/shard_map/dot_general | solution.py:122
  44.1 0.6 convert_reduce_fusion
  44.7 2.2 %fusion.22 = (bf16[8192,128]{1,0:T(8,128)(2,1)}, bf16[8192,128]{1,0:T(8,128)(2,1)}) fusion(bf16[8192,256]{1,0:T(8,128)(2,1)S(1)} %fusion.2), kind=kLoop, calls=%fused_computation.50 | loop fusion | bytes 8388608 | tf_op jit(solution)/shard_map/slice | solution.py:124
  47.0 4.8 %fusion.24 = f32[128,64,64]{2,1,0:T(8,128)} fusion(bf16[128,64,128]{2,1,0:T(8,128)(2,1)S(1)} %bitcast.27, bf16[128,64,128]{2,1,0:T(8,128)(2,1)} %bitcast.28), kind=kOutput, calls=%fused_computation.52 | convolution fusion | flops 134217728 | bytes 6291456 | tf_op jit(solution)/shard_map/bcm,bkm->bck/dot_general | solution.py:65
  51.8 3.5 %concatenate.30 = f32[16,8,4096]{2,1,0:T(8,128)S(1)} reshape(f32[128,64,64]{2,1,0:T(8,128)} %fusion.24) | data formatting | bytes 4194304 | tf_op jit(solution)/shard_map/concatenate | solution.py:127
  55.4 2.1 %concatenate.33 = f32[16,8,4224]{2,1,0:T(8,128)} concatenate(f32[16,8,4096]{2,1,0:T(8,128)S(1)} %concatenate.30, f32[16,8,64]{2,1,0:T(8,128)S(1)} %concatenate.31, f32[16,8,64]{2,1,0:T(8,128)S(1)} %concatenate.32), dimensions={2} | concatenate | bytes 4325376 | tf_op jit(solution)/shard_map/concatenate | solution.py:127
  57.8 57.4 %reduce-scatter.4.cloned.1.call-done = f32[1,8,4224]{2,1,0:T(8,128)} async-done(((f32[16,8,4224]{2,1,0:T(8,128)}), f32[1,8,4224]{2,1,0:T(8,128)}) %reduce-scatter.4.cloned.1.call-update) | async-done | bytes 135184
  115.2 0.8 fusion.23
  116.0 0.9 slice.123
  117.0 0.2 multiply_convert_fusion
  117.2 0.5 broadcast_in_dim.15
  117.7 1.5 reshape.117
  119.2 36.5 %all_to_all.5 = bf16[16,2,16384]{2,1,0:T(2,128)(2,1)} all-to-all(bf16[16,2,16384]{2,1,0:T(2,128)(2,1)S(1)} %reshape.117), channel_id=1, replica_groups=mesh['mem'=16,'reg'=16] {'mem'}, dimensions={0} | all-to-all | bytes 2097152 | tf_op jit(solution)/shard_map/all_to_all | solution.py:50
  155.7 3.8 %reshape.118 = bf16[16,8,64,64]{3,2,1,0:T(8,128)(2,1)S(1)} reshape(bf16[16,2,16384]{2,1,0:T(2,128)(2,1)} %all_to_all.5) | data formatting | bytes 2097152
  159.5 2.3 %convolution_convert_fusion = bf16[128,64,128]{2,1,0:T(8,128)(2,1)S(1)} fusion(bf16[128,64,64]{2,1,0:T(8,128)(2,1)S(1)} %bitcast.25, bf16[128,64,128]{2,1,0:T(8,128)(2,1)} %bitcast.26), kind=kOutput, calls=%fused_computation.22 | convolution fusion | flops 135266304 | bytes 5242880 | tf_op jit(solution)/shard_map/bck,bkm->bcm/dot_general | solution.py:82
  161.7 6.0 %convert_add_fusion = f32[8192,128]{1,0:T(8,128)} fusion(bf16[128,64,128]{2,1,0:T(8,128)(2,1)S(1)} %convolution_convert_fusion, f32[8193,128]{1,0:T(8,128)} %copy-done.1, f32[8192]{0:T(1024)S(1)} %copy-done.4), kind=kLoop, calls=%fused_computation.19 | loop fusion | flops 5242880 | bytes 14712832 | tf_op jit(solution)/shard_map/add | solution.py:143
  (35 shorter events, 1.0 us)
Async XLA Ops:
  6.5 51.0 %copy-start = (f32[128,64]{0,1:T(8,128)S(1)}, f32[128,64]{0,1:T(8,128)}, u32[]{:S(2)}) copy-start(f32[128,64]{0,1:T(8,128)} %param.15) | copy-start | bytes 98308
  6.5 108.6 %reduce-scatter.4.cloned.1.call-start = ((), (), s32[]{:S(2)}) async-start(), calls=%async_computation.2 | async-start | bytes 2297856
  8.1 11.8 %collective-permute-start = (f32[4,129]{1,0:T(4,128)S(1)}, f32[4,129]{1,0:T(4,128)S(1)}, u32[]{:S(2)}, u32[]{:S(2)}) collective-permute-start(f32[4,129]{1,0:T(4,128)S(1)} %pad_maximum_fusion.4), channel_id=1, source_target_pairs={{15,0},{0,1},{1,2},{2,3},{3,4},{4,5},{5,6},{6,7},{7,8},{8,9},{9,10... | collective-permute-start | bytes 6200 | tf_op jit(solution)/shard_map/ppermute | solution.py:14
  14.1 25.1 %collective-permute-start.1 = (bf16[2,64,128]{2,1,0:T(8,128)(2,1)S(1)}, bf16[2,64,128]{2,1,0:T(8,128)(2,1)S(1)}, u32[]{:S(2)}, u32[]{:S(2)}) collective-permute-start(bf16[2,64,128]{2,1,0:T(8,128)(2,1)S(1)} %get-tuple-element.13), channel_id=1, source_target_pairs={{0,1},{1,2},{2,3},{3,4},{4,5},{5,6},{6,7},{7,8},{8,9},{9,10},{10,1... | collective-permute-start | bytes 98312 | tf_op jit(solution)/shard_map/ppermute | solution.py:23
  15.5 23.7 %collective-permute-start.2 = (bf16[2,64,128]{2,1,0:T(8,128)(2,1)S(1)}, bf16[2,64,128]{2,1,0:T(8,128)(2,1)S(1)}, u32[]{:S(2)}, u32[]{:S(2)}) collective-permute-start(bf16[2,64,128]{2,1,0:T(8,128)(2,1)S(1)} %get-tuple-element.14), channel_id=1, source_target_pairs={{1,0},{2,1},{3,2},{4,3},{5,4},{6,5},{7,6},{8,7},{9,8},{10,9},{11,1... | collective-permute-start | bytes 98312 | tf_op jit(solution)/shard_map/ppermute | solution.py:26
  33.0 3.6 %copy-start.4 = (f32[8192]{0:T(1024)S(1)}, f32[8192]{0:T(1024)}, u32[]{:S(2)}) copy-start(f32[8192]{0:T(1024)} %param.9) | copy-start | bytes 98308
  36.5 2.6 %copy-start.1 = (f32[8193,128]{1,0:T(8,128)}, f32[8193,128]{1,0:T(8,128)S(1)}, u32[]{:S(2)}) copy-start(f32[8193,128]{1,0:T(8,128)S(1)} %fusion.4) | copy-start | bytes 12584452
  36.6 2.7 %copy-start.2 = (bf16[512,128]{1,0:T(8,128)(2,1)S(1)}, bf16[512,128]{1,0:T(8,128)(2,1)}, u32[]{:S(2)}) copy-start(bf16[512,128]{1,0:T(8,128)(2,1)} %param.10) | copy-start | bytes 393220
  36.6 2.7 %copy-start.3 = (bf16[512,128]{1,0:T(8,128)(2,1)S(1)}, bf16[512,128]{1,0:T(8,128)(2,1)}, u32[]{:S(2)}) copy-start(bf16[512,128]{1,0:T(8,128)(2,1)} %param.11) | copy-start | bytes 393220
  55.4 2.1 %copy-start.5 = (s32[128]{0:T(128)S(1)}, s32[128]{0:T(128)}, u32[]{:S(2)}) copy-start(s32[128]{0:T(128)} %param.14) | copy-start | bytes 1540
Sparse Core Ops, SparseCore 0:
  57.6 57.5 reduce-scatter.3

commit v3 on v2

--- a/solution.py
+++ b/solution.py
@@ -1,11 +1,55 @@
 import jax
 import jax.numpy as jnp
 from jax import lax
+from jax.experimental import pallas as pl
+from jax.experimental.pallas import tpu as pltpu
 from jax.sharding import PartitionSpec as P
 
 BLOCK = 64
 KB = 64
 STEPS = 4
+ROWS = 1024
+
+def advect_kernel(halo_ref, s_ref, x_ref, f_ref, fb_ref, carry_ref):
+    @pl.when(pl.program_id(0) == 0)
+    def _():
+        carry_ref[...] = halo_ref[...]
+    x = x_ref[...]
+    s = jnp.broadcast_to(s_ref[...], x.shape)
+    first = lax.broadcasted_iota(jnp.int32, x.shape, 0) == 0
+    last = x.shape[0] - 1
+    for k in range(STEPS):
+        before = jnp.where(first, carry_ref[k : k + 1, :], pltpu.roll(x, 1, 0))
+        carry_ref[k : k + 1, :] = x[last:, :]
+        x = x - s * (x - before)
+    f_ref[...] = x
+    fb_ref[...] = x.astype(jnp.bfloat16)
+
+def advect(halo, speeds, x, interpret=False):
+    cells, width = x.shape
+    rows = min(ROWS, cells)
+    return pl.pallas_call(
+        advect_kernel,
+        grid=(cells // rows,),
+        in_specs=[
+            pl.BlockSpec((8, width), lambda t: (0, 0)),
+            pl.BlockSpec((rows, 1), lambda t: (t, 0)),
+            pl.BlockSpec((rows, width), lambda t: (t, 0)),
+        ],
+        out_specs=[pl.BlockSpec((rows, width), lambda t: (t, 0)), pl.BlockSpec((rows, width), lambda t: (t, 0))],
+        out_shape=[jax.ShapeDtypeStruct(x.shape, jnp.float32), jax.ShapeDtypeStruct(x.shape, jnp.bfloat16)],
+        scratch_shapes=[pltpu.VMEM((8, width), jnp.float32)],
+        compiler_params=pltpu.CompilerParams(dimension_semantics=("arbitrary",)),
+        interpret=interpret,
+    )(halo, speeds[:, None], x)
+
+def halo_rows(arrived, arrived_speeds, width):
+    v = arrived
+    rows = [v[-1]]
+    for k in range(1, STEPS):
+        v = v[1:] - arrived_speeds[k:, None] * (v[1:] - v[:-1])
+        rows.append(v[-1])
+    return jnp.concatenate([jnp.stack(rows), jnp.zeros((8 - STEPS, width), v.dtype)], 0)
 
 
 def passed_along(block, axis, distance):
@@ -98,12 +142,9 @@
     concentration_map = member_vectors
     outgoing = jnp.concatenate([concentration_map[-STEPS:, :], flow_speed_ratio[-STEPS:, None]], 1)
     arrived = passed_along(outgoing, "reg", 1)
-    widened = jnp.concatenate([arrived[:, :-1], concentration_map], 0)
-    speeds = jnp.concatenate([arrived[:, -1], flow_speed_ratio], 0)
-    for sweep in range(STEPS):
-        widened = widened[1:] - speeds[sweep + 1 :, None] * (widened[1:] - widened[:-1])
-    concentration_map = widened
-    first_guess_state = concentration_map.astype(jnp.bfloat16)
+    width = concentration_map.shape[1]
+    halo = halo_rows(arrived[:, :-1], arrived[:, -1], width)
+    concentration_map, first_guess_state = advect(halo, flow_speed_ratio, concentration_map)
     lend = edge_list.shape[2]
     edge_rows = edge_list.reshape(-1)
     chosen = jnp.stack([obs_pert[edge_rows], obs_incr[edge_rows]])

time: 175 us -> 171 us (0.977)
  other arithmetic: 26 us -> 6.63 us
  Pallas kernels: 0 us -> 9.58 us
  local copies, waits for them, and re-layouts: 22.3 us -> 28.1 us
    sub x3, other arithmetic: 13.9 us -> 0.76 us  [halo_rows(): v = v[1:] - arrived_speeds[k:, None] * (v[1:] - v[:-1])]
    pallas_call x0 -> x1, Pallas kernels: none -> 9.58 us  [advect(): pl.pallas_call(advect_kernel, grid=(cells // rows,), in_specs=[pl.BlockSp...]
    broadcast_in_dim x0 -> x2, local copies, waits for them, and re-layouts: none -> 3.38 us  [the longest x1 3.38 us: advect(): speeds[:, None]]
    add x1, other arithmetic: 6.03 us -> 2.69 us  [per_device(): return concentration_map + returned.astype(jnp.float32)]
    concatenate x3 -> x0, other arithmetic: 2.52 us -> none  [per_device(): speeds = jnp.concatenate([arrived[:, -1], flow_speed_ratio], 0)]
  transfers between devices with their start and end apart: 4 -> 4, of which waited for: 1 -> 1; matrix products, arithmetic and copies ran while one was open for 14% -> 8% of each run, Pallas kernels for 0% -> 6%
where the time goes in v3:
time: 171 us; the launch traced here: 170 us
  waiting for transfers between devices  57 us (33%)
  blocking collectives  36 us (21%)
  local copies, waits for them, and re-layouts  28.1 us (16%)
  between operations  13.6 us (8%)
  matrix products  12 us (7%)
  Pallas kernels  9.58 us (6%)
  starting transfers between devices  6.98 us (4%)
  other arithmetic  6.63 us (4%)
    unnamed x2, waiting for transfers between devices  57 us
    all_to_all x1, blocking collectives, from_everyone(): return lax.all_to_all(copies, axis, split_axis=0, concat_axis=0, tiled=True)  36 us
    pallas_call x1, Pallas kernels, advect(): pl.pallas_call(advect_kernel, grid=(cells // rows,), in_specs=[pl.BlockSp...  9.58 us
    unnamed x15, local copies, waits for them, and re-layouts  7.1 us
    concatenate x4, local copies, waits for them, and re-layouts, per_device(): jnp.concatenate([partial_value[0].reshape(per_region, flat), partial_valu...  5.74 us
    dot_general x1, matrix products, block_sums(): jnp.einsum('bcm,bkm->bck', mesh_point_entries, obs_rows, preferred_elemen...  4.82 us
    dot_general x1, matrix products, per_device(): jnp.dot(picks, both, preferred_element_type=jnp.float32)  4.75 us
    ppermute x1, starting transfers between devices, padded(): lax.ppermute(lax.slice_in_dim(block, 0, width, axis=dim), axis, backward)  3.49 us
  transfers between devices with their start and end apart: 4, of which 1 were waited for; matrix products, arithmetic and copies ran while one was open for 8% of the time, Pallas kernels for 6%

profile of v3, /device:TPU:1, one launch (start us, length us, event | category | flops | bytes accessed | tf_op | source)
XLA Modules:
  0.0 169.8 jit_solution(15614026604130481069)
XLA Ops:
  6.5 0.8 slice_bitcast_fusion.2
  7.4 0.7 slice.81
  8.1 2.1 %collective-permute-start = (f32[4,129]{1,0:T(4,128)S(1)}, f32[4,129]{1,0:T(4,128)S(1)}, u32[]{:S(2)}, u32[]{:S(2)}) collective-permute-start(f32[4,129]{1,0:T(4,128)S(1)} %pad_maximum_fusion.2), channel_id=1, source_target_pairs={{15,0},{0,1},{1,2},{2,3},{3,4},{4,5},{5,6},{6,7},{7,8},{8,9},{9,10... | collective-permute-start | bytes 6200 | tf_op jit(solution)/shard_map/ppermute | solution.py:58
  10.2 0.8 reshape.96
  11.0 1.6 gather_fusion.1
  12.6 1.6 gather_fusion
  14.1 1.4 collective-permute-start.1
  15.5 3.5 %collective-permute-start.2 = (bf16[2,64,128]{2,1,0:T(8,128)(2,1)S(1)}, bf16[2,64,128]{2,1,0:T(8,128)(2,1)S(1)}, u32[]{:S(2)}, u32[]{:S(2)}) collective-permute-start(bf16[2,64,128]{2,1,0:T(8,128)(2,1)S(1)} %get-tuple-element.16), channel_id=1, source_target_pairs={{1,0},{2,1},{3,2},{4,3},{5,4},{6,5},{7,6},{8,7},{9,8},{10,9},{11,1... | collective-permute-start | bytes 98312 | tf_op jit(solution)/shard_map/ppermute | solution.py:70
  19.0 0.8 copy.17
  19.9 3.4 %copy.16.s_ref = f32[8192,1]{1,0:T(8,128)} copy(f32[8192,1]{0,1:T(1,128)} %bitcast.37) | data formatting | bytes 65536 | tf_op jit(solution)/shard_map/broadcast_in_dim | solution.py:44
  23.7 0.5 slice.112
  24.3 0.6 multiply_subtract_fusion.1
  24.9 0.6 concatenate.23.halo_ref
  25.5 9.6 %shard_map.82 = (f32[8192,128]{1,0:T(8,128)}, bf16[8192,128]{1,0:T(8,128)(2,1)}) custom-call(f32[8,128]{1,0:T(8,128)} %concatenate.23.halo_ref, f32[8192,1]{1,0:T(8,128)} %copy.16.s_ref, f32[8192,128]{1,0:T(8,128)} %x_ref.1), custom_call_target="tpu_custom_call" | custom-call | tf_op jit(solution)/shard_map/pallas_call | solution.py:31
  35.1 2.3 %convert_reduce_fusion.1 = f32[8192]{0:T(1024)S(1)} fusion(bf16[8192,128]{1,0:T(8,128)(2,1)} %get-tuple-element.8), kind=kLoop, calls=%fused_computation.8 | loop fusion | flops 2088960 | bytes 2129920 | tf_op jit(solution)/shard_map/reduce_sum | solution.py:112
  37.5 4.8 %fusion.2 = bf16[8192,256]{1,0:T(8,128)(2,1)S(1)} fusion(s32[8192]{0:T(1024)S(1)} %eq.15, bf16[640,128]{1,0:T(8,128)(2,1)S(1)} %get-tuple-element.12, bf16[640,128]{1,0:T(8,128)(2,1)S(1)} %get-tuple-element.11), kind=kOutput, calls=%fused_computation.5 | convolution fusion | flops 2692349952 | bytes 4554752 | tf_op jit(solution)/shard_map/dot_general | solution.py:163
  42.3 0.6 convert_reduce_fusion
  42.9 2.3 %fusion.11 = (bf16[8192,128]{1,0:T(8,128)(2,1)}, bf16[8192,128]{1,0:T(8,128)(2,1)}) fusion(bf16[8192,256]{1,0:T(8,128)(2,1)S(1)} %fusion.2), kind=kLoop, calls=%fused_computation.37 | loop fusion | bytes 8388608 | tf_op jit(solution)/shard_map/slice | solution.py:165
  45.3 4.8 %fusion.13 = f32[128,64,64]{2,1,0:T(8,128)} fusion(bf16[128,64,128]{2,1,0:T(8,128)(2,1)S(1)} %bitcast.29, bf16[128,64,128]{2,1,0:T(8,128)(2,1)} %bitcast.30), kind=kOutput, calls=%fused_computation.39 | convolution fusion | flops 134217728 | bytes 6291456 | tf_op jit(solution)/shard_map/bcm,bkm->bck/dot_general | solution.py:109
  50.2 3.5 %concatenate.26 = f32[16,8,4096]{2,1,0:T(8,128)S(1)} reshape(f32[128,64,64]{2,1,0:T(8,128)} %fusion.13) | data formatting | bytes 4194304 | tf_op jit(solution)/shard_map/concatenate | solution.py:168
  53.7 2.1 %concatenate.29 = f32[16,8,4224]{2,1,0:T(8,128)} concatenate(f32[16,8,4096]{2,1,0:T(8,128)S(1)} %concatenate.26, f32[16,8,64]{2,1,0:T(8,128)S(1)} %concatenate.27, f32[16,8,64]{2,1,0:T(8,128)S(1)} %concatenate.28), dimensions={2} | concatenate | bytes 4325376 | tf_op jit(solution)/shard_map/concatenate | solution.py:168
  55.8 0.6 copy-done.5
  56.7 57.0 %reduce-scatter.4.cloned.1.call-done = f32[1,8,4224]{2,1,0:T(8,128)} async-done(((f32[16,8,4224]{2,1,0:T(8,128)}), f32[1,8,4224]{2,1,0:T(8,128)}) %reduce-scatter.4.cloned.1.call-update) | async-done | bytes 135184
  113.7 0.8 fusion.12
  114.5 0.9 slice.118
  115.7 0.5 broadcast_in_dim.42
  116.2 1.5 reshape.122
  117.7 36.0 %all_to_all.5 = bf16[16,2,16384]{2,1,0:T(2,128)(2,1)} all-to-all(bf16[16,2,16384]{2,1,0:T(2,128)(2,1)S(1)} %reshape.122), channel_id=1, replica_groups=mesh['mem'=16,'reg'=16] {'mem'}, dimensions={0} | all-to-all | bytes 2097152 | tf_op jit(solution)/shard_map/all_to_all | solution.py:94
  153.7 3.8 %reshape.123 = bf16[16,8,64,64]{3,2,1,0:T(8,128)(2,1)S(1)} reshape(bf16[16,2,16384]{2,1,0:T(2,128)(2,1)} %all_to_all.5) | data formatting | bytes 2097152
  157.4 2.4 %convolution_convert_fusion = bf16[128,64,128]{2,1,0:T(8,128)(2,1)S(1)} fusion(bf16[128,64,64]{2,1,0:T(8,128)(2,1)S(1)} %bitcast.27, bf16[128,64,128]{2,1,0:T(8,128)(2,1)} %bitcast.28), kind=kOutput, calls=%fused_computation.9 | convolution fusion | flops 135266304 | bytes 5242880 | tf_op jit(solution)/shard_map/bck,bkm->bcm/dot_general | solution.py:126
  159.9 0.4 copy-done.2
  160.2 2.7 %convert_add_fusion = f32[8192,128]{1,0:T(8,128)} fusion(f32[8192,128]{1,0:T(8,128)S(1)} %copy-done.2, bf16[128,64,128]{2,1,0:T(8,128)(2,1)S(1)} %convolution_convert_fusion), kind=kLoop, calls=%fused_computation.6 | loop fusion | flops 2097152 | bytes 10485760 | tf_op jit(solution)/shard_map/add | solution.py:184
  (39 shorter events, 1.4 us)
Async XLA Ops:
  6.5 50.0 %copy-start = (f32[128,64]{0,1:T(8,128)S(1)}, f32[128,64]{0,1:T(8,128)}, u32[]{:S(2)}) copy-start(f32[128,64]{0,1:T(8,128)} %param.15) | copy-start | bytes 98308
  6.5 107.1 %reduce-scatter.4.cloned.1.call-start = ((), (), s32[]{:S(2)}) async-start(), calls=%async_computation.2 | async-start | bytes 2297856
  8.1 15.2 %collective-permute-start = (f32[4,129]{1,0:T(4,128)S(1)}, f32[4,129]{1,0:T(4,128)S(1)}, u32[]{:S(2)}, u32[]{:S(2)}) collective-permute-start(f32[4,129]{1,0:T(4,128)S(1)} %pad_maximum_fusion.2), channel_id=1, source_target_pairs={{15,0},{0,1},{1,2},{2,3},{3,4},{4,5},{5,6},{6,7},{7,8},{8,9},{9,10... | collective-permute-start | bytes 6200 | tf_op jit(solution)/shard_map/ppermute | solution.py:58
  14.1 23.3 %collective-permute-start.1 = (bf16[2,64,128]{2,1,0:T(8,128)(2,1)S(1)}, bf16[2,64,128]{2,1,0:T(8,128)(2,1)S(1)}, u32[]{:S(2)}, u32[]{:S(2)}) collective-permute-start(bf16[2,64,128]{2,1,0:T(8,128)(2,1)S(1)} %get-tuple-element.15), channel_id=1, source_target_pairs={{0,1},{1,2},{2,3},{3,4},{4,5},{5,6},{6,7},{7,8},{8,9},{9,10},{10,1... | collective-permute-start | bytes 98312 | tf_op jit(solution)/shard_map/ppermute | solution.py:67
  15.5 21.9 %collective-permute-start.2 = (bf16[2,64,128]{2,1,0:T(8,128)(2,1)S(1)}, bf16[2,64,128]{2,1,0:T(8,128)(2,1)S(1)}, u32[]{:S(2)}, u32[]{:S(2)}) collective-permute-start(bf16[2,64,128]{2,1,0:T(8,128)(2,1)S(1)} %get-tuple-element.16), channel_id=1, source_target_pairs={{1,0},{2,1},{3,2},{4,3},{5,4},{6,5},{7,6},{8,7},{9,8},{10,9},{11,1... | collective-permute-start | bytes 98312 | tf_op jit(solution)/shard_map/ppermute | solution.py:70
  35.1 2.4 %copy-start.3 = (bf16[512,128]{1,0:T(8,128)(2,1)S(1)}, bf16[512,128]{1,0:T(8,128)(2,1)}, u32[]{:S(2)}) copy-start(bf16[512,128]{1,0:T(8,128)(2,1)} %param.10) | copy-start | bytes 393220
  35.1 2.4 %copy-start.4 = (bf16[512,128]{1,0:T(8,128)(2,1)S(1)}, bf16[512,128]{1,0:T(8,128)(2,1)}, u32[]{:S(2)}) copy-start(bf16[512,128]{1,0:T(8,128)(2,1)} %param.11) | copy-start | bytes 393220
  42.9 2.4 %copy-start.1 = (bf16[8192,128]{1,0:T(8,128)(2,1)S(1)}, bf16[8192,128]{1,0:T(8,128)(2,1)}, u32[]{:S(2)}) copy-start(bf16[8192,128]{1,0:T(8,128)(2,1)} %get-tuple-element.8) | copy-start | bytes 6291460
  55.8 0.7 copy-start.5
  157.4 2.8 %copy-start.2 = (f32[8192,128]{1,0:T(8,128)S(1)}, f32[8192,128]{1,0:T(8,128)}, u32[]{:S(2)}) copy-start(f32[8192,128]{1,0:T(8,128)} %get-tuple-element.7) | copy-start | bytes 12582916
Sparse Core Ops, SparseCore 0:
  55.9 57.7 reduce-scatter.3

commit v4 on v3

--- a/solution.py
+++ b/solution.py
@@ -155,31 +155,49 @@
     member_dev = member_vectors.shape[1]
     members = member_dev * lax.axis_size("mem")
     per_region = block_obs.shape[0]
-    share = per_region // lax.axis_size("mem")
-    mesh_point_entries = first_guess_state.reshape(per_region, BLOCK, member_dev)
+    parts = lax.axis_size("mem")
+    pairs = per_region // 2
+    share = pairs // parts
     slots = extended.shape[1]
     picks = (block_obs.reshape(-1)[:, None] == jnp.arange(slots)[None, :]).astype(jnp.bfloat16)
-    both = jnp.concatenate([extended[0], extended[1]], 1)
-    rows = jnp.dot(picks, both, preferred_element_type=jnp.float32).astype(jnp.bfloat16)
-    obs_rows = rows[:, :member_dev].reshape(per_region, KB, member_dev)
-    incr_rows = rows[:, member_dev:].reshape(per_region, KB, member_dev)
-    partial_value = block_sums(mesh_point_entries, obs_rows)
-    flat = BLOCK * KB
-    payload = jnp.concatenate(
-        [partial_value[0].reshape(per_region, flat), partial_value[1], partial_value[2]], 1
-    )
-    parts = lax.axis_size("mem")
-    got = lax.psum_scatter(payload.reshape(parts, share, -1), "mem", scatter_dimension=0, tiled=True)
-    got = got.reshape(share, -1)
-    cross = got[:, :flat].reshape(share, BLOCK, KB)
-    sum_cells = got[:, flat : flat + BLOCK]
-    sum_obs = got[:, flat + BLOCK :]
-    first_block = lax.axis_index("mem") * share
-    live_counts = lax.dynamic_slice_in_dim(block_count, first_block, share, 0)
-    positions = lax.dynamic_slice_in_dim(obs_offset, first_block, share, 0)
-    own_cov = covariances(cross, sum_cells, sum_obs, positions, live_counts, members)
+    obs_rows = jnp.dot(picks, extended[0], preferred_element_type=jnp.float32).astype(jnp.bfloat16)
+    incr_rows = jnp.dot(picks, extended[1], preferred_element_type=jnp.float32).astype(jnp.bfloat16)
+    cells_p = first_guess_state.reshape(pairs, 2 * BLOCK, member_dev)
+    obs_p = obs_rows.reshape(pairs, 2 * KB, member_dev)
+    full = jnp.einsum("brm,blm->brl", cells_p, obs_p, preferred_element_type=jnp.float32)
+    upper = (jnp.arange(2 * KB) >= KB)[None, None, :]
+    cross = jnp.where(upper, full[:, BLOCK:, :], full[:, :BLOCK, :])
+    sum_cells = jnp.sum(first_guess_state.astype(jnp.float32), 1).reshape(pairs, 1, 2 * BLOCK)
+    sum_obs = jnp.sum(obs_rows.astype(jnp.float32), 1).reshape(pairs, 1, 2 * KB)
+    payload = jnp.concatenate([cross, sum_cells, sum_obs], 1)
+    got = lax.psum_scatter(
+        payload.reshape(parts, share, BLOCK + 2, 2 * KB), "mem", scatter_dimension=0, tiled=True
+    ).reshape(share, BLOCK + 2, 2 * KB)
+    cross = got[:, :BLOCK, :]
+    cells_sum = jnp.transpose(got[:, BLOCK, :].reshape(share, 2, BLOCK), (0, 2, 1))
+    cells_sum = jnp.broadcast_to(cells_sum[:, :, :, None], (share, BLOCK, 2, KB)).reshape(
+        share, BLOCK, 2 * KB
+    )
+    obs_sum = got[:, BLOCK + 1, :][:, None, :]
+    first_block = lax.axis_index("mem") * share * 2
+    live_counts = lax.dynamic_slice_in_dim(block_count, first_block, share * 2, 0)
+    positions = lax.dynamic_slice_in_dim(obs_offset, first_block, share * 2, 0)
+    position = jnp.arange(BLOCK).astype(jnp.float32)
+    distance = (position[None, :, None] - positions.reshape(share, 1, 2 * KB)) / (0.5 * BLOCK)
+    lane = jnp.arange(2 * KB)
+    counts = live_counts.reshape(share, 2)[:, lane // KB]
+    active = (lane % KB)[None, :] < counts
+    taper = jnp.where(active[:, None, :], 1.0 / (1.0 + distance * distance), 0.0)
+    own_cov = (
+        (cross - cells_sum * obs_sum / members) / (members - 1) * taper
+    ).astype(jnp.bfloat16)
     covariance = gathered_copies(own_cov, "mem", 0)
-    correction_delta = apply_cov(covariance, incr_rows)
+    same_block = (jnp.arange(2 * BLOCK) // BLOCK)[:, None] == (lane // KB)[None, :]
+    spread = jnp.where(same_block[None], jnp.concatenate([covariance, covariance], 1), 0)
+    incr_p = incr_rows.reshape(pairs, 2 * KB, member_dev)
+    correction_delta = jnp.einsum(
+        "brl,blm->brm", spread, incr_p, preferred_element_type=jnp.float32
+    ).astype(jnp.bfloat16)
     returned = correction_delta.reshape(per_region * BLOCK, member_dev)
     return concentration_map + returned.astype(jnp.float32)
 

time: 171 us -> 155 us (0.906)
  blocking collectives: 36 us -> 0 us
  waiting for transfers between devices: 57 us -> 78.8 us
  local copies, waits for them, and re-layouts: 28.1 us -> 15.9 us
  starting transfers between devices: 6.98 us -> 14.8 us
  other arithmetic: 6.63 us -> 9.07 us
    unnamed x2 -> x1, waiting for transfers between devices: 57 us -> 0.02 us
    reduce_scatter x0 -> x1, waiting for transfers between devices: none -> 56.6 us  [per_device(): lax.psum_scatter(payload.reshape(parts, share, BLOCK + 2, 2 * KB), 'mem',...]
    all_to_all x1 -> x0, blocking collectives: 36 us -> none  [from_everyone(): return lax.all_to_all(copies, axis, split_axis=0, concat_axis=0, tiled=True)]
    all_to_all x0 -> x1, waiting for transfers between devices: none -> 22.2 us  [from_everyone(): return lax.all_to_all(copies, axis, split_axis=0, concat_axis=0, tiled=True)]
    all_to_all x0 -> x1, starting transfers between devices: none -> 7.82 us  [from_everyone(): return lax.all_to_all(copies, axis, split_axis=0, concat_axis=0, tiled=True)]
    concatenate x4 -> x0, local copies, waits for them, and re-layouts: 5.74 us -> none  [per_device(): jnp.concatenate([partial_value[0].reshape(per_region, flat), partial_valu...]
    unnamed x15, local copies, waits for them, and re-layouts: 7.1 us -> 1.6 us
    slice x3 -> x1, local copies, waits for them, and re-layouts: 4.09 us -> 0.81 us  [per_device(): obs_sum = got[:, BLOCK + 1, :][:, None, :]]
  transfers between devices with their start and end apart: 4 -> 5, of which waited for: 1 -> 2; matrix products, arithmetic and copies ran while one was open for 8% -> 12% of each run, Pallas kernels for 6% -> 6%
where the time goes in v4:
time: 155 us; the launch traced here: 154 us
  waiting for transfers between devices  78.8 us (51%)
  local copies, waits for them, and re-layouts  15.9 us (10%)
  starting transfers between devices  14.8 us (10%)
  between operations  13.6 us (9%)
  matrix products  12.7 us (8%)
  Pallas kernels  9.61 us (6%)
  other arithmetic  9.07 us (6%)
    reduce_scatter x1, waiting for transfers between devices, per_device(): lax.psum_scatter(payload.reshape(parts, share, BLOCK + 2, 2 * KB), 'mem',...  56.6 us
    all_to_all x1, waiting for transfers between devices, from_everyone(): return lax.all_to_all(copies, axis, split_axis=0, concat_axis=0, tiled=True)  22.2 us
    pallas_call x1, Pallas kernels, advect(): pl.pallas_call(advect_kernel, grid=(cells // rows,), in_specs=[pl.BlockSp...  9.61 us
    all_to_all x1, starting transfers between devices, from_everyone(): return lax.all_to_all(copies, axis, split_axis=0, concat_axis=0, tiled=True)  7.82 us
    dot_general x1, matrix products, per_device(): jnp.dot(picks, extended[1], preferred_element_type=jnp.float32)  5.73 us
    dot_general x1, matrix products, per_device(): jnp.dot(picks, extended[0], preferred_element_type=jnp.float32)  4.75 us
    ppermute x1, starting transfers between devices, padded(): lax.ppermute(lax.slice_in_dim(block, 0, width, axis=dim), axis, backward)  3.49 us
    broadcast_in_dim x1, local copies, waits for them, and re-layouts, advect(): speeds[:, None]  3.37 us
  transfers between devices with their start and end apart: 5, of which 2 were waited for; matrix products, arithmetic and copies ran while one was open for 12% of the time, Pallas kernels for 6%

profile of v4, /device:TPU:1, one launch (start us, length us, event | category | flops | bytes accessed | tf_op | source)
XLA Modules:
  0.0 154.5 jit_solution(2202168134007162369)
XLA Ops:
  6.5 0.8 slice_bitcast_fusion.4
  7.4 0.7 slice.81
  8.1 2.1 %collective-permute-start = (f32[4,129]{1,0:T(4,128)S(1)}, f32[4,129]{1,0:T(4,128)S(1)}, u32[]{:S(2)}, u32[]{:S(2)}) collective-permute-start(f32[4,129]{1,0:T(4,128)S(1)} %pad_maximum_fusion.3), channel_id=1, source_target_pairs={{15,0},{0,1},{1,2},{2,3},{3,4},{4,5},{5,6},{6,7},{7,8},{8,9},{9,10... | collective-permute-start | bytes 6200 | tf_op jit(solution)/shard_map/ppermute | solution.py:58
  10.2 0.8 reshape.192
  11.0 1.6 %gather_fusion = bf16[128,128]{1,0:T(8,128)(2,1)S(1)} fusion(bf16[512,128]{1,0:T(8,128)(2,1)} %param.10, s32[1024]{0:T(1024)S(1)} %pad_clamp_fusion.1), kind=kCustom, calls=%fused_computation | custom fusion | bytes 66048 | tf_op jit(solution)/shard_map/gather | solution.py:150
  12.6 1.6 %gather_fusion.1 = bf16[128,128]{1,0:T(8,128)(2,1)S(1)} fusion(bf16[512,128]{1,0:T(8,128)(2,1)} %param.11, s32[1024]{0:T(1024)S(1)} %pad_clamp_fusion.1), kind=kCustom, calls=%fused_computation.1 | custom fusion | bytes 66048 | tf_op jit(solution)/shard_map/gather | solution.py:150
  14.2 1.4 collective-permute-start.1
  15.5 3.5 %collective-permute-start.2 = (bf16[2,64,128]{2,1,0:T(8,128)(2,1)S(1)}, bf16[2,64,128]{2,1,0:T(8,128)(2,1)S(1)}, u32[]{:S(2)}, u32[]{:S(2)}) collective-permute-start(bf16[2,64,128]{2,1,0:T(8,128)(2,1)S(1)} %get-tuple-element.12), channel_id=1, source_target_pairs={{1,0},{2,1},{3,2},{4,3},{5,4},{6,5},{7,6},{8,7},{9,8},{10,9},{11,1... | collective-permute-start | bytes 98312 | tf_op jit(solution)/shard_map/ppermute | solution.py:70
  19.0 3.4 %copy.14.s_ref = f32[8192,1]{1,0:T(8,128)} copy(f32[8192,1]{0,1:T(1,128)} %bitcast.49) | data formatting | bytes 65536 | tf_op jit(solution)/shard_map/broadcast_in_dim | solution.py:44
  22.6 0.1 slice_reduce_fusion.1
  23.0 0.6 slice.114
  23.6 0.6 multiply_subtract_fusion.1
  24.2 0.6 concatenate.23.halo_ref
  24.8 9.6 %shard_map.82 = (f32[8192,128]{1,0:T(8,128)}, bf16[8192,128]{1,0:T(8,128)(2,1)}) custom-call(f32[8,128]{1,0:T(8,128)} %concatenate.23.halo_ref, f32[8192,1]{1,0:T(8,128)} %copy.14.s_ref, f32[8192,128]{1,0:T(8,128)} %x_ref.1), custom_call_target="tpu_custom_call" | custom-call | tf_op jit(solution)/shard_map/pallas_call | solution.py:31
  34.4 2.2 %convert_reduce_fusion.1 = f32[8192]{0:T(1024)S(1)} fusion(bf16[8192,128]{1,0:T(8,128)(2,1)} %get-tuple-element.8), kind=kLoop, calls=%fused_computation.12 | loop fusion | flops 2088960 | bytes 2129920 | tf_op jit(solution)/shard_map/reduce_sum | solution.py:170
  36.7 4.7 %convert_reduce_fusion = (f32[8192]{0:T(1024)S(1)}, bf16[8192,128]{1,0:T(8,128)(2,1)S(1)}) fusion(bf16[2,640,128]{2,1,0:T(8,128)(2,1)S(1)} %pad_maximum_fusion.1, s32[8192]{0:T(1024)S(1)} %eq.37), kind=kOutput, calls=%fused_computation.11 | convolution fusion | flops 1350557696 | bytes 2326528 | tf_op jit(solution)/shard_map/dot_general | solution.py:163
  41.5 1.6 %fusion.23 = f32[64,128,128]{2,1,0:T(8,128)S(1)} fusion(bf16[64,128,128]{2,1,0:T(8,128)(2,1)S(1)} %bitcast.39, bf16[64,128,128]{2,1,0:T(8,128)(2,1)S(1)} %bitcast.40), kind=kOutput, calls=%fused_computation.66 | convolution fusion | flops 268435456 | bytes 8388608 | tf_op jit(solution)/shard_map/brm,blm->brl/dot_general | solution.py:167
  43.1 0.5 slice_select_fusion
  43.5 1.7 %pad_maximum_fusion = f32[16,4,66,128]{3,2,1,0:T(8,128)} fusion(f32[16,4,1,128]{3,2,1,0:T(1,128)S(1)} %bitcast.50, f32[16,4,1,128]{3,2,1,0:T(1,128)S(1)} %bitcast.44, f32[16,4,64,128]{3,2,1,0:T(8,128)S(1)} %bitcast.38), kind=kLoop, calls=%fused_computation.13 | loop fusion | flops 1081344 | bytes 4325376 | tf_op jit(solution)/shard_map/concatenate | solution.py:172
  45.5 0.6 gather_fusion.2
  46.6 56.6 %reduce-scatter.2.cloned.1.call-done = f32[1,4,66,128]{3,2,1,0:T(8,128)} async-done(((f32[16,4,66,128]{3,2,1,0:T(8,128)}), f32[1,4,66,128]{3,2,1,0:T(8,128)}) %reduce-scatter.2.cloned.1.call-update) | async-done | bytes 135184 | tf_op jit(solution)/shard_map/reduce_scatter | solution.py:173
  103.2 0.8 fusion.22
  104.2 0.3 broadcast_in_dim.69
  104.5 0.2 reshape.195
  104.7 1.0 fusion.14
  105.7 1.2 broadcast_in_dim.72
  107.0 7.8 %all-to-all-start = ((bf16[16,4,64,128]{3,2,1,0:T(8,128)(2,1)}), bf16[16,4,64,128]{3,2,1,0:T(8,128)(2,1)S(1)}, u32[]{:S(2)}, u32[]{:S(2)}) async-start(bf16[16,4,64,128]{3,2,1,0:T(8,128)(2,1)} %broadcast_in_dim.72), calls=%async_computation.1 | async-start | bytes 2097152 | tf_op jit(solution)/shard_map/all_to_all | solution.py:94
  114.9 5.7 %fusion.5 = bf16[8192,128]{1,0:T(8,128)(2,1)S(1)} fusion(s32[8192]{0:T(1024)S(1)} %eq.37, bf16[2,640,128]{2,1,0:T(8,128)(2,1)S(1)} %pad_maximum_fusion.1), kind=kOutput, calls=%fused_computation.9 | convolution fusion | flops 1348468736 | bytes 2293760 | tf_op jit(solution)/shard_map/dot_general | solution.py:164
  120.6 22.2 %all-to-all-done = bf16[16,4,64,128]{3,2,1,0:T(8,128)(2,1)S(1)} async-done(((bf16[16,4,64,128]{3,2,1,0:T(8,128)(2,1)}), bf16[16,4,64,128]{3,2,1,0:T(8,128)(2,1)S(1)}, u32[]{:S(2)}, u32[]{:S(2)}) %all-to-all-start) | async-done | bytes 1048608 | tf_op jit(solution)/shard_map/all_to_all | solution.py:94
  142.8 0.7 fusion.10
  143.5 1.5 copy-done.2
  145.0 2.7 %convert_add_fusion = f32[8192,128]{1,0:T(8,128)} fusion(f32[8192,128]{1,0:T(8,128)S(1)} %copy-done.2, bf16[64,128,128]{2,1,0:T(8,128)(2,1)S(1)} %fusion.10), kind=kLoop, calls=%fused_computation.10 | loop fusion | flops 2097152 | bytes 10485760 | tf_op jit(solution)/shard_map/add | solution.py:202
  (49 shorter events, 1.6 us)
Async XLA Ops:
  6.5 39.8 %copy-start = (f32[128,64]{0,1:T(8,128)S(1)}, f32[128,64]{0,1:T(8,128)}, u32[]{:S(2)}) copy-start(f32[128,64]{0,1:T(8,128)} %param.15) | copy-start | bytes 98308
  6.5 96.6 %reduce-scatter.2.cloned.1.call-start = ((), (), s32[]{:S(2)}) async-start(), calls=%async_computation.2 | async-start | bytes 2506752 | tf_op jit(solution)/shard_map/reduce_scatter | solution.py:173
  8.1 14.5 %collective-permute-start = (f32[4,129]{1,0:T(4,128)S(1)}, f32[4,129]{1,0:T(4,128)S(1)}, u32[]{:S(2)}, u32[]{:S(2)}) collective-permute-start(f32[4,129]{1,0:T(4,128)S(1)} %pad_maximum_fusion.3), channel_id=1, source_target_pairs={{15,0},{0,1},{1,2},{2,3},{3,4},{4,5},{5,6},{6,7},{7,8},{8,9},{9,10... | collective-permute-start | bytes 6200 | tf_op jit(solution)/shard_map/ppermute | solution.py:58
  12.6 9.8 %copy-start.5 = (s32[128,64]{0,1:T(8,128)S(1)}, s32[128,64]{0,1:T(8,128)}, u32[]{:S(2)}) copy-start(s32[128,64]{0,1:T(8,128)} %param.13) | copy-start | bytes 98308
  14.2 22.5 %collective-permute-start.1 = (bf16[2,64,128]{2,1,0:T(8,128)(2,1)S(1)}, bf16[2,64,128]{2,1,0:T(8,128)(2,1)S(1)}, u32[]{:S(2)}, u32[]{:S(2)}) collective-permute-start(bf16[2,64,128]{2,1,0:T(8,128)(2,1)S(1)} %get-tuple-element.11), channel_id=1, source_target_pairs={{0,1},{1,2},{2,3},{3,4},{4,5},{5,6},{6,7},{7,8},{8,9},{9,10},{10,1... | collective-permute-start | bytes 98312 | tf_op jit(solution)/shard_map/ppermute | solution.py:67
  15.5 21.1 %collective-permute-start.2 = (bf16[2,64,128]{2,1,0:T(8,128)(2,1)S(1)}, bf16[2,64,128]{2,1,0:T(8,128)(2,1)S(1)}, u32[]{:S(2)}, u32[]{:S(2)}) collective-permute-start(bf16[2,64,128]{2,1,0:T(8,128)(2,1)S(1)} %get-tuple-element.12), channel_id=1, source_target_pairs={{1,0},{2,1},{3,2},{4,3},{5,4},{6,5},{7,6},{8,7},{9,8},{10,9},{11,1... | collective-permute-start | bytes 98312 | tf_op jit(solution)/shard_map/ppermute | solution.py:70
  24.8 11.9 %copy-start.3 = (bf16[512,128]{1,0:T(8,128)(2,1)S(1)}, bf16[512,128]{1,0:T(8,128)(2,1)}, u32[]{:S(2)}) copy-start(bf16[512,128]{1,0:T(8,128)(2,1)} %param.10) | copy-start | bytes 393220
  24.8 11.9 %copy-start.4 = (bf16[512,128]{1,0:T(8,128)(2,1)S(1)}, bf16[512,128]{1,0:T(8,128)(2,1)}, u32[]{:S(2)}) copy-start(bf16[512,128]{1,0:T(8,128)(2,1)} %param.11) | copy-start | bytes 393220
  36.7 4.8 %copy-start.1 = (bf16[8192,128]{1,0:T(8,128)(2,1)S(1)}, bf16[8192,128]{1,0:T(8,128)(2,1)}, u32[]{:S(2)}) copy-start(bf16[8192,128]{1,0:T(8,128)(2,1)} %get-tuple-element.8) | copy-start | bytes 6291460
  43.5 1.7 %copy-start.6 = (s32[128]{0:T(128)S(1)}, s32[128]{0:T(128)}, u32[]{:S(2)}) copy-start(s32[128]{0:T(128)} %param.14) | copy-start | bytes 1540
  107.0 35.8 %all-to-all-start = ((bf16[16,4,64,128]{3,2,1,0:T(8,128)(2,1)}), bf16[16,4,64,128]{3,2,1,0:T(8,128)(2,1)S(1)}, u32[]{:S(2)}, u32[]{:S(2)}) async-start(bf16[16,4,64,128]{3,2,1,0:T(8,128)(2,1)} %broadcast_in_dim.72), calls=%async_computation.1 | async-start | bytes 2097152 | tf_op jit(solution)/shard_map/all_to_all | solution.py:94
  142.8 2.2 %copy-start.2 = (f32[8192,128]{1,0:T(8,128)S(1)}, f32[8192,128]{1,0:T(8,128)}, u32[]{:S(2)}) copy-start(f32[8192,128]{1,0:T(8,128)} %get-tuple-element.7) | copy-start | bytes 12582916
Sparse Core Ops, SparseCore 0:
  45.4 57.7 reduce-scatter.1

commit v5 on v4

--- a/solution.py
+++ b/solution.py
@@ -15,7 +15,10 @@
     def _():
         carry_ref[...] = halo_ref[...]
     x = x_ref[...]
-    s = jnp.broadcast_to(s_ref[...], x.shape)
+    lanes = x.shape[1]
+    s = jnp.concatenate(
+        [jnp.broadcast_to(s_ref[q : q + 1, :], (lanes, lanes)).T for q in range(s_ref.shape[0])], 0
+    )
     first = lax.broadcasted_iota(jnp.int32, x.shape, 0) == 0
     last = x.shape[0] - 1
     for k in range(STEPS):
@@ -33,7 +36,7 @@
         grid=(cells // rows,),
         in_specs=[
             pl.BlockSpec((8, width), lambda t: (0, 0)),
-            pl.BlockSpec((rows, 1), lambda t: (t, 0)),
+            pl.BlockSpec((rows // width, width), lambda t: (t, 0)),
             pl.BlockSpec((rows, width), lambda t: (t, 0)),
         ],
         out_specs=[pl.BlockSpec((rows, width), lambda t: (t, 0)), pl.BlockSpec((rows, width), lambda t: (t, 0))],
@@ -41,7 +44,7 @@
         scratch_shapes=[pltpu.VMEM((8, width), jnp.float32)],
         compiler_params=pltpu.CompilerParams(dimension_semantics=("arbitrary",)),
         interpret=interpret,
-    )(halo, speeds[:, None], x)
+    )(halo, speeds.reshape(-1, width), x)
 
 def halo_rows(arrived, arrived_speeds, width):
     v = arrived
@@ -147,7 +150,14 @@
     concentration_map, first_guess_state = advect(halo, flow_speed_ratio, concentration_map)
     lend = edge_list.shape[2]
     edge_rows = edge_list.reshape(-1)
-    chosen = jnp.stack([obs_pert[edge_rows], obs_incr[edge_rows]])
+    own = obs_pert.shape[0]
+    lent = (edge_rows[:, None] == jnp.arange(own)[None, :]).astype(jnp.bfloat16)
+    chosen = jnp.stack(
+        [
+            jnp.dot(lent, obs_pert, preferred_element_type=jnp.float32).astype(jnp.bfloat16),
+            jnp.dot(lent, obs_incr, preferred_element_type=jnp.float32).astype(jnp.bfloat16),
+        ]
+    )
     rimmed = padded(chosen, (("reg", 1),), lend)
     extended = jnp.concatenate(
         [rimmed[:, :lend], jnp.stack([obs_pert, obs_incr]), rimmed[:, -lend:]], 1

time: 155 us -> 150 us (0.968)
  local copies, waits for them, and re-layouts: 15.9 us -> 10.1 us
  matrix products: 12.7 us -> 15 us
    broadcast_in_dim x1 -> x0, local copies, waits for them, and re-layouts: 3.37 us -> none  [advect(): speeds[:, None]]
    gather x2 -> x0, local copies, waits for them, and re-layouts: 3.15 us -> none  [per_device(): chosen = jnp.stack([obs_pert[edge_rows], obs_incr[edge_rows]])]
    dot_general x0 -> x2, matrix products: none -> 2.27 us  [the longest x1 1.13 us: per_device(): jnp.dot(lent, obs_incr, preferred_element_type=jnp.float32)]
  transfers between devices with their start and end apart: 5 -> 5, of which waited for: 2 -> 2; matrix products, arithmetic and copies ran while one was open for 12% -> 10% of each run, Pallas kernels for 6% -> 6%
where the time goes in v5:
time: 150 us
  waiting for transfers between devices  78.7 us (52%)
  matrix products  15 us (10%)
  starting transfers between devices  14.9 us (10%)
  between operations  13.6 us (9%)
  local copies, waits for them, and re-layouts  10.1 us (7%)
  other arithmetic  9.09 us (6%)
  Pallas kernels  8.42 us (6%)
    reduce_scatter x1, waiting for transfers between devices, per_device(): lax.psum_scatter(payload.reshape(parts, share, BLOCK + 2, 2 * KB), 'mem',...  56.5 us
    all_to_all x1, waiting for transfers between devices, from_everyone(): return lax.all_to_all(copies, axis, split_axis=0, concat_axis=0, tiled=True)  22.2 us
    pallas_call x1, Pallas kernels, advect(): pl.pallas_call(advect_kernel, grid=(cells // rows,), in_specs=[pl.BlockSp...  8.42 us
    all_to_all x1, starting transfers between devices, from_everyone(): return lax.all_to_all(copies, axis, split_axis=0, concat_axis=0, tiled=True)  7.88 us
    dot_general x1, matrix products, per_device(): jnp.dot(picks, extended[1], preferred_element_type=jnp.float32)  5.73 us
    dot_general x1, matrix products, per_device(): jnp.dot(picks, extended[0], preferred_element_type=jnp.float32)  4.75 us
    ppermute x1, starting transfers between devices, padded(): lax.ppermute(lax.slice_in_dim(block, 0, width, axis=dim), axis, backward)  3.49 us
  transfers between devices with their start and end apart: 5, of which 2 were waited for; matrix products, arithmetic and copies ran while one was open for 10% of the time, Pallas kernels for 6%

profile of v5, /device:TPU:1, one launch (start us, length us, event | category | flops | bytes accessed | tf_op | source)
XLA Modules:
  0.0 149.8 jit_solution(2288643600408298961)
XLA Ops:
  6.5 0.8 slice_bitcast_fusion.4
  7.4 0.7 slice.81
  8.1 2.1 %collective-permute-start = (f32[4,129]{1,0:T(4,128)S(1)}, f32[4,129]{1,0:T(4,128)S(1)}, u32[]{:S(2)}, u32[]{:S(2)}) collective-permute-start(f32[4,129]{1,0:T(4,128)S(1)} %pad_maximum_fusion.3), channel_id=1, source_target_pairs={{15,0},{0,1},{1,2},{2,3},{3,4},{4,5},{5,6},{6,7},{7,8},{8,9},{9,10... | collective-permute-start | bytes 6200 | tf_op jit(solution)/shard_map/ppermute | solution.py:61
  10.2 0.8 eq.56
  11.0 1.1 fusion.11
  12.1 1.1 fusion.12
  13.3 1.4 collective-permute-start.1
  14.6 3.5 %collective-permute-start.2 = (bf16[2,64,128]{2,1,0:T(8,128)(2,1)S(1)}, bf16[2,64,128]{2,1,0:T(8,128)(2,1)S(1)}, u32[]{:S(2)}, u32[]{:S(2)}) collective-permute-start(bf16[2,64,128]{2,1,0:T(8,128)(2,1)S(1)} %get-tuple-element.12), channel_id=1, source_target_pairs={{1,0},{2,1},{3,2},{4,3},{5,4},{6,5},{7,6},{8,7},{9,8},{10,9},{11,1... | collective-permute-start | bytes 98312 | tf_op jit(solution)/shard_map/ppermute | solution.py:73
  18.1 0.8 copy.14
  19.5 0.5 slice.110
  20.0 0.7 multiply_subtract_fusion.1
  20.7 0.6 concatenate.23.halo_ref
  21.3 8.4 %shard_map.82 = (f32[8192,128]{1,0:T(8,128)}, bf16[8192,128]{1,0:T(8,128)(2,1)}) custom-call(f32[8,128]{1,0:T(8,128)} %concatenate.23.halo_ref, f32[64,128]{1,0:T(8,128)} %bitcast.49, f32[8192,128]{1,0:T(8,128)} %x_ref.1), custom_call_target="tpu_custom_call" | custom-call | tf_op jit(solution)/shard_map/pallas_call | solution.py:34
  29.7 2.2 %convert_reduce_fusion.1 = f32[8192]{0:T(1024)S(1)} fusion(bf16[8192,128]{1,0:T(8,128)(2,1)} %get-tuple-element.8), kind=kLoop, calls=%fused_computation.10 | loop fusion | flops 2088960 | bytes 2129920 | tf_op jit(solution)/shard_map/reduce_sum | solution.py:180
  32.0 4.7 %convert_reduce_fusion = (f32[8192]{0:T(1024)S(1)}, bf16[8192,128]{1,0:T(8,128)(2,1)S(1)}) fusion(bf16[2,640,128]{2,1,0:T(8,128)(2,1)S(1)} %pad_maximum_fusion.1, s32[8192]{0:T(1024)S(1)} %eq.52), kind=kOutput, calls=%fused_computation.9 | convolution fusion | flops 1350557696 | bytes 2326528 | tf_op jit(solution)/shard_map/dot_general | solution.py:173
  36.8 1.6 %fusion.26 = f32[64,128,128]{2,1,0:T(8,128)S(1)} fusion(bf16[64,128,128]{2,1,0:T(8,128)(2,1)S(1)} %bitcast.41, bf16[64,128,128]{2,1,0:T(8,128)(2,1)S(1)} %bitcast.42), kind=kOutput, calls=%fused_computation.68 | convolution fusion | flops 268435456 | bytes 8388608 | tf_op jit(solution)/shard_map/brm,blm->brl/dot_general | solution.py:177
  38.3 0.5 slice_select_fusion
  38.8 1.7 %pad_maximum_fusion = f32[16,4,66,128]{3,2,1,0:T(8,128)} fusion(f32[16,4,1,128]{3,2,1,0:T(1,128)S(1)} %bitcast.50, f32[16,4,1,128]{3,2,1,0:T(1,128)S(1)} %bitcast.44, f32[16,4,64,128]{3,2,1,0:T(8,128)S(1)} %bitcast.40), kind=kLoop, calls=%fused_computation.11 | loop fusion | flops 1081344 | bytes 4325376 | tf_op jit(solution)/shard_map/concatenate | solution.py:182
  40.8 0.6 gather_fusion
  41.9 56.5 %reduce-scatter.2.cloned.1.call-done = f32[1,4,66,128]{3,2,1,0:T(8,128)} async-done(((f32[16,4,66,128]{3,2,1,0:T(8,128)}), f32[1,4,66,128]{3,2,1,0:T(8,128)}) %reduce-scatter.2.cloned.1.call-update) | async-done | bytes 135184 | tf_op jit(solution)/shard_map/reduce_scatter | solution.py:183
  98.4 0.8 fusion.25
  99.3 0.1 copy.15
  99.4 0.3 broadcast_in_dim.64
  99.8 0.2 reshape.168
  99.9 1.0 fusion.16
  101.0 1.2 broadcast_in_dim.67
  102.2 7.9 %all-to-all-start = ((bf16[16,4,64,128]{3,2,1,0:T(8,128)(2,1)}), bf16[16,4,64,128]{3,2,1,0:T(8,128)(2,1)S(1)}, u32[]{:S(2)}, u32[]{:S(2)}) async-start(bf16[16,4,64,128]{3,2,1,0:T(8,128)(2,1)} %broadcast_in_dim.67), calls=%async_computation.1 | async-start | bytes 2097152 | tf_op jit(solution)/shard_map/all_to_all | solution.py:97
  110.2 5.7 %fusion.5 = bf16[8192,128]{1,0:T(8,128)(2,1)S(1)} fusion(s32[8192]{0:T(1024)S(1)} %eq.52, bf16[2,640,128]{2,1,0:T(8,128)(2,1)S(1)} %pad_maximum_fusion.1), kind=kOutput, calls=%fused_computation.7 | convolution fusion | flops 1348468736 | bytes 2293760 | tf_op jit(solution)/shard_map/dot_general | solution.py:174
  115.9 22.2 %all-to-all-done = bf16[16,4,64,128]{3,2,1,0:T(8,128)(2,1)S(1)} async-done(((bf16[16,4,64,128]{3,2,1,0:T(8,128)(2,1)}), bf16[16,4,64,128]{3,2,1,0:T(8,128)(2,1)S(1)}, u32[]{:S(2)}, u32[]{:S(2)}) %all-to-all-start) | async-done | bytes 1048608 | tf_op jit(solution)/shard_map/all_to_all | solution.py:97
  138.1 0.7 fusion.10
  138.8 1.5 copy-done.2
  140.2 2.7 %convert_add_fusion = f32[8192,128]{1,0:T(8,128)} fusion(f32[8192,128]{1,0:T(8,128)S(1)} %copy-done.2, bf16[64,128,128]{2,1,0:T(8,128)(2,1)S(1)} %fusion.10), kind=kLoop, calls=%fused_computation.8 | loop fusion | flops 2097152 | bytes 10485760 | tf_op jit(solution)/shard_map/add | solution.py:212
  (44 shorter events, 1.5 us)
Async XLA Ops:
  6.5 35.1 %copy-start = (f32[128,64]{0,1:T(8,128)S(1)}, f32[128,64]{0,1:T(8,128)}, u32[]{:S(2)}) copy-start(f32[128,64]{0,1:T(8,128)} %param.15) | copy-start | bytes 98308
  6.5 91.9 %reduce-scatter.2.cloned.1.call-start = ((), (), s32[]{:S(2)}) async-start(), calls=%async_computation.2 | async-start | bytes 2506752 | tf_op jit(solution)/shard_map/reduce_scatter | solution.py:183
  8.1 11.0 %collective-permute-start = (f32[4,129]{1,0:T(4,128)S(1)}, f32[4,129]{1,0:T(4,128)S(1)}, u32[]{:S(2)}, u32[]{:S(2)}) collective-permute-start(f32[4,129]{1,0:T(4,128)S(1)} %pad_maximum_fusion.3), channel_id=1, source_target_pairs={{15,0},{0,1},{1,2},{2,3},{3,4},{4,5},{5,6},{6,7},{7,8},{8,9},{9,10... | collective-permute-start | bytes 6200 | tf_op jit(solution)/shard_map/ppermute | solution.py:61
  13.3 18.6 %collective-permute-start.1 = (bf16[2,64,128]{2,1,0:T(8,128)(2,1)S(1)}, bf16[2,64,128]{2,1,0:T(8,128)(2,1)S(1)}, u32[]{:S(2)}, u32[]{:S(2)}) collective-permute-start(bf16[2,64,128]{2,1,0:T(8,128)(2,1)S(1)} %get-tuple-element.11), channel_id=1, source_target_pairs={{0,1},{1,2},{2,3},{3,4},{4,5},{5,6},{6,7},{7,8},{8,9},{9,10},{10,1... | collective-permute-start | bytes 98312 | tf_op jit(solution)/shard_map/ppermute | solution.py:70
  14.6 17.3 %collective-permute-start.2 = (bf16[2,64,128]{2,1,0:T(8,128)(2,1)S(1)}, bf16[2,64,128]{2,1,0:T(8,128)(2,1)S(1)}, u32[]{:S(2)}, u32[]{:S(2)}) collective-permute-start(bf16[2,64,128]{2,1,0:T(8,128)(2,1)S(1)} %get-tuple-element.12), channel_id=1, source_target_pairs={{1,0},{2,1},{3,2},{4,3},{5,4},{6,5},{7,6},{8,7},{9,8},{10,9},{11,1... | collective-permute-start | bytes 98312 | tf_op jit(solution)/shard_map/ppermute | solution.py:73
  21.3 10.7 %copy-start.3 = (bf16[512,128]{1,0:T(8,128)(2,1)S(1)}, bf16[512,128]{1,0:T(8,128)(2,1)}, u32[]{:S(2)}) copy-start(bf16[512,128]{1,0:T(8,128)(2,1)} %param.10) | copy-start | bytes 393220
  21.3 10.7 %copy-start.4 = (bf16[512,128]{1,0:T(8,128)(2,1)S(1)}, bf16[512,128]{1,0:T(8,128)(2,1)}, u32[]{:S(2)}) copy-start(bf16[512,128]{1,0:T(8,128)(2,1)} %param.11) | copy-start | bytes 393220
  32.0 4.8 %copy-start.1 = (bf16[8192,128]{1,0:T(8,128)(2,1)S(1)}, bf16[8192,128]{1,0:T(8,128)(2,1)}, u32[]{:S(2)}) copy-start(bf16[8192,128]{1,0:T(8,128)(2,1)} %get-tuple-element.8) | copy-start | bytes 6291460
  38.8 1.7 %copy-start.5 = (s32[128]{0:T(128)S(1)}, s32[128]{0:T(128)}, u32[]{:S(2)}) copy-start(s32[128]{0:T(128)} %param.14) | copy-start | bytes 1540
  102.2 35.9 %all-to-all-start = ((bf16[16,4,64,128]{3,2,1,0:T(8,128)(2,1)}), bf16[16,4,64,128]{3,2,1,0:T(8,128)(2,1)S(1)}, u32[]{:S(2)}, u32[]{:S(2)}) async-start(bf16[16,4,64,128]{3,2,1,0:T(8,128)(2,1)} %broadcast_in_dim.67), calls=%async_computation.1 | async-start | bytes 2097152 | tf_op jit(solution)/shard_map/all_to_all | solution.py:97
  138.1 2.2 %copy-start.2 = (f32[8192,128]{1,0:T(8,128)S(1)}, f32[8192,128]{1,0:T(8,128)}, u32[]{:S(2)}) copy-start(f32[8192,128]{1,0:T(8,128)} %get-tuple-element.7) | copy-start | bytes 12582916
Sparse Core Ops, SparseCore 0:
  40.6 57.7 reduce-scatter.1

commit v6 on v5

--- a/solution.py
+++ b/solution.py
@@ -3,12 +3,14 @@
 from jax import lax
 from jax.experimental import pallas as pl
 from jax.experimental.pallas import tpu as pltpu
-from jax.sharding import PartitionSpec as P
+from jax.sharding import Mesh, PartitionSpec as P
 
 BLOCK = 64
 KB = 64
 STEPS = 4
 ROWS = 1024
+CORES = 2
+MEM = ("z", "core")
 
 def advect_kernel(halo_ref, s_ref, x_ref, f_ref, fb_ref, carry_ref):
     @pl.when(pl.program_id(0) == 0)
@@ -98,7 +100,14 @@
 
 
 def gathered_copies(value, axis, dim):
-    return laid_out(from_everyone(value, axis), dim)
+    chips, cores = lax.axis_size("z"), lax.axis_size("core")
+    along_z = lax.all_to_all(
+        jnp.broadcast_to(value, (chips, *value.shape)), "z", split_axis=0, concat_axis=0, tiled=True
+    )
+    both = lax.all_to_all(
+        jnp.broadcast_to(along_z, (cores, *along_z.shape)), "core", split_axis=0, concat_axis=0, tiled=True
+    )
+    return laid_out(jnp.swapaxes(both, 0, 1).reshape(chips * cores, *value.shape), dim)
 
 
 def taper_mask(positions, live_counts):
@@ -163,9 +172,9 @@
         [rimmed[:, :lend], jnp.stack([obs_pert, obs_incr]), rimmed[:, -lend:]], 1
     )
     member_dev = member_vectors.shape[1]
-    members = member_dev * lax.axis_size("mem")
+    members = member_dev * lax.axis_size(MEM)
     per_region = block_obs.shape[0]
-    parts = lax.axis_size("mem")
+    parts = lax.axis_size(MEM)
     pairs = per_region // 2
     share = pairs // parts
     slots = extended.shape[1]
@@ -181,7 +190,7 @@
     sum_obs = jnp.sum(obs_rows.astype(jnp.float32), 1).reshape(pairs, 1, 2 * KB)
     payload = jnp.concatenate([cross, sum_cells, sum_obs], 1)
     got = lax.psum_scatter(
-        payload.reshape(parts, share, BLOCK + 2, 2 * KB), "mem", scatter_dimension=0, tiled=True
+        payload.reshape(parts, share, BLOCK + 2, 2 * KB), MEM, scatter_dimension=0, tiled=True
     ).reshape(share, BLOCK + 2, 2 * KB)
     cross = got[:, :BLOCK, :]
     cells_sum = jnp.transpose(got[:, BLOCK, :].reshape(share, 2, BLOCK), (0, 2, 1))
@@ -189,7 +198,7 @@
         share, BLOCK, 2 * KB
     )
     obs_sum = got[:, BLOCK + 1, :][:, None, :]
-    first_block = lax.axis_index("mem") * share * 2
+    first_block = lax.axis_index(MEM) * share * 2
     live_counts = lax.dynamic_slice_in_dim(block_count, first_block, share * 2, 0)
     positions = lax.dynamic_slice_in_dim(obs_offset, first_block, share * 2, 0)
     position = jnp.arange(BLOCK).astype(jnp.float32)
@@ -201,7 +210,7 @@
     own_cov = (
         (cross - cells_sum * obs_sum / members) / (members - 1) * taper
     ).astype(jnp.bfloat16)
-    covariance = gathered_copies(own_cov, "mem", 0)
+    covariance = gathered_copies(own_cov, MEM, 0)
     same_block = (jnp.arange(2 * BLOCK) // BLOCK)[:, None] == (lane // KB)[None, :]
     spread = jnp.where(same_block[None], jnp.concatenate([covariance, covariance], 1), 0)
     incr_p = incr_rows.reshape(pairs, 2 * KB, member_dev)
@@ -213,19 +222,21 @@
 
 
 def solution(mesh):
+    mem, reg = mesh.devices.shape
+    split = Mesh(mesh.devices.reshape(mem // CORES, CORES, reg), ("z", "core", "reg"))
     return jax.shard_map(
         per_device,
-        mesh=mesh,
+        mesh=split,
         in_specs=(
-            P("reg", "mem"),
+            P("reg", MEM),
             P("reg"),
-            P("reg", "mem"),
-            P("reg", "mem"),
+            P("reg", MEM),
+            P("reg", MEM),
             P("reg", None, None),
             P("reg", None),
             P("reg"),
             P("reg", None),
         ),
-        out_specs=P("reg", "mem"),
+        out_specs=P("reg", MEM),
         check_vma=False,
     )

time: 150 us -> 145 us (0.967)
  waiting for transfers between devices: 78.7 us -> 68.7 us
  blocking collectives: 0 us -> 4.67 us
    all_to_all x1, waiting for transfers between devices: 22.2 us -> 12.2 us  [gathered_copies(): lax.all_to_all(jnp.broadcast_to(value, (chips, *value.shape)), 'z', split...]
    all_to_all x0 -> x1, blocking collectives: none -> 4.67 us  [gathered_copies(): lax.all_to_all(jnp.broadcast_to(along_z, (cores, *along_z.shape)), 'core'...]
  transfers between devices with their start and end apart: 5 -> 5, of which waited for: 2 -> 2; matrix products, arithmetic and copies ran while one was open for 10% -> 11% of each run, Pallas kernels for 6% -> 6%
where the time goes in v6:
time: 145 us; the launch traced here: 144 us
  waiting for transfers between devices  68.7 us (47%)
  matrix products  15 us (10%)
  starting transfers between devices  14.5 us (10%)
  between operations  13.6 us (9%)
  local copies, waits for them, and re-layouts  10.1 us (7%)
  other arithmetic  9.09 us (6%)
  Pallas kernels  8.42 us (6%)
  blocking collectives  4.67 us (3%)
    reduce_scatter x1, waiting for transfers between devices, per_device(): lax.psum_scatter(payload.reshape(parts, share, BLOCK + 2, 2 * KB), MEM, s...  56.5 us
    all_to_all x1, waiting for transfers between devices, gathered_copies(): lax.all_to_all(jnp.broadcast_to(value, (chips, *value.shape)), 'z', split...  12.2 us
    pallas_call x1, Pallas kernels, advect(): pl.pallas_call(advect_kernel, grid=(cells // rows,), in_specs=[pl.BlockSp...  8.42 us
    all_to_all x1, starting transfers between devices, gathered_copies(): lax.all_to_all(jnp.broadcast_to(value, (chips, *value.shape)), 'z', split...  7.47 us
    dot_general x1, matrix products, per_device(): jnp.dot(picks, extended[1], preferred_element_type=jnp.float32)  5.73 us
    dot_general x1, matrix products, per_device(): jnp.dot(picks, extended[0], preferred_element_type=jnp.float32)  4.75 us
    all_to_all x1, blocking collectives, gathered_copies(): lax.all_to_all(jnp.broadcast_to(along_z, (cores, *along_z.shape)), 'core'...  4.67 us
    ppermute x1, starting transfers between devices, padded(): lax.ppermute(lax.slice_in_dim(block, 0, width, axis=dim), axis, backward)  3.49 us
  transfers between devices with their start and end apart: 5, of which 2 were waited for; matrix products, arithmetic and copies ran while one was open for 11% of the time, Pallas kernels for 6%

profile of v6, /device:TPU:1, one launch (start us, length us, event | category | flops | bytes accessed | tf_op | source)
XLA Modules:
  0.0 144.1 jit_solution(9192769048231562762)
XLA Ops:
  6.5 0.8 slice_bitcast_fusion.4
  7.4 0.7 slice.81
  8.1 2.1 %collective-permute-start = (f32[4,129]{1,0:T(4,128)S(1)}, f32[4,129]{1,0:T(4,128)S(1)}, u32[]{:S(2)}, u32[]{:S(2)}) collective-permute-start(f32[4,129]{1,0:T(4,128)S(1)} %pad_maximum_fusion.3), channel_id=1, source_target_pairs={{15,0},{0,1},{1,2},{2,3},{3,4},{4,5},{5,6},{6,7},{7,8},{8,9},{9,10... | collective-permute-start | bytes 6200 | tf_op jit(solution)/shard_map/ppermute | solution.py:63
  10.2 0.8 eq.56
  11.0 1.1 fusion.11
  12.1 1.1 fusion.12
  13.3 1.4 collective-permute-start.1
  14.6 3.5 %collective-permute-start.2 = (bf16[2,64,128]{2,1,0:T(8,128)(2,1)S(1)}, bf16[2,64,128]{2,1,0:T(8,128)(2,1)S(1)}, u32[]{:S(2)}, u32[]{:S(2)}) collective-permute-start(bf16[2,64,128]{2,1,0:T(8,128)(2,1)S(1)} %get-tuple-element.12), channel_id=1, source_target_pairs={{1,0},{2,1},{3,2},{4,3},{5,4},{6,5},{7,6},{8,7},{9,8},{10,9},{11,1... | collective-permute-start | bytes 98312 | tf_op jit(solution)/shard_map/ppermute | solution.py:75
  18.1 0.8 copy.26
  19.5 0.5 slice.110
  20.0 0.7 multiply_subtract_fusion.1
  20.7 0.6 concatenate.23.halo_ref
  21.3 8.4 %shard_map.82 = (f32[8192,128]{1,0:T(8,128)}, bf16[8192,128]{1,0:T(8,128)(2,1)}) custom-call(f32[8,128]{1,0:T(8,128)} %concatenate.23.halo_ref, f32[64,128]{1,0:T(8,128)} %bitcast.51, f32[8192,128]{1,0:T(8,128)} %x_ref.1), custom_call_target="tpu_custom_call" | custom-call | tf_op jit(solution)/shard_map/pallas_call | solution.py:36
  29.7 2.2 %convert_reduce_fusion.1 = f32[8192]{0:T(1024)S(1)} fusion(bf16[8192,128]{1,0:T(8,128)(2,1)} %get-tuple-element.8), kind=kLoop, calls=%fused_computation.10 | loop fusion | flops 2088960 | bytes 2129920 | tf_op jit(solution)/shard_map/reduce_sum | solution.py:189
  32.0 4.7 %convert_reduce_fusion = (f32[8192]{0:T(1024)S(1)}, bf16[8192,128]{1,0:T(8,128)(2,1)S(1)}) fusion(bf16[2,640,128]{2,1,0:T(8,128)(2,1)S(1)} %pad_maximum_fusion.1, s32[8192]{0:T(1024)S(1)} %eq.52), kind=kOutput, calls=%fused_computation.9 | convolution fusion | flops 1350557696 | bytes 2326528 | tf_op jit(solution)/shard_map/dot_general | solution.py:182
  36.8 1.6 %fusion.26 = f32[64,128,128]{2,1,0:T(8,128)S(1)} fusion(bf16[64,128,128]{2,1,0:T(8,128)(2,1)S(1)} %bitcast.43, bf16[64,128,128]{2,1,0:T(8,128)(2,1)S(1)} %bitcast.44), kind=kOutput, calls=%fused_computation.68 | convolution fusion | flops 268435456 | bytes 8388608 | tf_op jit(solution)/shard_map/brm,blm->brl/dot_general | solution.py:186
  38.3 0.5 slice_select_fusion
  38.8 1.7 %pad_maximum_fusion = f32[16,4,66,128]{3,2,1,0:T(8,128)} fusion(f32[16,4,1,128]{3,2,1,0:T(1,128)S(1)} %bitcast.52, f32[16,4,1,128]{3,2,1,0:T(1,128)S(1)} %bitcast.46, f32[16,4,64,128]{3,2,1,0:T(8,128)S(1)} %bitcast.42), kind=kLoop, calls=%fused_computation.11 | loop fusion | flops 1081344 | bytes 4325376 | tf_op jit(solution)/shard_map/concatenate | solution.py:191
  40.8 0.6 gather_fusion
  41.9 56.5 %reduce-scatter.2.cloned.1.call-done = f32[1,4,66,128]{3,2,1,0:T(8,128)} async-done(((f32[16,4,66,128]{3,2,1,0:T(8,128)}), f32[1,4,66,128]{3,2,1,0:T(8,128)}) %reduce-scatter.2.cloned.1.call-update) | async-done | bytes 135184 | tf_op jit(solution)/shard_map/reduce_scatter | solution.py:192
  98.4 0.8 fusion.25
  99.4 0.3 broadcast_in_dim.67
  99.9 1.0 fusion.16
  101.0 0.9 broadcast_in_dim.70
  101.9 7.5 %all-to-all-start = ((bf16[8,4,64,128]{3,2,1,0:T(8,128)(2,1)}), bf16[8,4,64,128]{3,2,1,0:T(8,128)(2,1)S(1)}, u32[]{:S(2)}, u32[]{:S(2)}) async-start(bf16[8,4,64,128]{3,2,1,0:T(8,128)(2,1)} %broadcast_in_dim.70), calls=%async_computation.1 | async-start | bytes 1048576 | tf_op jit(solution)/shard_map/all_to_all | solution.py:104
  109.4 5.7 %fusion.5 = bf16[8192,128]{1,0:T(8,128)(2,1)S(1)} fusion(s32[8192]{0:T(1024)S(1)} %eq.52, bf16[2,640,128]{2,1,0:T(8,128)(2,1)S(1)} %pad_maximum_fusion.1), kind=kOutput, calls=%fused_computation.7 | convolution fusion | flops 1348468736 | bytes 2293760 | tf_op jit(solution)/shard_map/dot_general | solution.py:183
  115.2 12.2 %all-to-all-done = bf16[8,4,64,128]{3,2,1,0:T(8,128)(2,1)S(1)} async-done(((bf16[8,4,64,128]{3,2,1,0:T(8,128)(2,1)}), bf16[8,4,64,128]{3,2,1,0:T(8,128)(2,1)S(1)}, u32[]{:S(2)}, u32[]{:S(2)}) %all-to-all-start) | async-done | bytes 524320 | tf_op jit(solution)/shard_map/all_to_all | solution.py:104
  127.3 0.3 broadcast_in_dim.71
  127.6 4.7 %all_to_all.10 = bf16[2,8,4,64,128]{4,3,2,1,0:T(8,128)(2,1)S(1)} all-to-all(bf16[2,8,4,64,128]{4,3,2,1,0:T(8,128)(2,1)S(1)} %broadcast_in_dim.71), channel_id=1, replica_groups=mesh['z'=8,'core'=2,'reg'=16] {'core'}, dimensions={0} | all-to-all | bytes 2097152 | tf_op jit(solution)/shard_map/all_to_all | solution.py:107
  132.4 0.7 fusion.10
  133.1 1.5 %copy-done.2 = f32[8192,128]{1,0:T(8,128)S(1)} copy-done((f32[8192,128]{1,0:T(8,128)S(1)}, f32[8192,128]{1,0:T(8,128)}, u32[]{:S(2)}) %copy-start.2) | copy-done | bytes 4194328
  134.6 2.7 %convert_add_fusion = f32[8192,128]{1,0:T(8,128)} fusion(f32[8192,128]{1,0:T(8,128)S(1)} %copy-done.2, bf16[64,128,128]{2,1,0:T(8,128)(2,1)S(1)} %fusion.10), kind=kLoop, calls=%fused_computation.8 | loop fusion | flops 2097152 | bytes 10485760 | tf_op jit(solution)/shard_map/add | solution.py:221
  (47 shorter events, 1.9 us)
Async XLA Ops:
  6.5 35.1 %copy-start = (f32[128,64]{0,1:T(8,128)S(1)}, f32[128,64]{0,1:T(8,128)}, u32[]{:S(2)}) copy-start(f32[128,64]{0,1:T(8,128)} %param.15) | copy-start | bytes 98308
  6.5 91.9 %reduce-scatter.2.cloned.1.call-start = ((), (), s32[]{:S(2)}) async-start(), calls=%async_computation.3 | async-start | bytes 2506752 | tf_op jit(solution)/shard_map/reduce_scatter | solution.py:192
  8.1 11.0 %collective-permute-start = (f32[4,129]{1,0:T(4,128)S(1)}, f32[4,129]{1,0:T(4,128)S(1)}, u32[]{:S(2)}, u32[]{:S(2)}) collective-permute-start(f32[4,129]{1,0:T(4,128)S(1)} %pad_maximum_fusion.3), channel_id=1, source_target_pairs={{15,0},{0,1},{1,2},{2,3},{3,4},{4,5},{5,6},{6,7},{7,8},{8,9},{9,10... | collective-permute-start | bytes 6200 | tf_op jit(solution)/shard_map/ppermute | solution.py:63
  13.3 18.6 %collective-permute-start.1 = (bf16[2,64,128]{2,1,0:T(8,128)(2,1)S(1)}, bf16[2,64,128]{2,1,0:T(8,128)(2,1)S(1)}, u32[]{:S(2)}, u32[]{:S(2)}) collective-permute-start(bf16[2,64,128]{2,1,0:T(8,128)(2,1)S(1)} %get-tuple-element.11), channel_id=1, source_target_pairs={{0,1},{1,2},{2,3},{3,4},{4,5},{5,6},{6,7},{7,8},{8,9},{9,10},{10,1... | collective-permute-start | bytes 98312 | tf_op jit(solution)/shard_map/ppermute | solution.py:72
  14.6 17.3 %collective-permute-start.2 = (bf16[2,64,128]{2,1,0:T(8,128)(2,1)S(1)}, bf16[2,64,128]{2,1,0:T(8,128)(2,1)S(1)}, u32[]{:S(2)}, u32[]{:S(2)}) collective-permute-start(bf16[2,64,128]{2,1,0:T(8,128)(2,1)S(1)} %get-tuple-element.12), channel_id=1, source_target_pairs={{1,0},{2,1},{3,2},{4,3},{5,4},{6,5},{7,6},{8,7},{9,8},{10,9},{11,1... | collective-permute-start | bytes 98312 | tf_op jit(solution)/shard_map/ppermute | solution.py:75
  21.3 10.7 %copy-start.3 = (bf16[512,128]{1,0:T(8,128)(2,1)S(1)}, bf16[512,128]{1,0:T(8,128)(2,1)}, u32[]{:S(2)}) copy-start(bf16[512,128]{1,0:T(8,128)(2,1)} %param.10) | copy-start | bytes 393220
  21.3 10.7 %copy-start.4 = (bf16[512,128]{1,0:T(8,128)(2,1)S(1)}, bf16[512,128]{1,0:T(8,128)(2,1)}, u32[]{:S(2)}) copy-start(bf16[512,128]{1,0:T(8,128)(2,1)} %param.11) | copy-start | bytes 393220
  32.0 4.8 %copy-start.1 = (bf16[8192,128]{1,0:T(8,128)(2,1)S(1)}, bf16[8192,128]{1,0:T(8,128)(2,1)}, u32[]{:S(2)}) copy-start(bf16[8192,128]{1,0:T(8,128)(2,1)} %get-tuple-element.8) | copy-start | bytes 6291460
  38.8 1.7 %copy-start.5 = (s32[128]{0:T(128)S(1)}, s32[128]{0:T(128)}, u32[]{:S(2)}) copy-start(s32[128]{0:T(128)} %param.14) | copy-start | bytes 1540
  101.9 25.5 %all-to-all-start = ((bf16[8,4,64,128]{3,2,1,0:T(8,128)(2,1)}), bf16[8,4,64,128]{3,2,1,0:T(8,128)(2,1)S(1)}, u32[]{:S(2)}, u32[]{:S(2)}) async-start(bf16[8,4,64,128]{3,2,1,0:T(8,128)(2,1)} %broadcast_in_dim.70), calls=%async_computation.1 | async-start | bytes 1048576 | tf_op jit(solution)/shard_map/all_to_all | solution.py:104
  132.4 2.2 %copy-start.2 = (f32[8192,128]{1,0:T(8,128)S(1)}, f32[8192,128]{1,0:T(8,128)}, u32[]{:S(2)}) copy-start(f32[8192,128]{1,0:T(8,128)} %get-tuple-element.7) | copy-start | bytes 12582916
Sparse Core Ops, SparseCore 0:
  40.6 57.7 reduce-scatter.1

commit v7 on v6

--- a/solution.py
+++ b/solution.py
@@ -8,7 +8,7 @@
 BLOCK = 64
 KB = 64
 STEPS = 4
-ROWS = 1024
+ROWS = 2048
 CORES = 2
 MEM = ("z", "core")
 
@@ -187,7 +187,8 @@
     upper = (jnp.arange(2 * KB) >= KB)[None, None, :]
     cross = jnp.where(upper, full[:, BLOCK:, :], full[:, :BLOCK, :])
     sum_cells = jnp.sum(first_guess_state.astype(jnp.float32), 1).reshape(pairs, 1, 2 * BLOCK)
-    sum_obs = jnp.sum(obs_rows.astype(jnp.float32), 1).reshape(pairs, 1, 2 * KB)
+    table_sums = jnp.sum(extended[0].astype(jnp.float32), 1)
+    sum_obs = table_sums[block_obs].reshape(pairs, 1, 2 * KB)
     payload = jnp.concatenate([cross, sum_cells, sum_obs], 1)
     got = lax.psum_scatter(
         payload.reshape(parts, share, BLOCK + 2, 2 * KB), MEM, scatter_dimension=0, tiled=True

time: 145 us -> 178 us (1.23)
  local copies, waits for them, and re-layouts: 10.1 us -> 43.2 us
  matrix products: 15 us -> 16.8 us
    gather x0 -> x1, local copies, waits for them, and re-layouts: none -> 32.9 us  [per_device(): sum_obs = table_sums[block_obs].reshape(pairs, 1, 2 * KB)]
  transfers between devices with their start and end apart: 5 -> 5, of which waited for: 2 -> 2; matrix products, arithmetic and copies ran while one was open for 11% -> 10% of each run, Pallas kernels for 6% -> 4%
where the time goes in v7:
time: 178 us; the launch traced here: 177 us
  waiting for transfers between devices  67.9 us (38%)
  local copies, waits for them, and re-layouts  43.2 us (24%)
  matrix products  16.8 us (9%)
  starting transfers between devices  14.4 us (8%)
  between operations  13.7 us (8%)
  other arithmetic  9.91 us (6%)
  Pallas kernels  6.87 us (4%)
  blocking collectives  4.81 us (3%)
    reduce_scatter x1, waiting for transfers between devices, per_device(): lax.psum_scatter(payload.reshape(parts, share, BLOCK + 2, 2 * KB), MEM, s...  56.5 us
    gather x1, local copies, waits for them, and re-layouts, per_device(): sum_obs = table_sums[block_obs].reshape(pairs, 1, 2 * KB)  32.9 us
    all_to_all x1, waiting for transfers between devices, gathered_copies(): lax.all_to_all(jnp.broadcast_to(value, (chips, *value.shape)), 'z', split...  11.4 us
    all_to_all x1, starting transfers between devices, gathered_copies(): lax.all_to_all(jnp.broadcast_to(value, (chips, *value.shape)), 'z', split...  7.41 us
    pallas_call x1, Pallas kernels, advect(): pl.pallas_call(advect_kernel, grid=(cells // rows,), in_specs=[pl.BlockSp...  6.87 us
    dot_general x1, matrix products, per_device(): jnp.dot(picks, extended[1], preferred_element_type=jnp.float32)  6.49 us
    dot_general x1, matrix products, per_device(): jnp.dot(picks, extended[0], preferred_element_type=jnp.float32)  5.72 us
    all_to_all x1, blocking collectives, gathered_copies(): lax.all_to_all(jnp.broadcast_to(along_z, (cores, *along_z.shape)), 'core'...  4.81 us
  transfers between devices with their start and end apart: 5, of which 2 were waited for; matrix products, arithmetic and copies ran while one was open for 10% of the time, Pallas kernels for 4%

profile of v7, /device:TPU:1, one launch (start us, length us, event | category | flops | bytes accessed | tf_op | source)
XLA Modules:
  0.0 177.5 jit_solution(6171409121079483659)
XLA Ops:
  6.5 0.8 slice_bitcast_fusion.4
  7.4 0.7 slice.82
  8.1 2.1 %collective-permute-start = (f32[4,129]{1,0:T(4,128)S(1)}, f32[4,129]{1,0:T(4,128)S(1)}, u32[]{:S(2)}, u32[]{:S(2)}) collective-permute-start(f32[4,129]{1,0:T(4,128)S(1)} %pad_maximum_fusion.3), channel_id=1, source_target_pairs={{15,0},{0,1},{1,2},{2,3},{3,4},{4,5},{5,6},{6,7},{7,8},{8,9},{9,10... | collective-permute-start | bytes 6200 | tf_op jit(solution)/shard_map/ppermute | solution.py:63
  10.2 0.8 eq.56
  11.0 1.1 fusion.11
  12.1 1.1 fusion.12
  13.3 1.4 collective-permute-start.1
  14.6 3.5 %collective-permute-start.2 = (bf16[2,64,128]{2,1,0:T(8,128)(2,1)S(1)}, bf16[2,64,128]{2,1,0:T(8,128)(2,1)S(1)}, u32[]{:S(2)}, u32[]{:S(2)}) collective-permute-start(bf16[2,64,128]{2,1,0:T(8,128)(2,1)S(1)} %get-tuple-element.12), channel_id=1, source_target_pairs={{1,0},{2,1},{3,2},{4,3},{5,4},{6,5},{7,6},{8,7},{9,8},{10,9},{11,1... | collective-permute-start | bytes 98312 | tf_op jit(solution)/shard_map/ppermute | solution.py:75
  18.1 0.8 compare_select_fusion
  19.1 0.8 copy.28
  20.4 0.5 slice.113
  20.9 0.7 multiply_subtract_fusion.1
  21.6 0.6 concatenate.23.halo_ref
  22.2 6.9 %shard_map.82 = (f32[8192,128]{1,0:T(8,128)}, bf16[8192,128]{1,0:T(8,128)(2,1)}) custom-call(f32[8,128]{1,0:T(8,128)} %concatenate.23.halo_ref, f32[64,128]{1,0:T(8,128)} %bitcast.52, f32[8192,128]{1,0:T(8,128)} %x_ref.1), custom_call_target="tpu_custom_call" | custom-call | tf_op jit(solution)/shard_map/pallas_call | solution.py:36
  29.1 2.2 %convert_reduce_fusion = f32[8192]{0:T(1024)S(1)} fusion(bf16[8192,128]{1,0:T(8,128)(2,1)} %get-tuple-element.8), kind=kLoop, calls=%fused_computation.10 | loop fusion | flops 2088960 | bytes 2129920 | tf_op jit(solution)/shard_map/reduce_sum | solution.py:189
  31.5 5.7 %fusion.4 = bf16[8192,128]{1,0:T(8,128)(2,1)S(1)} fusion(s32[8192]{0:T(1024)S(1)} %eq.52, bf16[2,640,128]{2,1,0:T(8,128)(2,1)S(1)} %pad_maximum_fusion.1), kind=kOutput, calls=%fused_computation.7 | convolution fusion | flops 1348468736 | bytes 2293760 | tf_op jit(solution)/shard_map/dot_general | solution.py:182
  37.3 1.6 fusion.26
  38.9 0.4 slice_select_fusion
  39.3 32.9 %gather_fusion = f32[8192]{0:T(1024)S(1)} fusion(f32[640]{0:T(1024)S(1)} %convert_reduce_fusion.1, s32[8192]{0:T(1024)S(1)} %broadcast_clamp_fusion), kind=kCustom, calls=%fused_computation | custom fusion | bytes 98304 | tf_op jit(solution)/shard_map/gather | solution.py:191
  72.2 1.7 pad_maximum_fusion
  74.1 0.6 gather_fusion.1
  75.2 56.5 %reduce-scatter.2.cloned.1.call-done = f32[1,4,66,128]{3,2,1,0:T(8,128)} async-done(((f32[16,4,66,128]{3,2,1,0:T(8,128)}), f32[1,4,66,128]{3,2,1,0:T(8,128)}) %reduce-scatter.2.cloned.1.call-update) | async-done | bytes 135184 | tf_op jit(solution)/shard_map/reduce_scatter | solution.py:193
  131.7 0.8 fusion.25
  133.2 1.0 fusion.16
  134.3 0.9 broadcast_in_dim.74
  135.2 7.4 %all-to-all-start = ((bf16[8,4,64,128]{3,2,1,0:T(8,128)(2,1)}), bf16[8,4,64,128]{3,2,1,0:T(8,128)(2,1)S(1)}, u32[]{:S(2)}, u32[]{:S(2)}) async-start(bf16[8,4,64,128]{3,2,1,0:T(8,128)(2,1)} %broadcast_in_dim.74), calls=%async_computation.1 | async-start | bytes 1048576 | tf_op jit(solution)/shard_map/all_to_all | solution.py:104
  142.7 6.5 %fusion.5 = bf16[8192,128]{1,0:T(8,128)(2,1)} fusion(s32[8192]{0:T(1024)S(1)} %eq.52, bf16[2,640,128]{2,1,0:T(8,128)(2,1)S(1)} %pad_maximum_fusion.1), kind=kOutput, calls=%fused_computation.8 | convolution fusion | flops 1348468736 | bytes 2293760 | tf_op jit(solution)/shard_map/dot_general | solution.py:183
  149.2 11.4 %all-to-all-done = bf16[8,4,64,128]{3,2,1,0:T(8,128)(2,1)S(1)} async-done(((bf16[8,4,64,128]{3,2,1,0:T(8,128)(2,1)}), bf16[8,4,64,128]{3,2,1,0:T(8,128)(2,1)S(1)}, u32[]{:S(2)}, u32[]{:S(2)}) %all-to-all-start) | async-done | bytes 524320 | tf_op jit(solution)/shard_map/all_to_all | solution.py:104
  160.8 4.8 %all_to_all.10 = bf16[2,8,4,64,128]{4,3,2,1,0:T(8,128)(2,1)S(1)} all-to-all(bf16[2,8,4,64,128]{4,3,2,1,0:T(8,128)(2,1)S(1)} %broadcast_in_dim.75), channel_id=1, replica_groups=mesh['z'=8,'core'=2,'reg'=16] {'core'}, dimensions={0} | all-to-all | bytes 2097152 | tf_op jit(solution)/shard_map/all_to_all | solution.py:107
  165.8 0.7 fusion.10
  166.5 1.5 copy-done.2
  167.9 2.7 %convert_add_fusion = f32[8192,128]{1,0:T(8,128)} fusion(f32[8192,128]{1,0:T(8,128)S(1)} %copy-done.2, bf16[64,128,128]{2,1,0:T(8,128)(2,1)S(1)} %fusion.10), kind=kLoop, calls=%fused_computation.9 | loop fusion | flops 2097152 | bytes 10485760 | tf_op jit(solution)/shard_map/add | solution.py:222
  (55 shorter events, 2.8 us)
Async XLA Ops:
  6.5 68.4 %copy-start = (f32[128,64]{0,1:T(8,128)S(1)}, f32[128,64]{0,1:T(8,128)}, u32[]{:S(2)}) copy-start(f32[128,64]{0,1:T(8,128)} %param.15) | copy-start | bytes 98308
  6.5 125.2 %reduce-scatter.2.cloned.1.call-start = ((), (), s32[]{:S(2)}) async-start(), calls=%async_computation.3 | async-start | bytes 2506752 | tf_op jit(solution)/shard_map/reduce_scatter | solution.py:193
  8.1 11.9 %collective-permute-start = (f32[4,129]{1,0:T(4,128)S(1)}, f32[4,129]{1,0:T(4,128)S(1)}, u32[]{:S(2)}, u32[]{:S(2)}) collective-permute-start(f32[4,129]{1,0:T(4,128)S(1)} %pad_maximum_fusion.3), channel_id=1, source_target_pairs={{15,0},{0,1},{1,2},{2,3},{3,4},{4,5},{5,6},{6,7},{7,8},{8,9},{9,10... | collective-permute-start | bytes 6200 | tf_op jit(solution)/shard_map/ppermute | solution.py:63
  13.3 18.1 %collective-permute-start.1 = (bf16[2,64,128]{2,1,0:T(8,128)(2,1)S(1)}, bf16[2,64,128]{2,1,0:T(8,128)(2,1)S(1)}, u32[]{:S(2)}, u32[]{:S(2)}) collective-permute-start(bf16[2,64,128]{2,1,0:T(8,128)(2,1)S(1)} %get-tuple-element.11), channel_id=1, source_target_pairs={{0,1},{1,2},{2,3},{3,4},{4,5},{5,6},{6,7},{7,8},{8,9},{9,10},{10,1... | collective-permute-start | bytes 98312 | tf_op jit(solution)/shard_map/ppermute | solution.py:72
  14.6 16.7 %collective-permute-start.2 = (bf16[2,64,128]{2,1,0:T(8,128)(2,1)S(1)}, bf16[2,64,128]{2,1,0:T(8,128)(2,1)S(1)}, u32[]{:S(2)}, u32[]{:S(2)}) collective-permute-start(bf16[2,64,128]{2,1,0:T(8,128)(2,1)S(1)} %get-tuple-element.12), channel_id=1, source_target_pairs={{1,0},{2,1},{3,2},{4,3},{5,4},{6,5},{7,6},{8,7},{9,8},{10,9},{11,1... | collective-permute-start | bytes 98312 | tf_op jit(solution)/shard_map/ppermute | solution.py:75
  22.2 9.1 %copy-start.3 = (bf16[512,128]{1,0:T(8,128)(2,1)S(1)}, bf16[512,128]{1,0:T(8,128)(2,1)}, u32[]{:S(2)}) copy-start(bf16[512,128]{1,0:T(8,128)(2,1)} %param.10) | copy-start | bytes 393220
  22.2 9.1 %copy-start.4 = (bf16[512,128]{1,0:T(8,128)(2,1)S(1)}, bf16[512,128]{1,0:T(8,128)(2,1)}, u32[]{:S(2)}) copy-start(bf16[512,128]{1,0:T(8,128)(2,1)} %param.11) | copy-start | bytes 393220
  31.5 5.7 %copy-start.1 = (bf16[8192,128]{1,0:T(8,128)(2,1)S(1)}, bf16[8192,128]{1,0:T(8,128)(2,1)}, u32[]{:S(2)}) copy-start(bf16[8192,128]{1,0:T(8,128)(2,1)} %get-tuple-element.8) | copy-start | bytes 6291460
  72.1 1.7 copy-start.5
  135.2 25.4 %all-to-all-start = ((bf16[8,4,64,128]{3,2,1,0:T(8,128)(2,1)}), bf16[8,4,64,128]{3,2,1,0:T(8,128)(2,1)S(1)}, u32[]{:S(2)}, u32[]{:S(2)}) async-start(bf16[8,4,64,128]{3,2,1,0:T(8,128)(2,1)} %broadcast_in_dim.74), calls=%async_computation.1 | async-start | bytes 1048576 | tf_op jit(solution)/shard_map/all_to_all | solution.py:104
  160.8 4.9 %copy-start.6 = (bf16[8192,128]{1,0:T(8,128)(2,1)S(1)}, bf16[8192,128]{1,0:T(8,128)(2,1)}, u32[]{:S(2)}) copy-start(bf16[8192,128]{1,0:T(8,128)(2,1)} %fusion.5) | copy-start | bytes 6291460
  165.7 2.2 %copy-start.2 = (f32[8192,128]{1,0:T(8,128)S(1)}, f32[8192,128]{1,0:T(8,128)}, u32[]{:S(2)}) copy-start(f32[8192,128]{1,0:T(8,128)} %get-tuple-element.7) | copy-start | bytes 12582916
Sparse Core Ops, SparseCore 0:
  74.0 57.6 reduce-scatter.1

commit v8 on v6

--- a/solution.py
+++ b/solution.py
@@ -8,7 +8,7 @@
 BLOCK = 64
 KB = 64
 STEPS = 4
-ROWS = 1024
+ROWS = 2048
 CORES = 2
 MEM = ("z", "core")
 

time: 145 us -> 143 us (0.986)
  Pallas kernels: 8.42 us -> 6.87 us
    pallas_call x1, Pallas kernels: 8.42 us -> 6.87 us  [advect(): pl.pallas_call(advect_kernel, grid=(cells // rows,), in_specs=[pl.BlockSp...]
  transfers between devices with their start and end apart: 5 -> 5, of which waited for: 2 -> 2; matrix products, arithmetic and copies ran while one was open for 11% -> 11% of each run, Pallas kernels for 6% -> 5%
where the time goes in v8:
time: 143 us; the launch traced here: 142 us
  waiting for transfers between devices  68.7 us (48%)
  matrix products  15 us (10%)
  starting transfers between devices  14.4 us (10%)
  between operations  13.6 us (10%)
  local copies, waits for them, and re-layouts  10.1 us (7%)
  other arithmetic  9.09 us (6%)
  Pallas kernels  6.87 us (5%)
  blocking collectives  4.67 us (3%)
    reduce_scatter x1, waiting for transfers between devices, per_device(): lax.psum_scatter(payload.reshape(parts, share, BLOCK + 2, 2 * KB), MEM, s...  56.5 us
    all_to_all x1, waiting for transfers between devices, gathered_copies(): lax.all_to_all(jnp.broadcast_to(value, (chips, *value.shape)), 'z', split...  12.1 us
    all_to_all x1, starting transfers between devices, gathered_copies(): lax.all_to_all(jnp.broadcast_to(value, (chips, *value.shape)), 'z', split...  7.42 us
    pallas_call x1, Pallas kernels, advect(): pl.pallas_call(advect_kernel, grid=(cells // rows,), in_specs=[pl.BlockSp...  6.87 us
    dot_general x1, matrix products, per_device(): jnp.dot(picks, extended[1], preferred_element_type=jnp.float32)  5.73 us
    dot_general x1, matrix products, per_device(): jnp.dot(picks, extended[0], preferred_element_type=jnp.float32)  4.75 us
    all_to_all x1, blocking collectives, gathered_copies(): lax.all_to_all(jnp.broadcast_to(along_z, (cores, *along_z.shape)), 'core'...  4.67 us
    ppermute x1, starting transfers between devices, padded(): lax.ppermute(lax.slice_in_dim(block, 0, width, axis=dim), axis, backward)  3.49 us
  transfers between devices with their start and end apart: 5, of which 2 were waited for; matrix products, arithmetic and copies ran while one was open for 11% of the time, Pallas kernels for 5%

profile of v8, /device:TPU:1, one launch (start us, length us, event | category | flops | bytes accessed | tf_op | source)
XLA Modules:
  0.0 142.4 jit_solution(6151303359505450217)
XLA Ops:
  6.5 0.8 slice_bitcast_fusion.4
  7.4 0.7 slice.81
  8.1 2.1 %collective-permute-start = (f32[4,129]{1,0:T(4,128)S(1)}, f32[4,129]{1,0:T(4,128)S(1)}, u32[]{:S(2)}, u32[]{:S(2)}) collective-permute-start(f32[4,129]{1,0:T(4,128)S(1)} %pad_maximum_fusion.3), channel_id=1, source_target_pairs={{15,0},{0,1},{1,2},{2,3},{3,4},{4,5},{5,6},{6,7},{7,8},{8,9},{9,10... | collective-permute-start | bytes 6200 | tf_op jit(solution)/shard_map/ppermute | solution.py:63
  10.2 0.8 eq.56
  11.0 1.1 fusion.11
  12.1 1.1 fusion.12
  13.3 1.4 collective-permute-start.1
  14.6 3.5 %collective-permute-start.2 = (bf16[2,64,128]{2,1,0:T(8,128)(2,1)S(1)}, bf16[2,64,128]{2,1,0:T(8,128)(2,1)S(1)}, u32[]{:S(2)}, u32[]{:S(2)}) collective-permute-start(bf16[2,64,128]{2,1,0:T(8,128)(2,1)S(1)} %get-tuple-element.12), channel_id=1, source_target_pairs={{1,0},{2,1},{3,2},{4,3},{5,4},{6,5},{7,6},{8,7},{9,8},{10,9},{11,1... | collective-permute-start | bytes 98312 | tf_op jit(solution)/shard_map/ppermute | solution.py:75
  18.1 0.8 copy.26
  19.5 0.5 slice.110
  20.0 0.7 multiply_subtract_fusion.1
  20.7 0.6 concatenate.23.halo_ref
  21.3 6.9 %shard_map.82 = (f32[8192,128]{1,0:T(8,128)}, bf16[8192,128]{1,0:T(8,128)(2,1)}) custom-call(f32[8,128]{1,0:T(8,128)} %concatenate.23.halo_ref, f32[64,128]{1,0:T(8,128)} %bitcast.51, f32[8192,128]{1,0:T(8,128)} %x_ref.1), custom_call_target="tpu_custom_call" | custom-call | tf_op jit(solution)/shard_map/pallas_call | solution.py:36
  28.1 2.2 %convert_reduce_fusion.1 = f32[8192]{0:T(1024)S(1)} fusion(bf16[8192,128]{1,0:T(8,128)(2,1)} %get-tuple-element.8), kind=kLoop, calls=%fused_computation.10 | loop fusion | flops 2088960 | bytes 2129920 | tf_op jit(solution)/shard_map/reduce_sum | solution.py:189
  30.4 4.8 %convert_reduce_fusion = (f32[8192]{0:T(1024)S(1)}, bf16[8192,128]{1,0:T(8,128)(2,1)S(1)}) fusion(bf16[2,640,128]{2,1,0:T(8,128)(2,1)S(1)} %pad_maximum_fusion.1, s32[8192]{0:T(1024)S(1)} %eq.52), kind=kOutput, calls=%fused_computation.9 | convolution fusion | flops 1350557696 | bytes 2326528 | tf_op jit(solution)/shard_map/dot_general | solution.py:182
  35.2 1.6 %fusion.26 = f32[64,128,128]{2,1,0:T(8,128)S(1)} fusion(bf16[64,128,128]{2,1,0:T(8,128)(2,1)S(1)} %bitcast.43, bf16[64,128,128]{2,1,0:T(8,128)(2,1)S(1)} %bitcast.44), kind=kOutput, calls=%fused_computation.68 | convolution fusion | flops 268435456 | bytes 8388608 | tf_op jit(solution)/shard_map/brm,blm->brl/dot_general | solution.py:186
  36.8 0.5 slice_select_fusion
  37.3 1.7 %pad_maximum_fusion = f32[16,4,66,128]{3,2,1,0:T(8,128)} fusion(f32[16,4,1,128]{3,2,1,0:T(1,128)S(1)} %bitcast.52, f32[16,4,1,128]{3,2,1,0:T(1,128)S(1)} %bitcast.46, f32[16,4,64,128]{3,2,1,0:T(8,128)S(1)} %bitcast.42), kind=kLoop, calls=%fused_computation.11 | loop fusion | flops 1081344 | bytes 4325376 | tf_op jit(solution)/shard_map/concatenate | solution.py:191
  39.3 0.6 gather_fusion
  40.3 56.5 %reduce-scatter.2.cloned.1.call-done = f32[1,4,66,128]{3,2,1,0:T(8,128)} async-done(((f32[16,4,66,128]{3,2,1,0:T(8,128)}), f32[1,4,66,128]{3,2,1,0:T(8,128)}) %reduce-scatter.2.cloned.1.call-update) | async-done | bytes 135184 | tf_op jit(solution)/shard_map/reduce_scatter | solution.py:192
  96.8 0.8 fusion.25
  97.8 0.3 broadcast_in_dim.67
  98.4 1.0 fusion.16
  99.4 0.9 broadcast_in_dim.70
  100.3 7.4 %all-to-all-start = ((bf16[8,4,64,128]{3,2,1,0:T(8,128)(2,1)}), bf16[8,4,64,128]{3,2,1,0:T(8,128)(2,1)S(1)}, u32[]{:S(2)}, u32[]{:S(2)}) async-start(bf16[8,4,64,128]{3,2,1,0:T(8,128)(2,1)} %broadcast_in_dim.70), calls=%async_computation.1 | async-start | bytes 1048576 | tf_op jit(solution)/shard_map/all_to_all | solution.py:104
  107.8 5.7 %fusion.5 = bf16[8192,128]{1,0:T(8,128)(2,1)S(1)} fusion(s32[8192]{0:T(1024)S(1)} %eq.52, bf16[2,640,128]{2,1,0:T(8,128)(2,1)S(1)} %pad_maximum_fusion.1), kind=kOutput, calls=%fused_computation.7 | convolution fusion | flops 1348468736 | bytes 2293760 | tf_op jit(solution)/shard_map/dot_general | solution.py:183
  113.5 12.1 %all-to-all-done = bf16[8,4,64,128]{3,2,1,0:T(8,128)(2,1)S(1)} async-done(((bf16[8,4,64,128]{3,2,1,0:T(8,128)(2,1)}), bf16[8,4,64,128]{3,2,1,0:T(8,128)(2,1)S(1)}, u32[]{:S(2)}, u32[]{:S(2)}) %all-to-all-start) | async-done | bytes 524320 | tf_op jit(solution)/shard_map/all_to_all | solution.py:104
  125.7 0.3 broadcast_in_dim.71
  125.9 4.7 %all_to_all.10 = bf16[2,8,4,64,128]{4,3,2,1,0:T(8,128)(2,1)S(1)} all-to-all(bf16[2,8,4,64,128]{4,3,2,1,0:T(8,128)(2,1)S(1)} %broadcast_in_dim.71), channel_id=1, replica_groups=mesh['z'=8,'core'=2,'reg'=16] {'core'}, dimensions={0} | all-to-all | bytes 2097152 | tf_op jit(solution)/shard_map/all_to_all | solution.py:107
  130.7 0.7 fusion.10
  131.4 1.5 %copy-done.2 = f32[8192,128]{1,0:T(8,128)S(1)} copy-done((f32[8192,128]{1,0:T(8,128)S(1)}, f32[8192,128]{1,0:T(8,128)}, u32[]{:S(2)}) %copy-start.2) | copy-done | bytes 4194328
  132.9 2.7 %convert_add_fusion = f32[8192,128]{1,0:T(8,128)} fusion(f32[8192,128]{1,0:T(8,128)S(1)} %copy-done.2, bf16[64,128,128]{2,1,0:T(8,128)(2,1)S(1)} %fusion.10), kind=kLoop, calls=%fused_computation.8 | loop fusion | flops 2097152 | bytes 10485760 | tf_op jit(solution)/shard_map/add | solution.py:221
  (47 shorter events, 1.9 us)
Async XLA Ops:
  6.5 33.5 %copy-start = (f32[128,64]{0,1:T(8,128)S(1)}, f32[128,64]{0,1:T(8,128)}, u32[]{:S(2)}) copy-start(f32[128,64]{0,1:T(8,128)} %param.15) | copy-start | bytes 98308
  6.5 90.3 %reduce-scatter.2.cloned.1.call-start = ((), (), s32[]{:S(2)}) async-start(), calls=%async_computation.3 | async-start | bytes 2506752 | tf_op jit(solution)/shard_map/reduce_scatter | solution.py:192
  8.1 11.0 %collective-permute-start = (f32[4,129]{1,0:T(4,128)S(1)}, f32[4,129]{1,0:T(4,128)S(1)}, u32[]{:S(2)}, u32[]{:S(2)}) collective-permute-start(f32[4,129]{1,0:T(4,128)S(1)} %pad_maximum_fusion.3), channel_id=1, source_target_pairs={{15,0},{0,1},{1,2},{2,3},{3,4},{4,5},{5,6},{6,7},{7,8},{8,9},{9,10... | collective-permute-start | bytes 6200 | tf_op jit(solution)/shard_map/ppermute | solution.py:63
  13.3 17.1 %collective-permute-start.1 = (bf16[2,64,128]{2,1,0:T(8,128)(2,1)S(1)}, bf16[2,64,128]{2,1,0:T(8,128)(2,1)S(1)}, u32[]{:S(2)}, u32[]{:S(2)}) collective-permute-start(bf16[2,64,128]{2,1,0:T(8,128)(2,1)S(1)} %get-tuple-element.11), channel_id=1, source_target_pairs={{0,1},{1,2},{2,3},{3,4},{4,5},{5,6},{6,7},{7,8},{8,9},{9,10},{10,1... | collective-permute-start | bytes 98312 | tf_op jit(solution)/shard_map/ppermute | solution.py:72
  14.6 15.7 %collective-permute-start.2 = (bf16[2,64,128]{2,1,0:T(8,128)(2,1)S(1)}, bf16[2,64,128]{2,1,0:T(8,128)(2,1)S(1)}, u32[]{:S(2)}, u32[]{:S(2)}) collective-permute-start(bf16[2,64,128]{2,1,0:T(8,128)(2,1)S(1)} %get-tuple-element.12), channel_id=1, source_target_pairs={{1,0},{2,1},{3,2},{4,3},{5,4},{6,5},{7,6},{8,7},{9,8},{10,9},{11,1... | collective-permute-start | bytes 98312 | tf_op jit(solution)/shard_map/ppermute | solution.py:75
  21.3 9.1 %copy-start.3 = (bf16[512,128]{1,0:T(8,128)(2,1)S(1)}, bf16[512,128]{1,0:T(8,128)(2,1)}, u32[]{:S(2)}) copy-start(bf16[512,128]{1,0:T(8,128)(2,1)} %param.10) | copy-start | bytes 393220
  21.3 9.1 %copy-start.4 = (bf16[512,128]{1,0:T(8,128)(2,1)S(1)}, bf16[512,128]{1,0:T(8,128)(2,1)}, u32[]{:S(2)}) copy-start(bf16[512,128]{1,0:T(8,128)(2,1)} %param.11) | copy-start | bytes 393220
  30.4 4.8 %copy-start.1 = (bf16[8192,128]{1,0:T(8,128)(2,1)S(1)}, bf16[8192,128]{1,0:T(8,128)(2,1)}, u32[]{:S(2)}) copy-start(bf16[8192,128]{1,0:T(8,128)(2,1)} %get-tuple-element.8) | copy-start | bytes 6291460
  37.2 1.7 %copy-start.5 = (s32[128]{0:T(128)S(1)}, s32[128]{0:T(128)}, u32[]{:S(2)}) copy-start(s32[128]{0:T(128)} %param.14) | copy-start | bytes 1540
  100.3 25.4 %all-to-all-start = ((bf16[8,4,64,128]{3,2,1,0:T(8,128)(2,1)}), bf16[8,4,64,128]{3,2,1,0:T(8,128)(2,1)S(1)}, u32[]{:S(2)}, u32[]{:S(2)}) async-start(bf16[8,4,64,128]{3,2,1,0:T(8,128)(2,1)} %broadcast_in_dim.70), calls=%async_computation.1 | async-start | bytes 1048576 | tf_op jit(solution)/shard_map/all_to_all | solution.py:104
  130.7 2.2 %copy-start.2 = (f32[8192,128]{1,0:T(8,128)S(1)}, f32[8192,128]{1,0:T(8,128)}, u32[]{:S(2)}) copy-start(f32[8192,128]{1,0:T(8,128)} %get-tuple-element.7) | copy-start | bytes 12582916
Sparse Core Ops, SparseCore 0:
  39.1 57.6 reduce-scatter.1

commit v9 on v8

--- a/solution.py
+++ b/solution.py
@@ -8,7 +8,7 @@
 BLOCK = 64
 KB = 64
 STEPS = 4
-ROWS = 2048
+ROWS = 4096
 CORES = 2
 MEM = ("z", "core")
 

time: 143 us -> 143 us (level)
  no operation moved by 1% of the time
where the time goes in v9:
time: 143 us; the launch traced here: 142 us
  waiting for transfers between devices  68.7 us (48%)
  matrix products  15 us (10%)
  starting transfers between devices  14.4 us (10%)
  between operations  13.6 us (10%)
  local copies, waits for them, and re-layouts  10.1 us (7%)
  other arithmetic  9.09 us (6%)
  Pallas kernels  6.4 us (4%)
  blocking collectives  4.67 us (3%)
    reduce_scatter x1, waiting for transfers between devices, per_device(): lax.psum_scatter(payload.reshape(parts, share, BLOCK + 2, 2 * KB), MEM, s...  56.5 us
    all_to_all x1, waiting for transfers between devices, gathered_copies(): lax.all_to_all(jnp.broadcast_to(value, (chips, *value.shape)), 'z', split...  12.1 us
    all_to_all x1, starting transfers between devices, gathered_copies(): lax.all_to_all(jnp.broadcast_to(value, (chips, *value.shape)), 'z', split...  7.41 us
    pallas_call x1, Pallas kernels, advect(): pl.pallas_call(advect_kernel, grid=(cells // rows,), in_specs=[pl.BlockSp...  6.4 us
    dot_general x1, matrix products, per_device(): jnp.dot(picks, extended[1], preferred_element_type=jnp.float32)  5.73 us
    dot_general x1, matrix products, per_device(): jnp.dot(picks, extended[0], preferred_element_type=jnp.float32)  4.75 us
    all_to_all x1, blocking collectives, gathered_copies(): lax.all_to_all(jnp.broadcast_to(along_z, (cores, *along_z.shape)), 'core'...  4.67 us
    ppermute x1, starting transfers between devices, padded(): lax.ppermute(lax.slice_in_dim(block, 0, width, axis=dim), axis, backward)  3.49 us
  transfers between devices with their start and end apart: 5, of which 2 were waited for; matrix products, arithmetic and copies ran while one was open for 11% of the time, Pallas kernels for 5%

profile of v9, /device:TPU:1, one launch (start us, length us, event | category | flops | bytes accessed | tf_op | source)
XLA Modules:
  0.0 142.0 jit_solution(2558058512576024075)
XLA Ops:
  6.5 0.8 slice_bitcast_fusion.4
  7.4 0.7 slice.81
  8.1 2.1 %collective-permute-start = (f32[4,129]{1,0:T(4,128)S(1)}, f32[4,129]{1,0:T(4,128)S(1)}, u32[]{:S(2)}, u32[]{:S(2)}) collective-permute-start(f32[4,129]{1,0:T(4,128)S(1)} %pad_maximum_fusion.3), channel_id=1, source_target_pairs={{15,0},{0,1},{1,2},{2,3},{3,4},{4,5},{5,6},{6,7},{7,8},{8,9},{9,10... | collective-permute-start | bytes 6200 | tf_op jit(solution)/shard_map/ppermute | solution.py:63
  10.2 0.8 eq.56
  11.0 1.1 fusion.11
  12.1 1.1 fusion.12
  13.3 1.4 collective-permute-start.1
  14.6 3.5 %collective-permute-start.2 = (bf16[2,64,128]{2,1,0:T(8,128)(2,1)S(1)}, bf16[2,64,128]{2,1,0:T(8,128)(2,1)S(1)}, u32[]{:S(2)}, u32[]{:S(2)}) collective-permute-start(bf16[2,64,128]{2,1,0:T(8,128)(2,1)S(1)} %get-tuple-element.12), channel_id=1, source_target_pairs={{1,0},{2,1},{3,2},{4,3},{5,4},{6,5},{7,6},{8,7},{9,8},{10,9},{11,1... | collective-permute-start | bytes 98312 | tf_op jit(solution)/shard_map/ppermute | solution.py:75
  18.1 0.8 copy.26
  19.5 0.5 slice.110
  20.0 0.7 multiply_subtract_fusion.1
  20.7 0.6 concatenate.23.halo_ref
  21.3 6.4 %shard_map.82 = (f32[8192,128]{1,0:T(8,128)}, bf16[8192,128]{1,0:T(8,128)(2,1)}) custom-call(f32[8,128]{1,0:T(8,128)} %concatenate.23.halo_ref, f32[64,128]{1,0:T(8,128)} %bitcast.51, f32[8192,128]{1,0:T(8,128)} %x_ref.1), custom_call_target="tpu_custom_call" | custom-call | tf_op jit(solution)/shard_map/pallas_call | solution.py:36
  27.7 2.2 %convert_reduce_fusion.1 = f32[8192]{0:T(1024)S(1)} fusion(bf16[8192,128]{1,0:T(8,128)(2,1)} %get-tuple-element.8), kind=kLoop, calls=%fused_computation.10 | loop fusion | flops 2088960 | bytes 2129920 | tf_op jit(solution)/shard_map/reduce_sum | solution.py:189
  30.0 4.8 %convert_reduce_fusion = (f32[8192]{0:T(1024)S(1)}, bf16[8192,128]{1,0:T(8,128)(2,1)S(1)}) fusion(bf16[2,640,128]{2,1,0:T(8,128)(2,1)S(1)} %pad_maximum_fusion.1, s32[8192]{0:T(1024)S(1)} %eq.52), kind=kOutput, calls=%fused_computation.9 | convolution fusion | flops 1350557696 | bytes 2326528 | tf_op jit(solution)/shard_map/dot_general | solution.py:182
  34.7 1.6 %fusion.26 = f32[64,128,128]{2,1,0:T(8,128)S(1)} fusion(bf16[64,128,128]{2,1,0:T(8,128)(2,1)S(1)} %bitcast.43, bf16[64,128,128]{2,1,0:T(8,128)(2,1)S(1)} %bitcast.44), kind=kOutput, calls=%fused_computation.68 | convolution fusion | flops 268435456 | bytes 8388608 | tf_op jit(solution)/shard_map/brm,blm->brl/dot_general | solution.py:186
  36.3 0.5 slice_select_fusion
  36.8 1.7 %pad_maximum_fusion = f32[16,4,66,128]{3,2,1,0:T(8,128)} fusion(f32[16,4,1,128]{3,2,1,0:T(1,128)S(1)} %bitcast.52, f32[16,4,1,128]{3,2,1,0:T(1,128)S(1)} %bitcast.46, f32[16,4,64,128]{3,2,1,0:T(8,128)S(1)} %bitcast.42), kind=kLoop, calls=%fused_computation.11 | loop fusion | flops 1081344 | bytes 4325376 | tf_op jit(solution)/shard_map/concatenate | solution.py:191
  38.8 0.6 gather_fusion
  39.9 56.5 %reduce-scatter.2.cloned.1.call-done = f32[1,4,66,128]{3,2,1,0:T(8,128)} async-done(((f32[16,4,66,128]{3,2,1,0:T(8,128)}), f32[1,4,66,128]{3,2,1,0:T(8,128)}) %reduce-scatter.2.cloned.1.call-update) | async-done | bytes 135184 | tf_op jit(solution)/shard_map/reduce_scatter | solution.py:192
  96.4 0.8 fusion.25
  97.4 0.3 broadcast_in_dim.67
  97.9 1.0 fusion.16
  98.9 0.9 broadcast_in_dim.70
  99.8 7.4 %all-to-all-start = ((bf16[8,4,64,128]{3,2,1,0:T(8,128)(2,1)}), bf16[8,4,64,128]{3,2,1,0:T(8,128)(2,1)S(1)}, u32[]{:S(2)}, u32[]{:S(2)}) async-start(bf16[8,4,64,128]{3,2,1,0:T(8,128)(2,1)} %broadcast_in_dim.70), calls=%async_computation.1 | async-start | bytes 1048576 | tf_op jit(solution)/shard_map/all_to_all | solution.py:104
  107.3 5.7 %fusion.5 = bf16[8192,128]{1,0:T(8,128)(2,1)S(1)} fusion(s32[8192]{0:T(1024)S(1)} %eq.52, bf16[2,640,128]{2,1,0:T(8,128)(2,1)S(1)} %pad_maximum_fusion.1), kind=kOutput, calls=%fused_computation.7 | convolution fusion | flops 1348468736 | bytes 2293760 | tf_op jit(solution)/shard_map/dot_general | solution.py:183
  113.1 12.1 %all-to-all-done = bf16[8,4,64,128]{3,2,1,0:T(8,128)(2,1)S(1)} async-done(((bf16[8,4,64,128]{3,2,1,0:T(8,128)(2,1)}), bf16[8,4,64,128]{3,2,1,0:T(8,128)(2,1)S(1)}, u32[]{:S(2)}, u32[]{:S(2)}) %all-to-all-start) | async-done | bytes 524320 | tf_op jit(solution)/shard_map/all_to_all | solution.py:104
  125.2 0.3 broadcast_in_dim.71
  125.5 4.7 %all_to_all.10 = bf16[2,8,4,64,128]{4,3,2,1,0:T(8,128)(2,1)S(1)} all-to-all(bf16[2,8,4,64,128]{4,3,2,1,0:T(8,128)(2,1)S(1)} %broadcast_in_dim.71), channel_id=1, replica_groups=mesh['z'=8,'core'=2,'reg'=16] {'core'}, dimensions={0} | all-to-all | bytes 2097152 | tf_op jit(solution)/shard_map/all_to_all | solution.py:107
  130.3 0.7 fusion.10
  131.0 1.5 %copy-done.2 = f32[8192,128]{1,0:T(8,128)S(1)} copy-done((f32[8192,128]{1,0:T(8,128)S(1)}, f32[8192,128]{1,0:T(8,128)}, u32[]{:S(2)}) %copy-start.2) | copy-done | bytes 4194328
  132.4 2.7 %convert_add_fusion = f32[8192,128]{1,0:T(8,128)} fusion(f32[8192,128]{1,0:T(8,128)S(1)} %copy-done.2, bf16[64,128,128]{2,1,0:T(8,128)(2,1)S(1)} %fusion.10), kind=kLoop, calls=%fused_computation.8 | loop fusion | flops 2097152 | bytes 10485760 | tf_op jit(solution)/shard_map/add | solution.py:221
  (47 shorter events, 1.9 us)
Async XLA Ops:
  6.5 33.1 %copy-start = (f32[128,64]{0,1:T(8,128)S(1)}, f32[128,64]{0,1:T(8,128)}, u32[]{:S(2)}) copy-start(f32[128,64]{0,1:T(8,128)} %param.15) | copy-start | bytes 98308
  6.5 89.8 %reduce-scatter.2.cloned.1.call-start = ((), (), s32[]{:S(2)}) async-start(), calls=%async_computation.3 | async-start | bytes 2506752 | tf_op jit(solution)/shard_map/reduce_scatter | solution.py:192
  8.1 11.0 %collective-permute-start = (f32[4,129]{1,0:T(4,128)S(1)}, f32[4,129]{1,0:T(4,128)S(1)}, u32[]{:S(2)}, u32[]{:S(2)}) collective-permute-start(f32[4,129]{1,0:T(4,128)S(1)} %pad_maximum_fusion.3), channel_id=1, source_target_pairs={{15,0},{0,1},{1,2},{2,3},{3,4},{4,5},{5,6},{6,7},{7,8},{8,9},{9,10... | collective-permute-start | bytes 6200 | tf_op jit(solution)/shard_map/ppermute | solution.py:63
  13.3 16.6 %collective-permute-start.1 = (bf16[2,64,128]{2,1,0:T(8,128)(2,1)S(1)}, bf16[2,64,128]{2,1,0:T(8,128)(2,1)S(1)}, u32[]{:S(2)}, u32[]{:S(2)}) collective-permute-start(bf16[2,64,128]{2,1,0:T(8,128)(2,1)S(1)} %get-tuple-element.11), channel_id=1, source_target_pairs={{0,1},{1,2},{2,3},{3,4},{4,5},{5,6},{6,7},{7,8},{8,9},{9,10},{10,1... | collective-permute-start | bytes 98312 | tf_op jit(solution)/shard_map/ppermute | solution.py:72
  14.6 15.3 %collective-permute-start.2 = (bf16[2,64,128]{2,1,0:T(8,128)(2,1)S(1)}, bf16[2,64,128]{2,1,0:T(8,128)(2,1)S(1)}, u32[]{:S(2)}, u32[]{:S(2)}) collective-permute-start(bf16[2,64,128]{2,1,0:T(8,128)(2,1)S(1)} %get-tuple-element.12), channel_id=1, source_target_pairs={{1,0},{2,1},{3,2},{4,3},{5,4},{6,5},{7,6},{8,7},{9,8},{10,9},{11,1... | collective-permute-start | bytes 98312 | tf_op jit(solution)/shard_map/ppermute | solution.py:75
  21.3 8.6 %copy-start.3 = (bf16[512,128]{1,0:T(8,128)(2,1)S(1)}, bf16[512,128]{1,0:T(8,128)(2,1)}, u32[]{:S(2)}) copy-start(bf16[512,128]{1,0:T(8,128)(2,1)} %param.10) | copy-start | bytes 393220
  21.3 8.7 %copy-start.4 = (bf16[512,128]{1,0:T(8,128)(2,1)S(1)}, bf16[512,128]{1,0:T(8,128)(2,1)}, u32[]{:S(2)}) copy-start(bf16[512,128]{1,0:T(8,128)(2,1)} %param.11) | copy-start | bytes 393220
  30.0 4.8 %copy-start.1 = (bf16[8192,128]{1,0:T(8,128)(2,1)S(1)}, bf16[8192,128]{1,0:T(8,128)(2,1)}, u32[]{:S(2)}) copy-start(bf16[8192,128]{1,0:T(8,128)(2,1)} %get-tuple-element.8) | copy-start | bytes 6291460
  36.8 1.7 %copy-start.5 = (s32[128]{0:T(128)S(1)}, s32[128]{0:T(128)}, u32[]{:S(2)}) copy-start(s32[128]{0:T(128)} %param.14) | copy-start | bytes 1540
  99.8 25.4 %all-to-all-start = ((bf16[8,4,64,128]{3,2,1,0:T(8,128)(2,1)}), bf16[8,4,64,128]{3,2,1,0:T(8,128)(2,1)S(1)}, u32[]{:S(2)}, u32[]{:S(2)}) async-start(bf16[8,4,64,128]{3,2,1,0:T(8,128)(2,1)} %broadcast_in_dim.70), calls=%async_computation.1 | async-start | bytes 1048576 | tf_op jit(solution)/shard_map/all_to_all | solution.py:104
  130.2 2.2 %copy-start.2 = (f32[8192,128]{1,0:T(8,128)S(1)}, f32[8192,128]{1,0:T(8,128)}, u32[]{:S(2)}) copy-start(f32[8192,128]{1,0:T(8,128)} %get-tuple-element.7) | copy-start | bytes 12582916
Sparse Core Ops, SparseCore 0:
  38.6 57.6 reduce-scatter.1

commit v10 on v9

--- a/solution.py
+++ b/solution.py
@@ -12,7 +12,7 @@
 CORES = 2
 MEM = ("z", "core")
 
-def advect_kernel(halo_ref, s_ref, x_ref, f_ref, fb_ref, carry_ref):
+def advect_kernel(halo_ref, s_ref, x_ref, f_ref, fb_ref, sum_ref, carry_ref):
     @pl.when(pl.program_id(0) == 0)
     def _():
         carry_ref[...] = halo_ref[...]
@@ -28,7 +28,12 @@
         carry_ref[k : k + 1, :] = x[last:, :]
         x = x - s * (x - before)
     f_ref[...] = x
-    fb_ref[...] = x.astype(jnp.bfloat16)
+    rounded = x.astype(jnp.bfloat16)
+    fb_ref[...] = rounded
+    totals = jnp.sum(rounded.astype(jnp.float32), axis=1, keepdims=True)
+    for q in range(sum_ref.shape[0]):
+        column = jnp.broadcast_to(totals[q * lanes : (q + 1) * lanes, :], (lanes, lanes))
+        sum_ref[q : q + 1, :] = column.T[0:1, :]
 
 def advect(halo, speeds, x, interpret=False):
     cells, width = x.shape
@@ -41,8 +46,16 @@
             pl.BlockSpec((rows // width, width), lambda t: (t, 0)),
             pl.BlockSpec((rows, width), lambda t: (t, 0)),
         ],
-        out_specs=[pl.BlockSpec((rows, width), lambda t: (t, 0)), pl.BlockSpec((rows, width), lambda t: (t, 0))],
-        out_shape=[jax.ShapeDtypeStruct(x.shape, jnp.float32), jax.ShapeDtypeStruct(x.shape, jnp.bfloat16)],
+        out_specs=[
+            pl.BlockSpec((rows, width), lambda t: (t, 0)),
+            pl.BlockSpec((rows, width), lambda t: (t, 0)),
+            pl.BlockSpec((rows // width, width), lambda t: (t, 0)),
+        ],
+        out_shape=[
+            jax.ShapeDtypeStruct(x.shape, jnp.float32),
+            jax.ShapeDtypeStruct(x.shape, jnp.bfloat16),
+            jax.ShapeDtypeStruct((cells // width, width), jnp.float32),
+        ],
         scratch_shapes=[pltpu.VMEM((8, width), jnp.float32)],
         compiler_params=pltpu.CompilerParams(dimension_semantics=("arbitrary",)),
         interpret=interpret,
@@ -156,7 +169,7 @@
     arrived = passed_along(outgoing, "reg", 1)
     width = concentration_map.shape[1]
     halo = halo_rows(arrived[:, :-1], arrived[:, -1], width)
-    concentration_map, first_guess_state = advect(halo, flow_speed_ratio, concentration_map)
+    concentration_map, first_guess_state, cell_sums = advect(halo, flow_speed_ratio, concentration_map)
     lend = edge_list.shape[2]
     edge_rows = edge_list.reshape(-1)
     own = obs_pert.shape[0]
@@ -186,7 +199,7 @@
     full = jnp.einsum("brm,blm->brl", cells_p, obs_p, preferred_element_type=jnp.float32)
     upper = (jnp.arange(2 * KB) >= KB)[None, None, :]
     cross = jnp.where(upper, full[:, BLOCK:, :], full[:, :BLOCK, :])
-    sum_cells = jnp.sum(first_guess_state.astype(jnp.float32), 1).reshape(pairs, 1, 2 * BLOCK)
+    sum_cells = cell_sums.reshape(pairs, 1, 2 * BLOCK)
     sum_obs = jnp.sum(obs_rows.astype(jnp.float32), 1).reshape(pairs, 1, 2 * KB)
     payload = jnp.concatenate([cross, sum_cells, sum_obs], 1)
     got = lax.psum_scatter(

time: 143 us -> 142 us (level)
  other arithmetic: 9.09 us -> 6.86 us
    reduce_sum x1 -> x0, other arithmetic: 2.21 us -> none  [per_device(): jnp.sum(first_guess_state.astype(jnp.float32), 1)]
  transfers between devices with their start and end apart: 5 -> 5, of which waited for: 2 -> 2; matrix products, arithmetic and copies ran while one was open for 11% -> 9% of each run, Pallas kernels for 5% -> 5%
where the time goes in v10:
time: 142 us; the launch traced here: 141 us
  waiting for transfers between devices  68.7 us (48%)
  matrix products  15.1 us (11%)
  starting transfers between devices  14.4 us (10%)
  between operations  13.6 us (10%)
  local copies, waits for them, and re-layouts  10.4 us (7%)
  Pallas kernels  7.49 us (5%)
  other arithmetic  6.86 us (5%)
  blocking collectives  4.68 us (3%)
    reduce_scatter x1, waiting for transfers between devices, per_device(): lax.psum_scatter(payload.reshape(parts, share, BLOCK + 2, 2 * KB), MEM, s...  56.5 us
    all_to_all x1, waiting for transfers between devices, gathered_copies(): lax.all_to_all(jnp.broadcast_to(value, (chips, *value.shape)), 'z', split...  12.1 us
    pallas_call x1, Pallas kernels, advect(): pl.pallas_call(advect_kernel, grid=(cells // rows,), in_specs=[pl.BlockSp...  7.49 us
    all_to_all x1, starting transfers between devices, gathered_copies(): lax.all_to_all(jnp.broadcast_to(value, (chips, *value.shape)), 'z', split...  7.4 us
    dot_general x1, matrix products, per_device(): jnp.dot(picks, extended[1], preferred_element_type=jnp.float32)  5.73 us
    dot_general x1, matrix products, per_device(): jnp.dot(picks, extended[0], preferred_element_type=jnp.float32)  4.75 us
    all_to_all x1, blocking collectives, gathered_copies(): lax.all_to_all(jnp.broadcast_to(along_z, (cores, *along_z.shape)), 'core'...  4.68 us
    ppermute x1, starting transfers between devices, padded(): lax.ppermute(lax.slice_in_dim(block, 0, width, axis=dim), axis, backward)  3.49 us
  transfers between devices with their start and end apart: 5, of which 2 were waited for; matrix products, arithmetic and copies ran while one was open for 9% of the time, Pallas kernels for 5%

profile of v10, /device:TPU:1, one launch (start us, length us, event | category | flops | bytes accessed | tf_op | source)
XLA Modules:
  0.0 141.2 jit_solution(4157931882072652945)
XLA Ops:
  6.5 0.8 slice_bitcast_fusion.4
  7.4 0.7 slice.81
  8.1 2.1 %collective-permute-start = (f32[4,129]{1,0:T(4,128)S(1)}, f32[4,129]{1,0:T(4,128)S(1)}, u32[]{:S(2)}, u32[]{:S(2)}) collective-permute-start(f32[4,129]{1,0:T(4,128)S(1)} %pad_maximum_fusion.3), channel_id=1, source_target_pairs={{15,0},{0,1},{1,2},{2,3},{3,4},{4,5},{5,6},{6,7},{7,8},{8,9},{9,10... | collective-permute-start | bytes 6200 | tf_op jit(solution)/shard_map/ppermute | solution.py:76
  10.2 0.8 eq.56
  11.0 1.1 fusion.11
  12.1 1.2 fusion.12
  13.4 1.4 collective-permute-start.1
  14.7 3.5 %collective-permute-start.2 = (bf16[2,64,128]{2,1,0:T(8,128)(2,1)S(1)}, bf16[2,64,128]{2,1,0:T(8,128)(2,1)S(1)}, u32[]{:S(2)}, u32[]{:S(2)}) collective-permute-start(bf16[2,64,128]{2,1,0:T(8,128)(2,1)S(1)} %get-tuple-element.14), channel_id=1, source_target_pairs={{1,0},{2,1},{3,2},{4,3},{5,4},{6,5},{7,6},{8,7},{9,8},{10,9},{11,1... | collective-permute-start | bytes 98312 | tf_op jit(solution)/shard_map/ppermute | solution.py:88
  18.2 0.8 copy.29
  19.5 0.5 slice.110
  20.1 0.7 multiply_subtract_fusion.1
  20.7 0.6 concatenate.23.halo_ref
  21.4 7.5 %shard_map.82 = (f32[8192,128]{1,0:T(8,128)}, bf16[8192,128]{1,0:T(8,128)(2,1)}, f32[64,128]{1,0:T(8,128)}) custom-call(f32[8,128]{1,0:T(8,128)} %concatenate.23.halo_ref, f32[64,128]{1,0:T(8,128)} %bitcast.52, f32[8192,128]{1,0:T(8,128)} %x_ref.1), custom_call_target="tpu_custom_call" | custom-call | tf_op jit(solution)/shard_map/pallas_call | solution.py:41
  28.9 4.7 %convert_reduce_fusion = (f32[8192]{0:T(1024)S(1)}, bf16[8192,128]{1,0:T(8,128)(2,1)S(1)}) fusion(bf16[2,640,128]{2,1,0:T(8,128)(2,1)S(1)} %pad_maximum_fusion.1, s32[8192]{0:T(1024)S(1)} %eq.52), kind=kOutput, calls=%fused_computation.9 | convolution fusion | flops 1350557696 | bytes 2326528 | tf_op jit(solution)/shard_map/dot_general | solution.py:195
  33.7 1.6 %fusion.26 = f32[64,128,128]{2,1,0:T(8,128)S(1)} fusion(bf16[64,128,128]{2,1,0:T(8,128)(2,1)S(1)} %bitcast.45, bf16[64,128,128]{2,1,0:T(8,128)(2,1)S(1)} %bitcast.46), kind=kOutput, calls=%fused_computation.67 | convolution fusion | flops 268435456 | bytes 8388608 | tf_op jit(solution)/shard_map/brm,blm->brl/dot_general | solution.py:199
  35.3 0.5 slice_select_fusion
  35.7 0.3 copy-done.5
  36.0 1.7 %pad_maximum_fusion = f32[16,4,66,128]{3,2,1,0:T(8,128)} fusion(f32[16,4,1,128]{3,2,1,0:T(1,128)S(1)} %bitcast.54, f32[16,4,1,128]{3,2,1,0:T(1,128)S(1)} %bitcast.53, f32[16,4,64,128]{3,2,1,0:T(8,128)S(1)} %bitcast.44), kind=kLoop, calls=%fused_computation.10 | loop fusion | flops 1081344 | bytes 4325376 | tf_op jit(solution)/shard_map/concatenate | solution.py:204
  38.0 0.6 gather_fusion
  39.1 56.5 %reduce-scatter.2.cloned.1.call-done = f32[1,4,66,128]{3,2,1,0:T(8,128)} async-done(((f32[16,4,66,128]{3,2,1,0:T(8,128)}), f32[1,4,66,128]{3,2,1,0:T(8,128)}) %reduce-scatter.2.cloned.1.call-update) | async-done | bytes 135184 | tf_op jit(solution)/shard_map/reduce_scatter | solution.py:205
  95.6 0.8 fusion.25
  96.6 0.3 broadcast_in_dim.67
  97.1 1.0 fusion.16
  98.1 0.9 broadcast_in_dim.70
  99.1 7.4 %all-to-all-start = ((bf16[8,4,64,128]{3,2,1,0:T(8,128)(2,1)}), bf16[8,4,64,128]{3,2,1,0:T(8,128)(2,1)S(1)}, u32[]{:S(2)}, u32[]{:S(2)}) async-start(bf16[8,4,64,128]{3,2,1,0:T(8,128)(2,1)} %broadcast_in_dim.70), calls=%async_computation.1 | async-start | bytes 1048576 | tf_op jit(solution)/shard_map/all_to_all | solution.py:117
  106.6 5.7 %fusion.5 = bf16[8192,128]{1,0:T(8,128)(2,1)S(1)} fusion(s32[8192]{0:T(1024)S(1)} %eq.52, bf16[2,640,128]{2,1,0:T(8,128)(2,1)S(1)} %pad_maximum_fusion.1), kind=kOutput, calls=%fused_computation.7 | convolution fusion | flops 1348468736 | bytes 2293760 | tf_op jit(solution)/shard_map/dot_general | solution.py:196
  112.3 12.1 %all-to-all-done = bf16[8,4,64,128]{3,2,1,0:T(8,128)(2,1)S(1)} async-done(((bf16[8,4,64,128]{3,2,1,0:T(8,128)(2,1)}), bf16[8,4,64,128]{3,2,1,0:T(8,128)(2,1)S(1)}, u32[]{:S(2)}, u32[]{:S(2)}) %all-to-all-start) | async-done | bytes 524320 | tf_op jit(solution)/shard_map/all_to_all | solution.py:117
  124.4 0.3 broadcast_in_dim.71
  124.7 4.7 %all_to_all.10 = bf16[2,8,4,64,128]{4,3,2,1,0:T(8,128)(2,1)S(1)} all-to-all(bf16[2,8,4,64,128]{4,3,2,1,0:T(8,128)(2,1)S(1)} %broadcast_in_dim.71), channel_id=1, replica_groups=mesh['z'=8,'core'=2,'reg'=16] {'core'}, dimensions={0} | all-to-all | bytes 2097152 | tf_op jit(solution)/shard_map/all_to_all | solution.py:120
  129.5 0.7 fusion.10
  130.2 1.5 %copy-done.1 = f32[8192,128]{1,0:T(8,128)S(1)} copy-done((f32[8192,128]{1,0:T(8,128)S(1)}, f32[8192,128]{1,0:T(8,128)}, u32[]{:S(2)}) %copy-start.1) | copy-done | bytes 4194328
  131.7 2.7 %convert_add_fusion = f32[8192,128]{1,0:T(8,128)} fusion(f32[8192,128]{1,0:T(8,128)S(1)} %copy-done.1, bf16[64,128,128]{2,1,0:T(8,128)(2,1)S(1)} %fusion.10), kind=kLoop, calls=%fused_computation.8 | loop fusion | flops 2097152 | bytes 10485760 | tf_op jit(solution)/shard_map/add | solution.py:234
  (48 shorter events, 1.9 us)
Async XLA Ops:
  6.5 32.3 %copy-start = (f32[128,64]{0,1:T(8,128)S(1)}, f32[128,64]{0,1:T(8,128)}, u32[]{:S(2)}) copy-start(f32[128,64]{0,1:T(8,128)} %param.15) | copy-start | bytes 98308
  6.5 89.0 %reduce-scatter.2.cloned.1.call-start = ((), (), s32[]{:S(2)}) async-start(), calls=%async_computation.3 | async-start | bytes 2506752 | tf_op jit(solution)/shard_map/reduce_scatter | solution.py:205
  8.1 11.1 %collective-permute-start = (f32[4,129]{1,0:T(4,128)S(1)}, f32[4,129]{1,0:T(4,128)S(1)}, u32[]{:S(2)}, u32[]{:S(2)}) collective-permute-start(f32[4,129]{1,0:T(4,128)S(1)} %pad_maximum_fusion.3), channel_id=1, source_target_pairs={{15,0},{0,1},{1,2},{2,3},{3,4},{4,5},{5,6},{6,7},{7,8},{8,9},{9,10... | collective-permute-start | bytes 6200 | tf_op jit(solution)/shard_map/ppermute | solution.py:76
  12.1 16.8 %copy-start.3 = (bf16[512,128]{1,0:T(8,128)(2,1)S(1)}, bf16[512,128]{1,0:T(8,128)(2,1)}, u32[]{:S(2)}) copy-start(bf16[512,128]{1,0:T(8,128)(2,1)} %param.10) | copy-start | bytes 393220
  12.1 16.8 %copy-start.4 = (bf16[512,128]{1,0:T(8,128)(2,1)S(1)}, bf16[512,128]{1,0:T(8,128)(2,1)}, u32[]{:S(2)}) copy-start(bf16[512,128]{1,0:T(8,128)(2,1)} %param.11) | copy-start | bytes 393220
  13.4 15.5 %collective-permute-start.1 = (bf16[2,64,128]{2,1,0:T(8,128)(2,1)S(1)}, bf16[2,64,128]{2,1,0:T(8,128)(2,1)S(1)}, u32[]{:S(2)}, u32[]{:S(2)}) collective-permute-start(bf16[2,64,128]{2,1,0:T(8,128)(2,1)S(1)} %get-tuple-element.13), channel_id=1, source_target_pairs={{0,1},{1,2},{2,3},{3,4},{4,5},{5,6},{6,7},{7,8},{8,9},{9,10},{10,1... | collective-permute-start | bytes 98312 | tf_op jit(solution)/shard_map/ppermute | solution.py:85
  14.7 14.1 %collective-permute-start.2 = (bf16[2,64,128]{2,1,0:T(8,128)(2,1)S(1)}, bf16[2,64,128]{2,1,0:T(8,128)(2,1)S(1)}, u32[]{:S(2)}, u32[]{:S(2)}) collective-permute-start(bf16[2,64,128]{2,1,0:T(8,128)(2,1)S(1)} %get-tuple-element.14), channel_id=1, source_target_pairs={{1,0},{2,1},{3,2},{4,3},{5,4},{6,5},{7,6},{8,7},{9,8},{10,9},{11,1... | collective-permute-start | bytes 98312 | tf_op jit(solution)/shard_map/ppermute | solution.py:88
  28.9 4.8 %copy-start.2 = (bf16[8192,128]{1,0:T(8,128)(2,1)S(1)}, bf16[8192,128]{1,0:T(8,128)(2,1)}, u32[]{:S(2)}) copy-start(bf16[8192,128]{1,0:T(8,128)(2,1)} %get-tuple-element.9) | copy-start | bytes 6291460
  35.3 0.8 copy-start.5
  36.0 1.7 %copy-start.6 = (s32[128]{0:T(128)S(1)}, s32[128]{0:T(128)}, u32[]{:S(2)}) copy-start(s32[128]{0:T(128)} %param.14) | copy-start | bytes 1540
  99.1 25.4 %all-to-all-start = ((bf16[8,4,64,128]{3,2,1,0:T(8,128)(2,1)}), bf16[8,4,64,128]{3,2,1,0:T(8,128)(2,1)S(1)}, u32[]{:S(2)}, u32[]{:S(2)}) async-start(bf16[8,4,64,128]{3,2,1,0:T(8,128)(2,1)} %broadcast_in_dim.70), calls=%async_computation.1 | async-start | bytes 1048576 | tf_op jit(solution)/shard_map/all_to_all | solution.py:117
  129.5 2.2 %copy-start.1 = (f32[8192,128]{1,0:T(8,128)S(1)}, f32[8192,128]{1,0:T(8,128)}, u32[]{:S(2)}) copy-start(f32[8192,128]{1,0:T(8,128)} %get-tuple-element.8) | copy-start | bytes 12582916
Sparse Core Ops, SparseCore 0:
  37.8 57.6 reduce-scatter.1

commit v11 on v10

--- a/solution.py
+++ b/solution.py
@@ -117,9 +117,9 @@
     along_z = lax.all_to_all(
         jnp.broadcast_to(value, (chips, *value.shape)), "z", split_axis=0, concat_axis=0, tiled=True
     )
-    both = lax.all_to_all(
-        jnp.broadcast_to(along_z, (cores, *along_z.shape)), "core", split_axis=0, concat_axis=0, tiled=True
-    )
+    other = lax.ppermute(along_z, "core", [(0, 1), (1, 0)])
+    low = lax.axis_index("core") == 0
+    both = jnp.stack([jnp.where(low, along_z, other), jnp.where(low, other, along_z)])
     return laid_out(jnp.swapaxes(both, 0, 1).reshape(chips * cores, *value.shape), dim)
 
 

time: 142 us -> 143 us (level)
  waiting for transfers between devices: 68.7 us -> 74.4 us
  blocking collectives: 4.68 us -> 0 us
    all_to_all x1, waiting for transfers between devices: 12.1 us -> 17.9 us  [gathered_copies(): lax.all_to_all(jnp.broadcast_to(value, (chips, *value.shape)), 'z', split...]
    all_to_all x1 -> x0, blocking collectives: 4.68 us -> none  [gathered_copies(): lax.all_to_all(jnp.broadcast_to(along_z, (cores, *along_z.shape)), 'core'...]
  transfers between devices with their start and end apart: 5 -> 6, of which waited for: 2 -> 2; matrix products, arithmetic and copies ran while one was open for 9% -> 9% of each run, Pallas kernels for 5% -> 5%
where the time goes in v11:
time: 143 us
  waiting for transfers between devices  74.4 us (52%)
  matrix products  15.1 us (11%)
  starting transfers between devices  14.9 us (10%)
  between operations  13.7 us (10%)
  local copies, waits for them, and re-layouts  10 us (7%)
  Pallas kernels  7.49 us (5%)
  other arithmetic  7.03 us (5%)
    reduce_scatter x1, waiting for transfers between devices, per_device(): lax.psum_scatter(payload.reshape(parts, share, BLOCK + 2, 2 * KB), MEM, s...  56.5 us
    all_to_all x1, waiting for transfers between devices, gathered_copies(): lax.all_to_all(jnp.broadcast_to(value, (chips, *value.shape)), 'z', split...  17.9 us
    pallas_call x1, Pallas kernels, advect(): pl.pallas_call(advect_kernel, grid=(cells // rows,), in_specs=[pl.BlockSp...  7.49 us
    all_to_all x1, starting transfers between devices, gathered_copies(): lax.all_to_all(jnp.broadcast_to(value, (chips, *value.shape)), 'z', split...  7.4 us
    dot_general x1, matrix products, per_device(): jnp.dot(picks, extended[1], preferred_element_type=jnp.float32)  5.71 us
    dot_general x1, matrix products, per_device(): jnp.dot(picks, extended[0], preferred_element_type=jnp.float32)  4.75 us
    ppermute x1, starting transfers between devices, padded(): lax.ppermute(lax.slice_in_dim(block, 0, width, axis=dim), axis, backward)  3.49 us
  transfers between devices with their start and end apart: 6, of which 2 were waited for; matrix products, arithmetic and copies ran while one was open for 9% of the time, Pallas kernels for 5%

profile of v11, /device:TPU:1, one launch (start us, length us, event | category | flops | bytes accessed | tf_op | source)
XLA Modules:
  0.0 142.5 jit_solution(10782459980145405107)
XLA Ops:
  6.5 0.8 slice_bitcast_fusion.4
  7.4 0.7 slice.81
  8.1 2.1 %collective-permute-start = (f32[4,129]{1,0:T(4,128)S(1)}, f32[4,129]{1,0:T(4,128)S(1)}, u32[]{:S(2)}, u32[]{:S(2)}) collective-permute-start(f32[4,129]{1,0:T(4,128)S(1)} %pad_maximum_fusion.4), channel_id=1, source_target_pairs={{15,0},{0,1},{1,2},{2,3},{3,4},{4,5},{5,6},{6,7},{7,8},{8,9},{9,10... | collective-permute-start | bytes 6200 | tf_op jit(solution)/shard_map/ppermute | solution.py:76
  10.2 0.8 eq.60
  11.0 1.1 fusion.11
  12.1 1.2 fusion.12
  13.4 1.4 collective-permute-start.1
  14.7 3.5 %collective-permute-start.2 = (bf16[2,64,128]{2,1,0:T(8,128)(2,1)S(1)}, bf16[2,64,128]{2,1,0:T(8,128)(2,1)S(1)}, u32[]{:S(2)}, u32[]{:S(2)}) collective-permute-start(bf16[2,64,128]{2,1,0:T(8,128)(2,1)S(1)} %get-tuple-element.16), channel_id=1, source_target_pairs={{1,0},{2,1},{3,2},{4,3},{5,4},{6,5},{7,6},{8,7},{9,8},{10,9},{11,1... | collective-permute-start | bytes 98312 | tf_op jit(solution)/shard_map/ppermute | solution.py:88
  18.2 0.8 copy.16
  19.5 0.5 slice.110
  20.1 0.7 multiply_subtract_fusion.1
  20.7 0.6 concatenate.23.halo_ref
  21.4 7.5 %shard_map.82 = (f32[8192,128]{1,0:T(8,128)}, bf16[8192,128]{1,0:T(8,128)(2,1)}, f32[64,128]{1,0:T(8,128)}) custom-call(f32[8,128]{1,0:T(8,128)} %concatenate.23.halo_ref, f32[64,128]{1,0:T(8,128)} %bitcast.58, f32[8192,128]{1,0:T(8,128)} %x_ref.1), custom_call_target="tpu_custom_call" | custom-call | tf_op jit(solution)/shard_map/pallas_call | solution.py:41
  28.9 4.7 %convert_reduce_fusion = (f32[8192]{0:T(1024)S(1)}, bf16[8192,128]{1,0:T(8,128)(2,1)S(1)}) fusion(bf16[2,640,128]{2,1,0:T(8,128)(2,1)S(1)} %pad_maximum_fusion.2, s32[8192]{0:T(1024)S(1)} %eq.56), kind=kOutput, calls=%fused_computation.9 | convolution fusion | flops 1350557696 | bytes 2326528 | tf_op jit(solution)/shard_map/dot_general | solution.py:195
  33.7 1.6 %fusion.26 = f32[64,128,128]{2,1,0:T(8,128)S(1)} fusion(bf16[64,128,128]{2,1,0:T(8,128)(2,1)S(1)} %bitcast.51, bf16[64,128,128]{2,1,0:T(8,128)(2,1)S(1)} %bitcast.52), kind=kOutput, calls=%fused_computation.70 | convolution fusion | flops 268435456 | bytes 8388608 | tf_op jit(solution)/shard_map/brm,blm->brl/dot_general | solution.py:199
  35.3 0.5 slice_select_fusion
  35.7 0.3 copy-done.5
  36.0 1.7 %pad_maximum_fusion = f32[16,4,66,128]{3,2,1,0:T(8,128)} fusion(f32[16,4,1,128]{3,2,1,0:T(1,128)S(1)} %bitcast.60, f32[16,4,1,128]{3,2,1,0:T(1,128)S(1)} %bitcast.59, f32[16,4,64,128]{3,2,1,0:T(8,128)S(1)} %bitcast.50), kind=kLoop, calls=%fused_computation.10 | loop fusion | flops 1081344 | bytes 4325376 | tf_op jit(solution)/shard_map/concatenate | solution.py:204
  38.0 0.6 gather_fusion
  39.1 56.5 %reduce-scatter.2.cloned.1.call-done = f32[1,4,66,128]{3,2,1,0:T(8,128)} async-done(((f32[16,4,66,128]{3,2,1,0:T(8,128)}), f32[1,4,66,128]{3,2,1,0:T(8,128)}) %reduce-scatter.2.cloned.1.call-update) | async-done | bytes 135184 | tf_op jit(solution)/shard_map/reduce_scatter | solution.py:205
  95.6 0.8 fusion.25
  96.6 0.3 broadcast_in_dim.64
  96.9 0.2 reshape.165
  97.1 1.0 fusion.16
  98.1 0.9 broadcast_in_dim.67
  99.0 7.4 %all-to-all-start = ((bf16[8,4,64,128]{3,2,1,0:T(8,128)(2,1)}), bf16[8,4,64,128]{3,2,1,0:T(8,128)(2,1)S(1)}, u32[]{:S(2)}, u32[]{:S(2)}) async-start(bf16[8,4,64,128]{3,2,1,0:T(8,128)(2,1)} %broadcast_in_dim.67), calls=%async_computation.1 | async-start | bytes 1048576 | tf_op jit(solution)/shard_map/all_to_all | solution.py:117
  106.5 17.9 %all-to-all-done = bf16[8,4,64,128]{3,2,1,0:T(8,128)(2,1)S(1)} async-done(((bf16[8,4,64,128]{3,2,1,0:T(8,128)(2,1)}), bf16[8,4,64,128]{3,2,1,0:T(8,128)(2,1)S(1)}, u32[]{:S(2)}, u32[]{:S(2)}) %all-to-all-start) | async-done | bytes 524320 | tf_op jit(solution)/shard_map/all_to_all | solution.py:117
  124.4 0.5 collective-permute-start.3
  124.9 5.7 %fusion.5 = bf16[8192,128]{1,0:T(8,128)(2,1)S(1)} fusion(s32[8192]{0:T(1024)S(1)} %eq.56, bf16[2,640,128]{2,1,0:T(8,128)(2,1)S(1)} %pad_maximum_fusion.2), kind=kOutput, calls=%fused_computation.7 | convolution fusion | flops 1348468736 | bytes 2293760 | tf_op jit(solution)/shard_map/dot_general | solution.py:196
  130.8 0.7 fusion.10
  131.5 1.5 %copy-done.1 = f32[8192,128]{1,0:T(8,128)S(1)} copy-done((f32[8192,128]{1,0:T(8,128)S(1)}, f32[8192,128]{1,0:T(8,128)}, u32[]{:S(2)}) %copy-start.1) | copy-done | bytes 4194328
  133.0 2.7 %convert_add_fusion = f32[8192,128]{1,0:T(8,128)} fusion(f32[8192,128]{1,0:T(8,128)S(1)} %copy-done.1, bf16[64,128,128]{2,1,0:T(8,128)(2,1)S(1)} %fusion.10), kind=kLoop, calls=%fused_computation.8 | loop fusion | flops 2097152 | bytes 10485760 | tf_op jit(solution)/shard_map/add | solution.py:234
  (49 shorter events, 1.8 us)
Async XLA Ops:
  6.5 32.3 %copy-start = (f32[128,64]{0,1:T(8,128)S(1)}, f32[128,64]{0,1:T(8,128)}, u32[]{:S(2)}) copy-start(f32[128,64]{0,1:T(8,128)} %param.15) | copy-start | bytes 98308
  6.5 89.0 %reduce-scatter.2.cloned.1.call-start = ((), (), s32[]{:S(2)}) async-start(), calls=%async_computation.2 | async-start | bytes 2506752 | tf_op jit(solution)/shard_map/reduce_scatter | solution.py:205
  8.1 11.1 %collective-permute-start = (f32[4,129]{1,0:T(4,128)S(1)}, f32[4,129]{1,0:T(4,128)S(1)}, u32[]{:S(2)}, u32[]{:S(2)}) collective-permute-start(f32[4,129]{1,0:T(4,128)S(1)} %pad_maximum_fusion.4), channel_id=1, source_target_pairs={{15,0},{0,1},{1,2},{2,3},{3,4},{4,5},{5,6},{6,7},{7,8},{8,9},{9,10... | collective-permute-start | bytes 6200 | tf_op jit(solution)/shard_map/ppermute | solution.py:76
  12.1 16.8 %copy-start.3 = (bf16[512,128]{1,0:T(8,128)(2,1)S(1)}, bf16[512,128]{1,0:T(8,128)(2,1)}, u32[]{:S(2)}) copy-start(bf16[512,128]{1,0:T(8,128)(2,1)} %param.10) | copy-start | bytes 393220
  12.1 16.8 %copy-start.4 = (bf16[512,128]{1,0:T(8,128)(2,1)S(1)}, bf16[512,128]{1,0:T(8,128)(2,1)}, u32[]{:S(2)}) copy-start(bf16[512,128]{1,0:T(8,128)(2,1)} %param.11) | copy-start | bytes 393220
  13.4 15.5 %collective-permute-start.1 = (bf16[2,64,128]{2,1,0:T(8,128)(2,1)S(1)}, bf16[2,64,128]{2,1,0:T(8,128)(2,1)S(1)}, u32[]{:S(2)}, u32[]{:S(2)}) collective-permute-start(bf16[2,64,128]{2,1,0:T(8,128)(2,1)S(1)} %get-tuple-element.15), channel_id=1, source_target_pairs={{0,1},{1,2},{2,3},{3,4},{4,5},{5,6},{6,7},{7,8},{8,9},{9,10},{10,1... | collective-permute-start | bytes 98312 | tf_op jit(solution)/shard_map/ppermute | solution.py:85
  14.7 14.1 %collective-permute-start.2 = (bf16[2,64,128]{2,1,0:T(8,128)(2,1)S(1)}, bf16[2,64,128]{2,1,0:T(8,128)(2,1)S(1)}, u32[]{:S(2)}, u32[]{:S(2)}) collective-permute-start(bf16[2,64,128]{2,1,0:T(8,128)(2,1)S(1)} %get-tuple-element.16), channel_id=1, source_target_pairs={{1,0},{2,1},{3,2},{4,3},{5,4},{6,5},{7,6},{8,7},{9,8},{10,9},{11,1... | collective-permute-start | bytes 98312 | tf_op jit(solution)/shard_map/ppermute | solution.py:88
  28.9 4.8 %copy-start.2 = (bf16[8192,128]{1,0:T(8,128)(2,1)S(1)}, bf16[8192,128]{1,0:T(8,128)(2,1)}, u32[]{:S(2)}) copy-start(bf16[8192,128]{1,0:T(8,128)(2,1)} %get-tuple-element.9) | copy-start | bytes 6291460
  35.3 0.8 copy-start.5
  36.0 1.7 %copy-start.6 = (s32[128]{0:T(128)S(1)}, s32[128]{0:T(128)}, u32[]{:S(2)}) copy-start(s32[128]{0:T(128)} %param.14) | copy-start | bytes 1540
  99.0 25.4 %all-to-all-start = ((bf16[8,4,64,128]{3,2,1,0:T(8,128)(2,1)}), bf16[8,4,64,128]{3,2,1,0:T(8,128)(2,1)S(1)}, u32[]{:S(2)}, u32[]{:S(2)}) async-start(bf16[8,4,64,128]{3,2,1,0:T(8,128)(2,1)} %broadcast_in_dim.67), calls=%async_computation.1 | async-start | bytes 1048576 | tf_op jit(solution)/shard_map/all_to_all | solution.py:117
  124.4 6.2 %collective-permute-start.3 = (bf16[8,4,64,128]{3,2,1,0:T(8,128)(2,1)S(1)}, bf16[8,4,64,128]{3,2,1,0:T(8,128)(2,1)S(1)}, u32[]{:S(2)}, u32[]{:S(2)}) collective-permute-start(bf16[8,4,64,128]{3,2,1,0:T(8,128)(2,1)S(1)} %all-to-all-done), channel_id=1, source_target_pairs={{0,16},{16,0},{1,17},{17,1},{2,18},{18,2},{3,19},{19,3},{4,20},{20... | collective-permute-start | bytes 1572872 | tf_op jit(solution)/shard_map/ppermute | solution.py:120
  130.8 2.2 %copy-start.1 = (f32[8192,128]{1,0:T(8,128)S(1)}, f32[8192,128]{1,0:T(8,128)}, u32[]{:S(2)}) copy-start(f32[8192,128]{1,0:T(8,128)} %get-tuple-element.8) | copy-start | bytes 12582916
Sparse Core Ops, SparseCore 0:
  37.8 57.6 reduce-scatter.1

commit v12 on v10

--- a/solution.py
+++ b/solution.py
@@ -174,12 +174,11 @@
     edge_rows = edge_list.reshape(-1)
     own = obs_pert.shape[0]
     lent = (edge_rows[:, None] == jnp.arange(own)[None, :]).astype(jnp.bfloat16)
-    chosen = jnp.stack(
-        [
-            jnp.dot(lent, obs_pert, preferred_element_type=jnp.float32).astype(jnp.bfloat16),
-            jnp.dot(lent, obs_incr, preferred_element_type=jnp.float32).astype(jnp.bfloat16),
-        ]
-    )
+    member_dev = member_vectors.shape[1]
+    lent_rows = jnp.dot(
+        lent, jnp.concatenate([obs_pert, obs_incr], 1), preferred_element_type=jnp.float32
+    ).astype(jnp.bfloat16)
+    chosen = jnp.stack([lent_rows[:, :member_dev], lent_rows[:, member_dev:]])
     rimmed = padded(chosen, (("reg", 1),), lend)
     extended = jnp.concatenate(
         [rimmed[:, :lend], jnp.stack([obs_pert, obs_incr]), rimmed[:, -lend:]], 1

time: 142 us -> 141 us (level)
  no operation moved by 1% of the time
where the time goes in v12:
time: 141 us; the launch traced here: 140 us
  waiting for transfers between devices  68.7 us (49%)
  starting transfers between devices  14.4 us (10%)
  matrix products  13.9 us (10%)
  between operations  13.7 us (10%)
  local copies, waits for them, and re-layouts  10.4 us (7%)
  Pallas kernels  7.49 us (5%)
  other arithmetic  6.85 us (5%)
  blocking collectives  4.67 us (3%)
    reduce_scatter x1, waiting for transfers between devices, per_device(): lax.psum_scatter(payload.reshape(parts, share, BLOCK + 2, 2 * KB), MEM, s...  56.5 us
    all_to_all x1, waiting for transfers between devices, gathered_copies(): lax.all_to_all(jnp.broadcast_to(value, (chips, *value.shape)), 'z', split...  12.1 us
    pallas_call x1, Pallas kernels, advect(): pl.pallas_call(advect_kernel, grid=(cells // rows,), in_specs=[pl.BlockSp...  7.49 us
    all_to_all x1, starting transfers between devices, gathered_copies(): lax.all_to_all(jnp.broadcast_to(value, (chips, *value.shape)), 'z', split...  7.44 us
    dot_general x1, matrix products, per_device(): jnp.dot(picks, extended[1], preferred_element_type=jnp.float32)  5.73 us
    dot_general x1, matrix products, per_device(): jnp.dot(picks, extended[0], preferred_element_type=jnp.float32)  4.75 us
    all_to_all x1, blocking collectives, gathered_copies(): lax.all_to_all(jnp.broadcast_to(along_z, (cores, *along_z.shape)), 'core'...  4.67 us
    ppermute x1, starting transfers between devices, padded(): lax.ppermute(lax.slice_in_dim(block, 0, width, axis=dim), axis, backward)  3.49 us
  transfers between devices with their start and end apart: 5, of which 2 were waited for; matrix products, arithmetic and copies ran while one was open for 9% of the time, Pallas kernels for 5%

profile of v12, /device:TPU:1, one launch (start us, length us, event | category | flops | bytes accessed | tf_op | source)
XLA Modules:
  0.0 140.1 jit_solution(14452146445564829261)
XLA Ops:
  6.5 0.8 slice_bitcast_fusion.6
  7.4 0.7 slice.87
  8.1 2.1 %collective-permute-start = (f32[4,129]{1,0:T(4,128)S(1)}, f32[4,129]{1,0:T(4,128)S(1)}, u32[]{:S(2)}, u32[]{:S(2)}) collective-permute-start(f32[4,129]{1,0:T(4,128)S(1)} %pad_maximum_fusion.3), channel_id=1, source_target_pairs={{15,0},{0,1},{1,2},{2,3},{3,4},{4,5},{5,6},{6,7},{7,8},{8,9},{9,10... | collective-permute-start | bytes 6200 | tf_op jit(solution)/shard_map/ppermute | solution.py:76
  10.2 0.8 eq.56
  11.0 1.2 convolution_convert_fusion
  12.2 1.4 collective-permute-start.1
  13.6 3.5 %collective-permute-start.2 = (bf16[2,64,128]{2,1,0:T(8,128)(2,1)S(1)}, bf16[2,64,128]{2,1,0:T(8,128)(2,1)S(1)}, u32[]{:S(2)}, u32[]{:S(2)}) collective-permute-start(bf16[2,64,128]{2,1,0:T(8,128)(2,1)S(1)} %get-tuple-element.14), channel_id=1, source_target_pairs={{1,0},{2,1},{3,2},{4,3},{5,4},{6,5},{7,6},{8,7},{9,8},{10,9},{11,1... | collective-permute-start | bytes 98312 | tf_op jit(solution)/shard_map/ppermute | solution.py:88
  17.1 0.8 copy.29
  18.4 0.5 slice.118
  18.9 0.7 multiply_subtract_fusion.1
  19.6 0.6 concatenate.26.halo_ref
  20.2 7.5 %shard_map.82 = (f32[8192,128]{1,0:T(8,128)}, bf16[8192,128]{1,0:T(8,128)(2,1)}, f32[64,128]{1,0:T(8,128)}) custom-call(f32[8,128]{1,0:T(8,128)} %concatenate.26.halo_ref, f32[64,128]{1,0:T(8,128)} %bitcast.50, f32[8192,128]{1,0:T(8,128)} %x_ref.1), custom_call_target="tpu_custom_call" | custom-call | tf_op jit(solution)/shard_map/pallas_call | solution.py:41
  27.8 4.8 %convert_reduce_fusion = (f32[8192]{0:T(1024)S(1)}, bf16[8192,128]{1,0:T(8,128)(2,1)S(1)}) fusion(bf16[2,640,128]{2,1,0:T(8,128)(2,1)S(1)} %pad_maximum_fusion.1, s32[8192]{0:T(1024)S(1)} %eq.52), kind=kOutput, calls=%fused_computation.9 | convolution fusion | flops 1350557696 | bytes 2326528 | tf_op jit(solution)/shard_map/dot_general | solution.py:194
  32.6 1.6 %fusion.27 = f32[64,128,128]{2,1,0:T(8,128)S(1)} fusion(bf16[64,128,128]{2,1,0:T(8,128)(2,1)S(1)} %bitcast.43, bf16[64,128,128]{2,1,0:T(8,128)(2,1)S(1)} %bitcast.44), kind=kOutput, calls=%fused_computation.69 | convolution fusion | flops 268435456 | bytes 8388608 | tf_op jit(solution)/shard_map/brm,blm->brl/dot_general | solution.py:198
  34.1 0.5 slice_select_fusion
  34.6 0.3 copy-done.5
  34.9 1.7 %pad_maximum_fusion = f32[16,4,66,128]{3,2,1,0:T(8,128)} fusion(f32[16,4,1,128]{3,2,1,0:T(1,128)S(1)} %bitcast.52, f32[16,4,1,128]{3,2,1,0:T(1,128)S(1)} %bitcast.51, f32[16,4,64,128]{3,2,1,0:T(8,128)S(1)} %bitcast.42), kind=kLoop, calls=%fused_computation.10 | loop fusion | flops 1081344 | bytes 4325376 | tf_op jit(solution)/shard_map/concatenate | solution.py:203
  36.9 0.6 gather_fusion
  37.9 56.5 %reduce-scatter.2.cloned.1.call-done = f32[1,4,66,128]{3,2,1,0:T(8,128)} async-done(((f32[16,4,66,128]{3,2,1,0:T(8,128)}), f32[1,4,66,128]{3,2,1,0:T(8,128)}) %reduce-scatter.2.cloned.1.call-update) | async-done | bytes 135184 | tf_op jit(solution)/shard_map/reduce_scatter | solution.py:204
  94.4 0.8 fusion.26
  95.5 0.3 broadcast_in_dim.67
  95.8 0.2 reshape.165
  96.0 1.0 fusion.17
  97.0 0.9 broadcast_in_dim.70
  97.9 7.4 %all-to-all-start = ((bf16[8,4,64,128]{3,2,1,0:T(8,128)(2,1)}), bf16[8,4,64,128]{3,2,1,0:T(8,128)(2,1)S(1)}, u32[]{:S(2)}, u32[]{:S(2)}) async-start(bf16[8,4,64,128]{3,2,1,0:T(8,128)(2,1)} %broadcast_in_dim.70), calls=%async_computation.1 | async-start | bytes 1048576 | tf_op jit(solution)/shard_map/all_to_all | solution.py:117
  105.5 5.7 %fusion.5 = bf16[8192,128]{1,0:T(8,128)(2,1)S(1)} fusion(s32[8192]{0:T(1024)S(1)} %eq.52, bf16[2,640,128]{2,1,0:T(8,128)(2,1)S(1)} %pad_maximum_fusion.1), kind=kOutput, calls=%fused_computation.7 | convolution fusion | flops 1348468736 | bytes 2293760 | tf_op jit(solution)/shard_map/dot_general | solution.py:195
  111.2 12.1 %all-to-all-done = bf16[8,4,64,128]{3,2,1,0:T(8,128)(2,1)S(1)} async-done(((bf16[8,4,64,128]{3,2,1,0:T(8,128)(2,1)}), bf16[8,4,64,128]{3,2,1,0:T(8,128)(2,1)S(1)}, u32[]{:S(2)}, u32[]{:S(2)}) %all-to-all-start) | async-done | bytes 524320 | tf_op jit(solution)/shard_map/all_to_all | solution.py:117
  123.3 0.3 broadcast_in_dim.71
  123.6 4.7 %all_to_all.10 = bf16[2,8,4,64,128]{4,3,2,1,0:T(8,128)(2,1)S(1)} all-to-all(bf16[2,8,4,64,128]{4,3,2,1,0:T(8,128)(2,1)S(1)} %broadcast_in_dim.71), channel_id=1, replica_groups=mesh['z'=8,'core'=2,'reg'=16] {'core'}, dimensions={0} | all-to-all | bytes 2097152 | tf_op jit(solution)/shard_map/all_to_all | solution.py:120
  128.4 0.7 fusion.10
  129.1 1.5 %copy-done.1 = f32[8192,128]{1,0:T(8,128)S(1)} copy-done((f32[8192,128]{1,0:T(8,128)S(1)}, f32[8192,128]{1,0:T(8,128)}, u32[]{:S(2)}) %copy-start.1) | copy-done | bytes 4194328
  130.6 2.7 %convert_add_fusion = f32[8192,128]{1,0:T(8,128)} fusion(f32[8192,128]{1,0:T(8,128)S(1)} %copy-done.1, bf16[64,128,128]{2,1,0:T(8,128)(2,1)S(1)} %fusion.10), kind=kLoop, calls=%fused_computation.8 | loop fusion | flops 2097152 | bytes 10485760 | tf_op jit(solution)/shard_map/add | solution.py:233
  (48 shorter events, 1.7 us)
Async XLA Ops:
  6.5 31.2 %copy-start = (f32[128,64]{0,1:T(8,128)S(1)}, f32[128,64]{0,1:T(8,128)}, u32[]{:S(2)}) copy-start(f32[128,64]{0,1:T(8,128)} %param.15) | copy-start | bytes 98308
  6.5 87.9 %reduce-scatter.2.cloned.1.call-start = ((), (), s32[]{:S(2)}) async-start(), calls=%async_computation.3 | async-start | bytes 2506752 | tf_op jit(solution)/shard_map/reduce_scatter | solution.py:204
  8.1 9.9 %collective-permute-start = (f32[4,129]{1,0:T(4,128)S(1)}, f32[4,129]{1,0:T(4,128)S(1)}, u32[]{:S(2)}, u32[]{:S(2)}) collective-permute-start(f32[4,129]{1,0:T(4,128)S(1)} %pad_maximum_fusion.3), channel_id=1, source_target_pairs={{15,0},{0,1},{1,2},{2,3},{3,4},{4,5},{5,6},{6,7},{7,8},{8,9},{9,10... | collective-permute-start | bytes 6200 | tf_op jit(solution)/shard_map/ppermute | solution.py:76
  12.2 15.6 %copy-start.3 = (bf16[512,128]{1,0:T(8,128)(2,1)S(1)}, bf16[512,128]{1,0:T(8,128)(2,1)}, u32[]{:S(2)}) copy-start(bf16[512,128]{1,0:T(8,128)(2,1)} %param.11) | copy-start | bytes 393220
  12.2 15.6 %copy-start.4 = (bf16[512,128]{1,0:T(8,128)(2,1)S(1)}, bf16[512,128]{1,0:T(8,128)(2,1)}, u32[]{:S(2)}) copy-start(bf16[512,128]{1,0:T(8,128)(2,1)} %param.10) | copy-start | bytes 393220
  12.2 15.5 %collective-permute-start.1 = (bf16[2,64,128]{2,1,0:T(8,128)(2,1)S(1)}, bf16[2,64,128]{2,1,0:T(8,128)(2,1)S(1)}, u32[]{:S(2)}, u32[]{:S(2)}) collective-permute-start(bf16[2,64,128]{2,1,0:T(8,128)(2,1)S(1)} %get-tuple-element.13), channel_id=1, source_target_pairs={{0,1},{1,2},{2,3},{3,4},{4,5},{5,6},{6,7},{7,8},{8,9},{9,10},{10,1... | collective-permute-start | bytes 98312 | tf_op jit(solution)/shard_map/ppermute | solution.py:85
  13.6 14.1 %collective-permute-start.2 = (bf16[2,64,128]{2,1,0:T(8,128)(2,1)S(1)}, bf16[2,64,128]{2,1,0:T(8,128)(2,1)S(1)}, u32[]{:S(2)}, u32[]{:S(2)}) collective-permute-start(bf16[2,64,128]{2,1,0:T(8,128)(2,1)S(1)} %get-tuple-element.14), channel_id=1, source_target_pairs={{1,0},{2,1},{3,2},{4,3},{5,4},{6,5},{7,6},{8,7},{9,8},{10,9},{11,1... | collective-permute-start | bytes 98312 | tf_op jit(solution)/shard_map/ppermute | solution.py:88
  27.8 4.8 %copy-start.2 = (bf16[8192,128]{1,0:T(8,128)(2,1)S(1)}, bf16[8192,128]{1,0:T(8,128)(2,1)}, u32[]{:S(2)}) copy-start(bf16[8192,128]{1,0:T(8,128)(2,1)} %get-tuple-element.9) | copy-start | bytes 6291460
  34.1 0.8 copy-start.5
  34.9 1.7 %copy-start.6 = (s32[128]{0:T(128)S(1)}, s32[128]{0:T(128)}, u32[]{:S(2)}) copy-start(s32[128]{0:T(128)} %param.14) | copy-start | bytes 1540
  97.9 25.4 %all-to-all-start = ((bf16[8,4,64,128]{3,2,1,0:T(8,128)(2,1)}), bf16[8,4,64,128]{3,2,1,0:T(8,128)(2,1)S(1)}, u32[]{:S(2)}, u32[]{:S(2)}) async-start(bf16[8,4,64,128]{3,2,1,0:T(8,128)(2,1)} %broadcast_in_dim.70), calls=%async_computation.1 | async-start | bytes 1048576 | tf_op jit(solution)/shard_map/all_to_all | solution.py:117
  128.4 2.2 %copy-start.1 = (f32[8192,128]{1,0:T(8,128)S(1)}, f32[8192,128]{1,0:T(8,128)}, u32[]{:S(2)}) copy-start(f32[8192,128]{1,0:T(8,128)} %get-tuple-element.8) | copy-start | bytes 12582916
Sparse Core Ops, SparseCore 0:
  36.7 57.6 reduce-scatter.1

commit v13 on v12

--- a/solution.py
+++ b/solution.py
@@ -8,7 +8,7 @@
 BLOCK = 64
 KB = 64
 STEPS = 4
-ROWS = 4096
+ROWS = 8192
 CORES = 2
 MEM = ("z", "core")
 

time: 141 us -> 142 us (level)
  transfers between devices with their start and end apart: 5 -> 5, of which waited for: 2 -> 2; matrix products, arithmetic and copies ran while one was open for 9% -> 9% of each run, Pallas kernels for 5% -> 6%
where the time goes in v13:
time: 142 us; the launch traced here: 141 us
  waiting for transfers between devices  68.7 us (48%)
  starting transfers between devices  14.4 us (10%)
  matrix products  13.9 us (10%)
  between operations  13.6 us (10%)
  local copies, waits for them, and re-layouts  10.4 us (7%)
  Pallas kernels  8.57 us (6%)
  other arithmetic  6.85 us (5%)
  blocking collectives  4.68 us (3%)
    reduce_scatter x1, waiting for transfers between devices, per_device(): lax.psum_scatter(payload.reshape(parts, share, BLOCK + 2, 2 * KB), MEM, s...  56.5 us
    all_to_all x1, waiting for transfers between devices, gathered_copies(): lax.all_to_all(jnp.broadcast_to(value, (chips, *value.shape)), 'z', split...  12.1 us
    pallas_call x1, Pallas kernels, advect(): pl.pallas_call(advect_kernel, grid=(cells // rows,), in_specs=[pl.BlockSp...  8.57 us
    all_to_all x1, starting transfers between devices, gathered_copies(): lax.all_to_all(jnp.broadcast_to(value, (chips, *value.shape)), 'z', split...  7.41 us
    dot_general x1, matrix products, per_device(): jnp.dot(picks, extended[1], preferred_element_type=jnp.float32)  5.72 us
    dot_general x1, matrix products, per_device(): jnp.dot(picks, extended[0], preferred_element_type=jnp.float32)  4.75 us
    all_to_all x1, blocking collectives, gathered_copies(): lax.all_to_all(jnp.broadcast_to(along_z, (cores, *along_z.shape)), 'core'...  4.68 us
    ppermute x1, starting transfers between devices, padded(): lax.ppermute(lax.slice_in_dim(block, 0, width, axis=dim), axis, backward)  3.49 us
  transfers between devices with their start and end apart: 5, of which 2 were waited for; matrix products, arithmetic and copies ran while one was open for 9% of the time, Pallas kernels for 6%

profile of v13, /device:TPU:1, one launch (start us, length us, event | category | flops | bytes accessed | tf_op | source)
XLA Modules:
  0.0 141.1 jit_solution(17732779714113648976)
XLA Ops:
  6.5 0.8 slice_bitcast_fusion.6
  7.4 0.7 slice.87
  8.1 2.1 %collective-permute-start = (f32[4,129]{1,0:T(4,128)S(1)}, f32[4,129]{1,0:T(4,128)S(1)}, u32[]{:S(2)}, u32[]{:S(2)}) collective-permute-start(f32[4,129]{1,0:T(4,128)S(1)} %pad_maximum_fusion.3), channel_id=1, source_target_pairs={{15,0},{0,1},{1,2},{2,3},{3,4},{4,5},{5,6},{6,7},{7,8},{8,9},{9,10... | collective-permute-start | bytes 6200 | tf_op jit(solution)/shard_map/ppermute | solution.py:76
  10.2 0.8 eq.56
  11.0 1.2 convolution_convert_fusion
  12.2 1.4 collective-permute-start.1
  13.6 3.5 %collective-permute-start.2 = (bf16[2,64,128]{2,1,0:T(8,128)(2,1)S(1)}, bf16[2,64,128]{2,1,0:T(8,128)(2,1)S(1)}, u32[]{:S(2)}, u32[]{:S(2)}) collective-permute-start(bf16[2,64,128]{2,1,0:T(8,128)(2,1)S(1)} %get-tuple-element.14), channel_id=1, source_target_pairs={{1,0},{2,1},{3,2},{4,3},{5,4},{6,5},{7,6},{8,7},{9,8},{10,9},{11,1... | collective-permute-start | bytes 98312 | tf_op jit(solution)/shard_map/ppermute | solution.py:88
  17.1 0.8 copy.29
  18.4 0.5 slice.118
  18.9 0.7 multiply_subtract_fusion.1
  19.6 0.6 concatenate.26.halo_ref
  20.2 8.6 %shard_map.82 = (f32[8192,128]{1,0:T(8,128)}, bf16[8192,128]{1,0:T(8,128)(2,1)}, f32[64,128]{1,0:T(8,128)}) custom-call(f32[8,128]{1,0:T(8,128)} %concatenate.26.halo_ref, f32[64,128]{1,0:T(8,128)} %bitcast.50, f32[8192,128]{1,0:T(8,128)} %x_ref.1), custom_call_target="tpu_custom_call" | custom-call | tf_op jit(solution)/shard_map/pallas_call | solution.py:41
  28.9 4.8 %convert_reduce_fusion = (f32[8192]{0:T(1024)S(1)}, bf16[8192,128]{1,0:T(8,128)(2,1)S(1)}) fusion(bf16[2,640,128]{2,1,0:T(8,128)(2,1)S(1)} %pad_maximum_fusion.1, s32[8192]{0:T(1024)S(1)} %eq.52), kind=kOutput, calls=%fused_computation.9 | convolution fusion | flops 1350557696 | bytes 2326528 | tf_op jit(solution)/shard_map/dot_general | solution.py:194
  33.6 1.6 %fusion.27 = f32[64,128,128]{2,1,0:T(8,128)S(1)} fusion(bf16[64,128,128]{2,1,0:T(8,128)(2,1)S(1)} %bitcast.43, bf16[64,128,128]{2,1,0:T(8,128)(2,1)S(1)} %bitcast.44), kind=kOutput, calls=%fused_computation.69 | convolution fusion | flops 268435456 | bytes 8388608 | tf_op jit(solution)/shard_map/brm,blm->brl/dot_general | solution.py:198
  35.2 0.5 slice_select_fusion
  35.7 0.3 copy-done.5
  36.0 1.7 %pad_maximum_fusion = f32[16,4,66,128]{3,2,1,0:T(8,128)} fusion(f32[16,4,1,128]{3,2,1,0:T(1,128)S(1)} %bitcast.52, f32[16,4,1,128]{3,2,1,0:T(1,128)S(1)} %bitcast.51, f32[16,4,64,128]{3,2,1,0:T(8,128)S(1)} %bitcast.42), kind=kLoop, calls=%fused_computation.10 | loop fusion | flops 1081344 | bytes 4325376 | tf_op jit(solution)/shard_map/concatenate | solution.py:203
  38.0 0.6 gather_fusion
  39.0 56.5 %reduce-scatter.2.cloned.1.call-done = f32[1,4,66,128]{3,2,1,0:T(8,128)} async-done(((f32[16,4,66,128]{3,2,1,0:T(8,128)}), f32[1,4,66,128]{3,2,1,0:T(8,128)}) %reduce-scatter.2.cloned.1.call-update) | async-done | bytes 135184 | tf_op jit(solution)/shard_map/reduce_scatter | solution.py:204
  95.5 0.8 fusion.26
  96.5 0.3 broadcast_in_dim.67
  96.9 0.2 reshape.165
  97.1 1.0 fusion.17
  98.1 0.9 broadcast_in_dim.70
  99.0 7.4 %all-to-all-start = ((bf16[8,4,64,128]{3,2,1,0:T(8,128)(2,1)}), bf16[8,4,64,128]{3,2,1,0:T(8,128)(2,1)S(1)}, u32[]{:S(2)}, u32[]{:S(2)}) async-start(bf16[8,4,64,128]{3,2,1,0:T(8,128)(2,1)} %broadcast_in_dim.70), calls=%async_computation.1 | async-start | bytes 1048576 | tf_op jit(solution)/shard_map/all_to_all | solution.py:117
  106.5 5.7 %fusion.5 = bf16[8192,128]{1,0:T(8,128)(2,1)S(1)} fusion(s32[8192]{0:T(1024)S(1)} %eq.52, bf16[2,640,128]{2,1,0:T(8,128)(2,1)S(1)} %pad_maximum_fusion.1), kind=kOutput, calls=%fused_computation.7 | convolution fusion | flops 1348468736 | bytes 2293760 | tf_op jit(solution)/shard_map/dot_general | solution.py:195
  112.2 12.1 %all-to-all-done = bf16[8,4,64,128]{3,2,1,0:T(8,128)(2,1)S(1)} async-done(((bf16[8,4,64,128]{3,2,1,0:T(8,128)(2,1)}), bf16[8,4,64,128]{3,2,1,0:T(8,128)(2,1)S(1)}, u32[]{:S(2)}, u32[]{:S(2)}) %all-to-all-start) | async-done | bytes 524320 | tf_op jit(solution)/shard_map/all_to_all | solution.py:117
  124.4 0.3 broadcast_in_dim.71
  124.6 4.7 %all_to_all.10 = bf16[2,8,4,64,128]{4,3,2,1,0:T(8,128)(2,1)S(1)} all-to-all(bf16[2,8,4,64,128]{4,3,2,1,0:T(8,128)(2,1)S(1)} %broadcast_in_dim.71), channel_id=1, replica_groups=mesh['z'=8,'core'=2,'reg'=16] {'core'}, dimensions={0} | all-to-all | bytes 2097152 | tf_op jit(solution)/shard_map/all_to_all | solution.py:120
  129.4 0.7 fusion.10
  130.1 1.5 %copy-done.1 = f32[8192,128]{1,0:T(8,128)S(1)} copy-done((f32[8192,128]{1,0:T(8,128)S(1)}, f32[8192,128]{1,0:T(8,128)}, u32[]{:S(2)}) %copy-start.1) | copy-done | bytes 4194328
  131.6 2.7 %convert_add_fusion = f32[8192,128]{1,0:T(8,128)} fusion(f32[8192,128]{1,0:T(8,128)S(1)} %copy-done.1, bf16[64,128,128]{2,1,0:T(8,128)(2,1)S(1)} %fusion.10), kind=kLoop, calls=%fused_computation.8 | loop fusion | flops 2097152 | bytes 10485760 | tf_op jit(solution)/shard_map/add | solution.py:233
  (48 shorter events, 1.7 us)
Async XLA Ops:
  6.5 32.2 %copy-start = (f32[128,64]{0,1:T(8,128)S(1)}, f32[128,64]{0,1:T(8,128)}, u32[]{:S(2)}) copy-start(f32[128,64]{0,1:T(8,128)} %param.15) | copy-start | bytes 98308
  6.5 89.0 %reduce-scatter.2.cloned.1.call-start = ((), (), s32[]{:S(2)}) async-start(), calls=%async_computation.3 | async-start | bytes 2506752 | tf_op jit(solution)/shard_map/reduce_scatter | solution.py:204
  8.1 9.9 %collective-permute-start = (f32[4,129]{1,0:T(4,128)S(1)}, f32[4,129]{1,0:T(4,128)S(1)}, u32[]{:S(2)}, u32[]{:S(2)}) collective-permute-start(f32[4,129]{1,0:T(4,128)S(1)} %pad_maximum_fusion.3), channel_id=1, source_target_pairs={{15,0},{0,1},{1,2},{2,3},{3,4},{4,5},{5,6},{6,7},{7,8},{8,9},{9,10... | collective-permute-start | bytes 6200 | tf_op jit(solution)/shard_map/ppermute | solution.py:76
  12.2 16.6 %copy-start.3 = (bf16[512,128]{1,0:T(8,128)(2,1)S(1)}, bf16[512,128]{1,0:T(8,128)(2,1)}, u32[]{:S(2)}) copy-start(bf16[512,128]{1,0:T(8,128)(2,1)} %param.11) | copy-start | bytes 393220
  12.2 16.6 %copy-start.4 = (bf16[512,128]{1,0:T(8,128)(2,1)S(1)}, bf16[512,128]{1,0:T(8,128)(2,1)}, u32[]{:S(2)}) copy-start(bf16[512,128]{1,0:T(8,128)(2,1)} %param.10) | copy-start | bytes 393220
  12.2 16.6 %collective-permute-start.1 = (bf16[2,64,128]{2,1,0:T(8,128)(2,1)S(1)}, bf16[2,64,128]{2,1,0:T(8,128)(2,1)S(1)}, u32[]{:S(2)}, u32[]{:S(2)}) collective-permute-start(bf16[2,64,128]{2,1,0:T(8,128)(2,1)S(1)} %get-tuple-element.13), channel_id=1, source_target_pairs={{0,1},{1,2},{2,3},{3,4},{4,5},{5,6},{6,7},{7,8},{8,9},{9,10},{10,1... | collective-permute-start | bytes 98312 | tf_op jit(solution)/shard_map/ppermute | solution.py:85
  13.6 15.2 %collective-permute-start.2 = (bf16[2,64,128]{2,1,0:T(8,128)(2,1)S(1)}, bf16[2,64,128]{2,1,0:T(8,128)(2,1)S(1)}, u32[]{:S(2)}, u32[]{:S(2)}) collective-permute-start(bf16[2,64,128]{2,1,0:T(8,128)(2,1)S(1)} %get-tuple-element.14), channel_id=1, source_target_pairs={{1,0},{2,1},{3,2},{4,3},{5,4},{6,5},{7,6},{8,7},{9,8},{10,9},{11,1... | collective-permute-start | bytes 98312 | tf_op jit(solution)/shard_map/ppermute | solution.py:88
  28.9 4.8 %copy-start.2 = (bf16[8192,128]{1,0:T(8,128)(2,1)S(1)}, bf16[8192,128]{1,0:T(8,128)(2,1)}, u32[]{:S(2)}) copy-start(bf16[8192,128]{1,0:T(8,128)(2,1)} %get-tuple-element.9) | copy-start | bytes 6291460
  35.2 0.8 copy-start.5
  36.0 1.7 %copy-start.6 = (s32[128]{0:T(128)S(1)}, s32[128]{0:T(128)}, u32[]{:S(2)}) copy-start(s32[128]{0:T(128)} %param.14) | copy-start | bytes 1540
  99.0 25.4 %all-to-all-start = ((bf16[8,4,64,128]{3,2,1,0:T(8,128)(2,1)}), bf16[8,4,64,128]{3,2,1,0:T(8,128)(2,1)S(1)}, u32[]{:S(2)}, u32[]{:S(2)}) async-start(bf16[8,4,64,128]{3,2,1,0:T(8,128)(2,1)} %broadcast_in_dim.70), calls=%async_computation.1 | async-start | bytes 1048576 | tf_op jit(solution)/shard_map/all_to_all | solution.py:117
  129.4 2.2 %copy-start.1 = (f32[8192,128]{1,0:T(8,128)S(1)}, f32[8192,128]{1,0:T(8,128)}, u32[]{:S(2)}) copy-start(f32[8192,128]{1,0:T(8,128)} %get-tuple-element.8) | copy-start | bytes 12582916
Sparse Core Ops, SparseCore 0:
  37.8 57.6 reduce-scatter.1
